TPU v7x, 512 devices: a whole 4x8x8 slice. The times are simulated.
512 devices in a mesh: pool: 64 (over z, y), mp: 8 (over x, core).
Axes of the slice: x: 4, y: 8, z: 8, core: 2. Of those that a mesh axis runs over, the one named last changes fastest.
Arguments:
- hidden: float32 [64, 2048], P('pool', 'mp'), may hold values from -40 to 40
- norm_gain: float32 [2048], replicated, may hold values from 0.5 to 2
- w_query: bfloat16 [2048, 2048], P(None, 'mp'), may hold values from -0.75 to 0.75
- w_keyval: bfloat16 [2048, 1024], P(None, 'mp'), may hold values from -0.75 to 0.75
- w_out: bfloat16 [2048, 2048], P('mp'), may hold values from -0.125 to 0.125
- kv_cache: bfloat16 [6144, 8, 128, 128], P('pool', 'mp'), may hold values from -900 to 900
- block_slot: int32 [64, 128], replicated, may hold values from 0 to 6143, as said below
- lengths: int32 [64], replicated, may hold values from 1 to 16384, as said below
Outputs:
- layer_out: float32 [64, 2048], P('pool', 'mp')
- new_kv: bfloat16 [64, 1024], P('pool', 'mp')
Inputs may be any that keep to these rules, and one draw needn't show every extreme that they name: `lengths`: some request holds exactly 16384 tokens in every draw. `block_slot`: A slot number s lies on index s // 96 of pool, at its slot s % 96. Entries of live blocks (b * 128 < lengths[r]) are all distinct; entries of other blocks are arbitrary slot numbers and must be ignored. The live blocks number exactly 4128 in all.
All inputs are finite; a program needn't handle non-finite values.
Results may differ from a plain program's by a relative error of at most 0.029.
Values may be sent and summed in bfloat16 or wider, within the bound.
No kernel may reach another device: no remote copies, remote signals or barrier semaphores. Data moves between devices by JAX's collectives and lax.ppermute only.
A program may use at most 64 MiB of HBM per device.

v0:
```python
import jax
import jax.numpy as jnp
from jax import lax
from jax.sharding import PartitionSpec as P

EPSILON = 1e-05
RESIDUAL_SCALE = 0.22
SCORE_SCALE = 0.015625
ROPE_BASE = 10000000.0
MASKED = -1e30


def rotate(values, positions):
    half_dim = values.shape[-1] // 2
    inverse = ROPE_BASE ** (-jnp.arange(half_dim).astype(jnp.float32) * 2.0 / values.shape[-1])
    angles = positions[:, None] * inverse[None, :]
    cosine = jnp.cos(angles)[:, None, :]
    sine_part = jnp.sin(angles)[:, None, :]
    front_half = values[..., :half_dim]
    back_half = values[..., half_dim:]
    return jnp.concatenate(
        [front_half * cosine - back_half * sine_part, back_half * cosine + front_half * sine_part],
        -1,
    )


def per_device(hidden, norm_gain, w_query, w_keyval, w_out, kv_cache, block_slot, lengths):
    local_rows = hidden.shape[0]
    slots_here = kv_cache.shape[0]
    kv_heads = kv_cache.shape[1]
    block_len = kv_cache.shape[2]
    head_dim = kv_cache.shape[3] // 2
    q_heads = w_query.shape[1] // head_dim
    group_size = q_heads // kv_heads
    all_requests = block_slot.shape[0]
    max_blocks = block_slot.shape[1]
    pool_size = lax.axis_size("pool")
    pool_index = lax.axis_index("pool")
    full_rows = lax.all_gather(hidden, "mp", axis=1, tiled=True)
    variance = jnp.mean(full_rows * full_rows, axis=-1, keepdims=True)
    normed = (full_rows * lax.rsqrt(variance + EPSILON) * norm_gain).astype(jnp.bfloat16)
    queries = jnp.dot(normed, w_query, preferred_element_type=jnp.float32).reshape(
        local_rows, q_heads, head_dim
    )
    key_value = jnp.dot(normed, w_keyval, preferred_element_type=jnp.float32).reshape(
        local_rows, kv_heads, 2, head_dim
    )
    own_lengths = lax.dynamic_slice_in_dim(lengths, pool_index * local_rows, local_rows)
    positions = own_lengths.astype(jnp.float32)
    queries = rotate(queries, positions).astype(jnp.bfloat16)
    new_key = rotate(key_value[:, :, 0], positions).astype(jnp.bfloat16)
    new_value = key_value[:, :, 1].astype(jnp.bfloat16)
    new_kv = jnp.stack([new_key, new_value], 2).reshape(local_rows, kv_heads * 2 * head_dim)
    query_wide = queries.astype(jnp.float32).reshape(local_rows, kv_heads, group_size, head_dim)
    self_score = (
        jnp.sum(query_wide * new_key.astype(jnp.float32)[:, :, None, :], -1).reshape(
            local_rows, q_heads
        )
        * SCORE_SCALE
    )
    value_heads = jnp.broadcast_to(
        new_value.astype(jnp.float32)[:, :, None, :], (local_rows, kv_heads, group_size, head_dim)
    ).reshape(local_rows, q_heads, head_dim)
    flat_slots = block_slot.reshape(-1)
    entry_ids = jnp.arange(all_requests * max_blocks, dtype=jnp.int32)
    entry_req = entry_ids // max_blocks
    entry_block = entry_ids % max_blocks
    entry_live = entry_block * block_len < jnp.repeat(lengths, max_blocks)
    here_ids = pool_index * slots_here + jnp.arange(slots_here, dtype=jnp.int32)
    matches = (flat_slots[None, :] == here_ids[:, None]) & entry_live[None, :]
    slot_used = jnp.any(matches, axis=1)
    slot_owner = jnp.sum(jnp.where(matches, entry_req[None, :], 0), axis=1)
    block_of = jnp.sum(jnp.where(matches, entry_block[None, :], 0), axis=1)
    token_limit = jnp.where(slot_used, lengths[slot_owner] - block_of * block_len, 0)
    all_queries = lax.all_gather(
        queries.reshape(local_rows, q_heads * head_dim), "pool", axis=0, tiled=True
    )
    slot_query = all_queries[slot_owner].reshape(slots_here, kv_heads, group_size, head_dim)
    cache_keys = kv_cache[..., :head_dim]
    cache_values = kv_cache[..., head_dim:]
    scores = (
        jnp.einsum("skgd,sktd->skgt", slot_query, cache_keys, preferred_element_type=jnp.float32)
        * SCORE_SCALE
    )
    token_live = jnp.arange(block_len)[None, :] < token_limit[:, None]
    live_mask = token_live[:, None, None, :]
    scores = jnp.where(live_mask, scores, MASKED)
    block_max = jnp.max(scores, axis=-1)
    weights = jnp.where(live_mask, jnp.exp(scores - block_max[..., None]), 0.0).astype(jnp.bfloat16)
    block_sum = jnp.sum(weights.astype(jnp.float32), axis=-1)
    block_out = jnp.einsum(
        "skgt,sktd->skgd", weights, cache_values, preferred_element_type=jnp.float32
    )
    block_max = jnp.where(slot_used[:, None, None], block_max, MASKED)
    member = (slot_owner[None, :] == jnp.arange(all_requests)[:, None]) & slot_used[None, :]
    member_mask = member[:, :, None, None]
    local_max = jnp.max(jnp.where(member_mask, block_max[None], MASKED), axis=1)
    rescale = jnp.where(member_mask, jnp.exp(block_max[None] - local_max[:, None]), 0.0)
    local_sum = jnp.sum(rescale * block_sum[None], axis=1)
    local_out = jnp.einsum("rskg,skgd->rkgd", rescale, block_out)
    flat_out = local_out.reshape(all_requests, q_heads * head_dim)
    flat_max = local_max.reshape(all_requests, q_heads)
    flat_sum = local_sum.reshape(all_requests, q_heads)
    got_out, got_max, got_sum = (
        lax.all_to_all(
            flat_out.reshape(pool_size, local_rows, q_heads * head_dim),
            "pool",
            split_axis=0,
            concat_axis=0,
            tiled=True,
        ),
        lax.all_to_all(
            flat_max.reshape(pool_size, local_rows, q_heads),
            "pool",
            split_axis=0,
            concat_axis=0,
            tiled=True,
        ),
        lax.all_to_all(
            flat_sum.reshape(pool_size, local_rows, q_heads),
            "pool",
            split_axis=0,
            concat_axis=0,
            tiled=True,
        ),
    )
    overall = jnp.maximum(jnp.max(got_max, axis=0), self_score)
    part_w = jnp.exp(got_max - overall[None])
    numerator = jnp.sum(
        part_w[..., None] * got_out.reshape(pool_size, local_rows, q_heads, head_dim), axis=0
    )
    denominator = jnp.sum(part_w * got_sum, axis=0)
    self_w = jnp.exp(self_score - overall)
    numerator = numerator + self_w[..., None] * value_heads
    denominator = denominator + self_w
    attended = (
        (numerator / denominator[..., None])
        .reshape(local_rows, q_heads * head_dim)
        .astype(jnp.bfloat16)
    )
    partial_value = jnp.dot(attended, w_out, preferred_element_type=jnp.float32)
    mixed_rows = lax.psum_scatter(partial_value, "mp", scatter_dimension=1, tiled=True)
    return (hidden + RESIDUAL_SCALE * mixed_rows, new_kv)


def solution(mesh):
    return jax.shard_map(
        per_device,
        mesh=mesh,
        in_specs=(
            P("pool", "mp"),
            P(),
            P(None, "mp"),
            P(None, "mp"),
            P("mp", None),
            P("pool", "mp", None, None),
            P(),
            P(),
        ),
        out_specs=(P("pool", "mp"), P("pool", "mp")),
        check_vma=False,
    )
```

profile of v0, /device:TPU:1, one launch (start us, length us, event | category | flops | bytes accessed | tf_op | source)
XLA Modules:
  0.0 183.1 jit_solution(15372942022111984126)
XLA Ops:
  7.2 1.3 dynamic_slice.3
  9.3 0.7 bitcast_compare_fusion
  10.1 14.8 %all_gather.6 = f32[1,2048]{1,0:T(1,128)S(1)} all-gather(f32[1,256]{1,0:T(1,128)} %param.8), channel_id=1, replica_groups=mesh['pool'=64,'mp'=8] {'mp'}, dimensions={1}, use_global_device_ids=true | all-gather | bytes 9216 | tf_op jit(solution)/shard_map/all_gather | solution.py:39
  24.9 0.6 multiply_reduce_fusion.3
  26.2 1.3 fusion.6
  27.5 1.8 select_reduce_fusion
  29.3 1.6 gather_fusion
  31.0 1.5 copy.52
  32.5 1.3 fusion.30
  33.8 0.1 subtract_convert_fusion
  34.0 0.1 reshape.571
  34.0 41.4 %all-gather = bf16[64,1,256]{2,1,0:T(2,128)(2,1)S(1)} all-gather(bf16[1,1,256]{2,1,0:T(2,128)(2,1)S(1)} %reshape.571), channel_id=1, replica_groups=mesh['pool'=64,'mp'=8] {'pool'}, dimensions={0}, use_global_device_ids=true | all-gather | bytes 33280 | tf_op jit(solution)/shard_map/all_gather | solution.py:75
  75.5 0.8 gather_fusion.1
  76.3 0.1 copy.53
  76.4 0.1 copy.55
  76.5 3.7 %fusion.43 = (f32[96,4]{1,0:T(8,128)S(1)}, f32[96,4,128]{2,1,0:T(4,128)S(1)}) fusion(bf16[96,4,64]{2,1,0:T(4,128)(2,1)S(1)} %copy.55, bf16[96,1,128,128]{3,2,1,0:T(8,128)(2,1)} %param.13, pred[96,128]{1,0:T(8,128)(4,1)S(1)} %iota_compare_fusion), kind=kOutput, calls=%fused_computation.90 | convolution fusion | flops 6438528 | bytes 3405312 | tf_op jit(solution)/shard_map/skgd,sktd->skgt/dot_general | solution.py:82
  80.2 0.1 broadcast_select_fusion
  80.4 0.1 select_reduce_fusion.2
  80.5 0.7 copy.57
  81.2 7.1 %all-to-all-start = ((f32[64,1,4]{2,1,0:T(1,128)}), f32[64,1,4]{2,1,0:T(1,128)S(1)}, u32[]{:S(2)}, u32[]{:S(2)}) async-start(f32[64,1,4]{2,1,0:T(1,128)} %copy.57), calls=%async_computation | async-start | bytes 65536 | tf_op jit(solution)/shard_map/all_to_all | solution.py:112
  88.3 0.2 copy.58
  88.6 0.3 fusion.28
  88.9 0.3 convert_reduce_fusion
  89.2 3.0 %fusion = bf16[96,4,64]{2,1,0:T(4,128)(2,1)S(1)} fusion(bf16[96,1,128,128]{3,2,1,0:T(8,128)(2,1)} %param.13, f32[96,4,128]{2,1,0:T(4,128)S(1)} %get-tuple-element.15, f32[96,4]{1,0:T(8,128)S(1)} %get-tuple-element.14, pred[96,128]{1,0:T(8,128)(4,1)S(1)} %iota_compare_fusion), kind=kOutput, calls=%fused_computation.2 | convolution fusion | flops 6438912 | bytes 3405312 | tf_op jit(solution)/shard_map/skgt,sktd->skgd/dot_general | solution.py:91
  92.4 0.2 multiply_reduce_fusion
  92.6 0.3 fusion.13
  92.9 0.2 multiply_reduce_fusion.4
  93.1 0.1 reshape.551
  93.2 0.7 copy.62
  93.9 0.7 copy.64
  94.6 4.5 %all-to-all-done = f32[64,1,4]{2,1,0:T(1,128)S(1)} async-done(((f32[64,1,4]{2,1,0:T(1,128)}), f32[64,1,4]{2,1,0:T(1,128)S(1)}, u32[]{:S(2)}, u32[]{:S(2)}) %all-to-all-start) | async-done | bytes 1056 | tf_op jit(solution)/shard_map/all_to_all | solution.py:112
  99.2 7.6 %all-to-all-start.2 = ((f32[64,1,4]{2,1,0:T(1,128)}), f32[64,1,4]{2,1,0:T(1,128)S(1)}, u32[]{:S(2)}, u32[]{:S(2)}) async-start(f32[64,1,4]{2,1,0:T(1,128)} %copy.64), calls=%async_computation.2 | async-start | bytes 65536 | tf_op jit(solution)/shard_map/all_to_all | solution.py:119
  106.8 0.1 reduce_max.32
  106.9 10.8 %all-to-all-done.2 = f32[64,1,4]{2,1,0:T(1,128)S(1)} async-done(((f32[64,1,4]{2,1,0:T(1,128)}), f32[64,1,4]{2,1,0:T(1,128)S(1)}, u32[]{:S(2)}, u32[]{:S(2)}) %all-to-all-start.2) | async-done | bytes 1056 | tf_op jit(solution)/shard_map/all_to_all | solution.py:119
  117.6 4.6 %all-to-all-start.1 = ((f32[64,1,256]{2,1,0:T(1,128)}), f32[64,1,256]{2,1,0:T(1,128)S(1)}, u32[]{:S(2)}, u32[]{:S(2)}) async-start(f32[64,1,256]{2,1,0:T(1,128)} %copy.62), calls=%async_computation.1 | async-start | bytes 131072 | tf_op jit(solution)/shard_map/all_to_all | solution.py:105
  122.3 0.1 multiply_reduce_fusion.2
  122.4 0.1 broadcast_reduce_fusion
  122.5 0.1 div.44
  122.6 0.1 mul.244
  122.7 0.1 mul.240
  122.8 0.1 mul.241
  123.0 10.4 %all-to-all-done.1 = f32[64,1,256]{2,1,0:T(1,128)S(1)} async-done(((f32[64,1,256]{2,1,0:T(1,128)}), f32[64,1,256]{2,1,0:T(1,128)S(1)}, u32[]{:S(2)}, u32[]{:S(2)}) %all-to-all-start.1) | async-done | bytes 65568 | tf_op jit(solution)/shard_map/all_to_all | solution.py:105
  133.3 0.1 multiply_reduce_fusion.1
  133.5 1.5 convolution_bitcast_fusion
  135.1 0.6 reshape.552
  135.7 39.0 %reduce-scatter.4.cloned.1.call-done = f32[256,1]{1,0:T(8,128)} async-done(((f32[2048,1]{1,0:T(8,128)}), f32[256,1]{1,0:T(8,128)}) %reduce-scatter.4.cloned.1.call-update) | async-done | bytes 1040
  174.7 1.0 copy.68
  175.7 0.6 multiply_add_fusion
  (35 shorter events, 0.8 us)
Async XLA Ops:
  7.2 126.3 %copy-start = (bf16[256,2048]{1,0:T(8,128)(2,1)S(1)}, bf16[256,2048]{1,0:T(8,128)(2,1)}, u32[]{:S(2)}) copy-start(bf16[256,2048]{1,0:T(8,128)(2,1)} %param.12) | copy-start | bytes 3145732
  32.5 55.8 %copy-start.1 = (bf16[2048,128]{1,0:T(8,128)(2,1)S(1)}, bf16[2048,128]{1,0:T(8,128)(2,1)}, u32[]{:S(2)}) copy-start(bf16[2048,128]{1,0:T(8,128)(2,1)} %param.11) | copy-start | bytes 1572868
  33.8 54.8 %copy-start.2 = (f32[2048]{0:T(1024)S(1)}, f32[2048]{0:T(1024)}, u32[]{:S(2)}) copy-start(f32[2048]{0:T(1024)} %param.9) | copy-start | bytes 24580
  81.2 17.9 %all-to-all-start = ((f32[64,1,4]{2,1,0:T(1,128)}), f32[64,1,4]{2,1,0:T(1,128)S(1)}, u32[]{:S(2)}, u32[]{:S(2)}) async-start(f32[64,1,4]{2,1,0:T(1,128)} %copy.57), calls=%async_computation | async-start | bytes 65536 | tf_op jit(solution)/shard_map/all_to_all | solution.py:112
  92.2 83.4 %copy-start.3 = (f32[1,256]{1,0:T(1,128)S(1)}, f32[1,256]{1,0:T(1,128)}, u32[]{:S(2)}) copy-start(f32[1,256]{1,0:T(1,128)} %param.8) | copy-start | bytes 3076
  99.2 18.5 %all-to-all-start.2 = ((f32[64,1,4]{2,1,0:T(1,128)}), f32[64,1,4]{2,1,0:T(1,128)S(1)}, u32[]{:S(2)}, u32[]{:S(2)}) async-start(f32[64,1,4]{2,1,0:T(1,128)} %copy.64), calls=%async_computation.2 | async-start | bytes 65536 | tf_op jit(solution)/shard_map/all_to_all | solution.py:119
  117.6 15.7 %all-to-all-start.1 = ((f32[64,1,256]{2,1,0:T(1,128)}), f32[64,1,256]{2,1,0:T(1,128)S(1)}, u32[]{:S(2)}, u32[]{:S(2)}) async-start(f32[64,1,256]{2,1,0:T(1,128)} %copy.62), calls=%async_computation.1 | async-start | bytes 131072 | tf_op jit(solution)/shard_map/all_to_all | solution.py:105
  122.3 52.4 %reduce-scatter.4.cloned.1.call-start = ((), (), s32[]{:S(2)}) async-start(), calls=%async_computation.4 | async-start | bytes 1179648
Sparse Core Ops, SparseCore 0:
  135.2 39.4 reduce-scatter.3
where the time goes:
time: 184 us; the launch traced here: 183 us
  waiting for transfers between devices  64.6 us (35%)
  blocking collectives  56.2 us (31%)
  starting transfers between devices  19.4 us (11%)
  between operations  15.6 us (8%)
  local copies, waits for them, and re-layouts  10.2 us (6%)
  matrix products  10.1 us (5%)
  other arithmetic  6.91 us (4%)
    all_gather x1, blocking collectives, per_device(): lax.all_gather(queries.reshape(local_rows, q_heads * head_dim), 'pool', a...  41.4 us
    unnamed x2, waiting for transfers between devices  39 us
    all_gather x1, blocking collectives, per_device(): full_rows = lax.all_gather(hidden, 'mp', axis=1, tiled=True)  14.8 us
    all_to_all x1, waiting for transfers between devices, per_device(): lax.all_to_all(flat_sum.reshape(pool_size, local_rows, q_heads), 'pool',...  10.8 us
    all_to_all x1, waiting for transfers between devices, per_device(): lax.all_to_all(flat_out.reshape(pool_size, local_rows, q_heads * head_dim...  10.4 us
    all_to_all x1, starting transfers between devices, per_device(): lax.all_to_all(flat_sum.reshape(pool_size, local_rows, q_heads), 'pool',...  7.62 us
    all_to_all x1, starting transfers between devices, per_device(): lax.all_to_all(flat_max.reshape(pool_size, local_rows, q_heads), 'pool',...  7.1 us
    all_to_all x1, starting transfers between devices, per_device(): lax.all_to_all(flat_out.reshape(pool_size, local_rows, q_heads * head_dim...  4.61 us
  transfers between devices with their start and end apart: 4, of which 4 were waited for; matrix products, arithmetic and copies ran while one was open for 4% of the time, Pallas kernels for 0%

commit v1 on v0

v1 whole, which is shorter than its diff:
```python
import jax
import jax.numpy as jnp
from jax import lax
from jax.experimental import pallas as pl
from jax.experimental.pallas import tpu as pltpu
from jax.sharding import PartitionSpec as P

EPSILON = 1e-05
RESIDUAL_SCALE = 0.22
SCORE_SCALE = 0.015625
ROPE_BASE = 10000000.0
MASKED = -1e30

F32 = jnp.float32
BF16 = jnp.bfloat16
VMEM = pl.BlockSpec(memory_space=pltpu.VMEM)
SMEM = pl.BlockSpec(memory_space=pltpu.SMEM)


def lanes(shape):
    return lax.broadcasted_iota(jnp.int32, shape, len(shape) - 1)


def rows_of(shape):
    return lax.broadcasted_iota(jnp.int32, shape, 0)


def rope(x, cosine, sine, half):
    wide = x.shape[-1]
    ahead = pltpu.roll(x, wide - half, 1)
    behind = pltpu.roll(x, half, 1)
    first = lanes(x.shape) % (2 * half) < half
    return x * cosine + jnp.where(first, ahead, behind) * sine


def table_kernel(slots_here, block_len, base_ref, lengths_ref, slot_ref, out_ref):
    requests, blocks = slot_ref.shape
    base = base_ref[0]
    sub = lax.broadcasted_iota(jnp.int32, (8, blocks), 0)
    lane = lax.broadcasted_iota(jnp.int32, (8, blocks), 1)
    wanted, payload = [], []
    for v in range(requests // 8):
        length = jnp.zeros((8, blocks), jnp.int32)
        for i in range(8):
            length = jnp.where(sub == i, lengths_ref[8 * v + i], length)
        limit = length - lane * block_len
        here = slot_ref[pl.ds(8 * v, 8), :] - base
        wanted.append(jnp.where(limit > 0, here, -1))
        payload.append((sub + 8 * v) * 256 + jnp.minimum(limit, block_len))
    for tile in range(slots_here // 8):
        picked = jnp.zeros((8, blocks), jnp.int32)
        for i in range(8):
            found = jnp.zeros((8, blocks), jnp.int32)
            for w, p in zip(wanted, payload):
                found = jnp.where(w == 8 * tile + i, p, found)
            picked = jnp.where(sub == i, jnp.max(found, axis=0, keepdims=True), picked)
        out_ref[pl.ds(8 * tile, 8), :] = jnp.broadcast_to(
            jnp.max(picked.astype(F32), axis=1, keepdims=True), (8, blocks)
        ).astype(jnp.int32)


def normalise(rows_ref, gain_ref):
    chunks, wide = rows_ref.shape
    x = rows_ref[...]
    total = jnp.sum(jnp.sum(x * x, axis=1, keepdims=True), axis=0, keepdims=True)
    scale = lax.rsqrt(total * (1.0 / (chunks * wide)) + EPSILON)
    return (x * scale * gain_ref[...]).astype(BF16)


def project(normed, weight_ref):
    chunks, wide = normed.shape
    out = jnp.zeros((chunks, weight_ref.shape[1]), F32)
    row = rows_of(out.shape)
    for j in range(chunks):
        part = jnp.dot(
            normed, weight_ref[pl.ds(j * wide, wide), :], preferred_element_type=F32
        )
        out = out + jnp.where(row == j, part, 0.0)
    return jnp.sum(out, axis=0, keepdims=True)


def query_kernel(half, rows_ref, gain_ref, w_ref, cos_ref, sin_ref, out_ref, normed_ref):
    normed = normalise(rows_ref, gain_ref)
    normed_ref[...] = normed
    query = jnp.broadcast_to(project(normed, w_ref), (8, w_ref.shape[1]))
    query = rope(query, cos_ref[...], sin_ref[...], half).astype(BF16).astype(F32)
    for v in range(out_ref.shape[0] // 8):
        out_ref[pl.ds(8 * v, 8), :] = query


def keyval_kernel(
    half, normed_ref, w_ref, cos_ref, sin_ref, query_ref, kv_ref, self_ref, value_ref
):
    head_dim = 2 * half
    keyval = jnp.broadcast_to(project(normed_ref[...], w_ref), (8, w_ref.shape[1]))
    wide = keyval.shape[-1]
    turned = rope(keyval, cos_ref[:, :wide], sin_ref[:, :wide], half)
    is_key = lanes(keyval.shape) < head_dim
    both = jnp.where(is_key, turned, keyval).astype(BF16)
    kv_ref[...] = both[:1]
    both = both.astype(F32)
    swapped = pltpu.roll(both, head_dim, 1)
    key = jnp.where(is_key, both, swapped)
    value = jnp.where(is_key, swapped, both)
    for c in range(self_ref.shape[1] // wide):
        product = query_ref[:8, pl.ds(c * wide, wide)] * key
        low = jnp.sum(jnp.where(is_key, product, 0.0), axis=1, keepdims=True)
        high = jnp.sum(jnp.where(is_key, 0.0, product), axis=1, keepdims=True)
        self_ref[:, pl.ds(c * wide, wide)] = jnp.where(is_key, low, high) * SCORE_SCALE
        value_ref[:, pl.ds(c * wide, wide)] = value


def attend_kernel(
    head_dim, tab_ref, query_ref, kv_ref, out_ref, q_s, score_s, max_s, sum_s, acc_s
):
    slots_here, block_len, wide = kv_ref.shape
    requests = query_ref.shape[0]
    groups = query_ref.shape[1] // head_dim
    is_key = lanes((requests, wide)) < head_dim
    q_s[...] = jnp.zeros_like(q_s)
    for h in range(groups):
        chunk = query_ref[:, pl.ds((h // 2) * wide, wide)]
        if h % 2:
            chunk = pltpu.roll(chunk, head_dim, 1)
        q_s[:, h, :] = jnp.where(is_key, chunk, 0.0)
    max_s[...] = jnp.full_like(max_s, MASKED)
    sum_s[...] = jnp.zeros_like(sum_s)
    acc_s[...] = jnp.zeros_like(acc_s)
    token = lanes((8, block_len))
    step = 8

    def score(i, carry):
        for u in range(step):
            s = i * step + u
            entry = tab_ref[s]
            r = entry // 256
            limit = entry % 256
            q = q_s[r].astype(BF16)
            scores = lax.dot_general(
                q, kv_ref[s], (((1,), (1,)), ((), ())), preferred_element_type=F32
            )
            scores = jnp.where(token < limit, scores * SCORE_SCALE, MASKED)
            score_s[s] = scores
            top = jnp.broadcast_to(jnp.max(scores, axis=1, keepdims=True), scores.shape)
            max_s[r] = jnp.maximum(max_s[r], top)
        return carry

    lax.fori_loop(0, slots_here // step, score, 0)

    def gather(i, carry):
        for u in range(step):
            s = i * step + u
            entry = tab_ref[s]
            r = entry // 256
            limit = entry % 256
            weight = jnp.where(token < limit, jnp.exp(score_s[s] - max_s[r]), 0.0).astype(BF16)
            out = jnp.dot(weight, kv_ref[s], preferred_element_type=F32)
            total = jnp.sum(weight.astype(F32), axis=1, keepdims=True)
            acc_s[r] = acc_s[r] + out
            sum_s[r] = sum_s[r] + jnp.broadcast_to(total, out.shape)
        return carry

    lax.fori_loop(0, slots_here // step, gather, 0)

    for c in range(groups // 2):
        low = pltpu.roll(acc_s[:, 2 * c, :], head_dim, 1)
        out_ref[:, pl.ds(c * wide, wide)] = jnp.where(is_key, low, acc_s[:, 2 * c + 1, :])
    tail = jnp.zeros((requests, wide), F32)
    lane = lanes((requests, wide))
    for h in range(groups):
        tail = jnp.where(lane == h, max_s[:, h, :], tail)
        tail = jnp.where(lane == groups + h, sum_s[:, h, :], tail)
    out_ref[:, pl.ds(groups // 2 * wide, wide)] = tail


def combine_kernel(head_dim, got_ref, self_ref, value_ref, w_ref, out_ref):
    wide = 2 * head_dim
    parts = got_ref.shape[0]
    inner = self_ref.shape[1]
    groups = inner // head_dim
    tail = got_ref[:, pl.ds(inner, wide)]
    is_low = lanes((parts, wide)) < head_dim
    attended = []
    for c in range(inner // wide):
        here = pl.ds(c * wide, wide)
        tops = jnp.where(is_low, tail[:, 2 * c : 2 * c + 1], tail[:, 2 * c + 1 : 2 * c + 2])
        at = groups + 2 * c
        sums = jnp.where(is_low, tail[:, at : at + 1], tail[:, at + 1 : at + 2])
        own = self_ref[:1, here]
        overall = jnp.maximum(jnp.max(tops, axis=0, keepdims=True), own)
        weight = jnp.exp(tops - overall)
        own_weight = jnp.exp(own - overall)
        numerator = jnp.sum(weight * got_ref[:, here], axis=0, keepdims=True)
        denominator = jnp.sum(weight * sums, axis=0, keepdims=True)
        numerator = numerator + own_weight * value_ref[:1, here]
        attended.append(numerator / (denominator + own_weight))
    row = jnp.broadcast_to(jnp.concatenate(attended, axis=1), (8, inner)).astype(BF16)
    chunks, step = out_ref.shape
    for j in range(chunks):
        part = jnp.dot(row, w_ref[:, pl.ds(j * step, step)], preferred_element_type=F32)
        out_ref[pl.ds(j, 1), :] = part[:1]


def per_device(hidden, norm_gain, w_query, w_keyval, w_out, kv_cache, block_slot, lengths):
    slots_here, _, block_len, wide = kv_cache.shape
    head_dim = wide // 2
    half = head_dim // 2
    inner = w_query.shape[1]
    groups = inner // head_dim
    requests = block_slot.shape[0]
    shards = lax.axis_size("mp")
    features = hidden.shape[1]
    pool_index = lax.axis_index("pool")

    rows = lax.all_to_all(
        jnp.broadcast_to(hidden, (shards, features)), "mp", split_axis=0, concat_axis=0, tiled=True
    )

    position = lax.dynamic_slice_in_dim(lengths, pool_index, 1).astype(F32)
    lane = jnp.arange(inner, dtype=jnp.int32) % head_dim
    inverse = ROPE_BASE ** (-(lane % half).astype(F32) * 2.0 / head_dim)
    angle = (position[0] * inverse)[None, :]
    cosine = jnp.cos(angle)
    sine = jnp.where(lane[None, :] < half, -jnp.sin(angle), jnp.sin(angle))

    table = pl.pallas_call(
        lambda *refs: table_kernel(slots_here, block_len, *refs),
        out_shape=jax.ShapeDtypeStruct((slots_here, block_slot.shape[1]), jnp.int32),
        in_specs=[SMEM, SMEM, VMEM],
        out_specs=VMEM,
        name="slot_table",
    )((pool_index * slots_here).reshape(1).astype(jnp.int32), lengths, block_slot)[:, 0]

    query, normed = pl.pallas_call(
        lambda *refs: query_kernel(half, *refs),
        out_shape=(
            jax.ShapeDtypeStruct((requests, inner), F32),
            jax.ShapeDtypeStruct((shards, features), BF16),
        ),
        in_specs=[VMEM] * 5,
        out_specs=(VMEM, VMEM),
        name="query",
    )(rows, norm_gain.reshape(shards, features), w_query, cosine, sine)

    all_queries = lax.all_to_all(query, "pool", split_axis=0, concat_axis=0, tiled=True)

    new_kv, own_score, own_value = pl.pallas_call(
        lambda *refs: keyval_kernel(half, *refs),
        out_shape=(
            jax.ShapeDtypeStruct((1, wide), BF16),
            jax.ShapeDtypeStruct((8, inner), F32),
            jax.ShapeDtypeStruct((8, inner), F32),
        ),
        in_specs=[VMEM] * 5,
        out_specs=(VMEM, VMEM, VMEM),
        name="keyval",
    )(normed, w_keyval, cosine, sine, query)

    per_request = (requests, 8, wide)
    partial = pl.pallas_call(
        lambda *refs: attend_kernel(head_dim, *refs),
        out_shape=jax.ShapeDtypeStruct((requests, inner + wide), F32),
        in_specs=[SMEM, VMEM, VMEM],
        out_specs=VMEM,
        scratch_shapes=[
            pltpu.VMEM(per_request, F32),
            pltpu.VMEM((slots_here, 8, block_len), F32),
            pltpu.VMEM(per_request, F32),
            pltpu.VMEM(per_request, F32),
            pltpu.VMEM(per_request, F32),
        ],
        name="attend",
    )(table, all_queries, kv_cache.reshape(slots_here, block_len, wide))

    got = lax.all_to_all(partial, "pool", split_axis=0, concat_axis=0, tiled=True)

    mixed = pl.pallas_call(
        lambda *refs: combine_kernel(head_dim, *refs),
        out_shape=jax.ShapeDtypeStruct((shards, features), F32),
        in_specs=[VMEM] * 4,
        out_specs=VMEM,
        name="combine",
    )(got, own_score, own_value, w_out)

    spread = lax.all_to_all(mixed, "mp", split_axis=0, concat_axis=0, tiled=True)
    return (hidden + RESIDUAL_SCALE * jnp.sum(spread, axis=0, keepdims=True), new_kv)


def solution(mesh):
    return jax.shard_map(
        per_device,
        mesh=mesh,
        in_specs=(
            P("pool", "mp"),
            P(),
            P(None, "mp"),
            P(None, "mp"),
            P("mp", None),
            P("pool", "mp", None, None),
            P(),
            P(),
        ),
        out_specs=(P("pool", "mp"), P("pool", "mp")),
        check_vma=False,
    )
```

time: 184 us -> 87.5 us (0.48)
  waiting for transfers between devices: 64.6 us -> 17.9 us
  blocking collectives: 56.2 us -> 11 us
  Pallas kernels: 0 us -> 17.7 us
  between operations: 15.6 us -> 1.32 us
  matrix products: 10.1 us -> 0 us
  starting transfers between devices: 19.4 us -> 26.7 us
  other arithmetic: 6.91 us -> 1.23 us
    all_gather x2 -> x0, blocking collectives: 56.2 us -> none  [the longest x1 41.4 us: per_device(): lax.all_gather(queries.reshape(local_rows, q_heads * head_dim), 'pool', a...]
    unnamed x2 -> x0, waiting for transfers between devices: 39 us -> none
    pallas_call x0 -> x5, Pallas kernels: none -> 17.7 us  [the longest x1 9.19 us: per_device(): pl.pallas_call(lambda *refs: attend_kernel(head_dim, *refs), out_shape=ja...]
    all_to_all x0 -> x1, blocking collectives: none -> 11 us  [per_device(): lax.all_to_all(mixed, 'mp', split_axis=0, concat_axis=0, tiled=True)]
    dot_general x5 -> x0, matrix products: 8.55 us -> none  [the longest x1 3.71 us: per_device(): jnp.einsum('skgd,sktd->skgt', slot_query, cache_keys, preferred_element_t...]
    all_to_all x3, waiting for transfers between devices: 25.7 us -> 17.9 us  [the longest x1 9.24 us: per_device(): lax.all_to_all(partial, 'pool', split_axis=0, concat_axis=0, tiled=True)]
    all_to_all x3, starting transfers between devices: 19.3 us -> 26.7 us  [the longest x1 12 us: per_device(): lax.all_to_all(query, 'pool', split_axis=0, concat_axis=0, tiled=True)]
    all_to_all x0 -> x3, local copies, waits for them, and re-layouts: none -> 3.87 us  [the longest x1 1.63 us: per_device(): lax.all_to_all(partial, 'pool', split_axis=0, concat_axis=0, tiled=True)]
  transfers between devices with their start and end apart: 4 -> 3, of which waited for: 4 -> 3; matrix products, arithmetic and copies ran while one was open for 4% -> 5% of each run, Pallas kernels for 0% -> 4%
where the time goes in v1:
time: 87.5 us; the launch traced here: 86.8 us
  starting transfers between devices  26.7 us (31%)
  waiting for transfers between devices  17.9 us (20%)
  Pallas kernels  17.7 us (20%)
  local copies, waits for them, and re-layouts  11 us (13%)
  blocking collectives  11 us (13%)
  between operations  1.32 us (2%)
  other arithmetic  1.23 us (1%)
    all_to_all x1, starting transfers between devices, per_device(): lax.all_to_all(query, 'pool', split_axis=0, concat_axis=0, tiled=True)  12 us
    all_to_all x1, blocking collectives, per_device(): lax.all_to_all(mixed, 'mp', split_axis=0, concat_axis=0, tiled=True)  11 us
    all_to_all x1, starting transfers between devices, per_device(): lax.all_to_all(jnp.broadcast_to(hidden, (shards, features)), 'mp', split_...  10.1 us
    all_to_all x1, waiting for transfers between devices, per_device(): lax.all_to_all(partial, 'pool', split_axis=0, concat_axis=0, tiled=True)  9.24 us
    pallas_call x1, Pallas kernels, per_device(): pl.pallas_call(lambda *refs: attend_kernel(head_dim, *refs), out_shape=ja...  9.19 us
    all_to_all x1, waiting for transfers between devices, per_device(): lax.all_to_all(query, 'pool', split_axis=0, concat_axis=0, tiled=True)  7.83 us
    all_to_all x1, starting transfers between devices, per_device(): lax.all_to_all(partial, 'pool', split_axis=0, concat_axis=0, tiled=True)  4.6 us
    pallas_call x1, Pallas kernels, per_device(): pl.pallas_call(lambda *refs: combine_kernel(head_dim, *refs), out_shape=j...  2.31 us
  transfers between devices with their start and end apart: 3, of which 3 were waited for; matrix products, arithmetic and copies ran while one was open for 5% of the time, Pallas kernels for 4%

profile of v1, /device:TPU:1, one launch (start us, length us, event | category | flops | bytes accessed | tf_op | source)
XLA Modules:
  0.0 86.8 jit_solution(17821815735578801018)
XLA Ops:
  0.6 1.3 %broadcast_in_dim.2 = f32[8,1,256]{2,1,0:T(1,128)} broadcast(f32[256]{0:T(256)} %bitcast.24), dimensions={2} | broadcast | bytes 9216 | tf_op jit(solution)/shard_map/broadcast_in_dim | solution.py:216
  1.9 10.1 %all-to-all-start = ((f32[8,1,256]{2,1,0:T(1,128)}), f32[8,1,256]{2,1,0:T(1,128)S(1)}, u32[]{:S(2)}, u32[]{:S(2)}) async-start(f32[8,1,256]{2,1,0:T(1,128)} %broadcast_in_dim.2), calls=%async_computation | async-start | bytes 16384 | tf_op jit(solution)/shard_map/all_to_all | solution.py:215
  12.0 1.2 %dynamic_slice.3 = s32[1]{0:T(128)} dynamic-slice(s32[64]{0:T(128)} %refs_1_.2, s32[]{:T(128)S(6)} %select_n.42), dynamic_slice_sizes={1} | dynamic-slice | bytes 12 | tf_op jit(solution)/shard_map/dynamic_slice | solution.py:219
  13.9 0.6 compare_select_fusion.2
  14.5 1.3 %reshape.127.refs_1_ = f32[8,256]{1,0:T(8,128)} reshape(f32[2048]{0:T(1024)} %param.9) | data formatting | bytes 16384 | tf_op jit(solution)/shard_map/reshape | solution.py:243
  15.8 0.8 all-to-all-done
  16.6 0.6 copy.21
  17.2 2.3 %query.1 = (f32[64,256]{1,0:T(8,128)}, bf16[8,256]{1,0:T(8,128)(2,1)}) custom-call(f32[8,256]{1,0:T(8,128)} %bitcast.22, f32[8,256]{1,0:T(8,128)} %reshape.127.refs_1_, bf16[2048,256]{1,0:T(8,128)(2,1)} %refs_2_.3, f32[1,256]{1,0:T(1,128)} %get-tuple-element.13.refs_3_.refs_2_, f32[1,256]{1,0:T(1,128)} %get-tuple-element.12.refs_4_.refs_3_), custom_call_target="tpu_custom_call" | custom-call | tf_op jit(solution)/shard_map/query/pallas_call | solution.py:234
  19.5 0.0 copy-start
  19.5 1.5 %copy.10 = f32[64,1,256]{2,1,0:T(1,128)} copy(f32[64,1,256]{2,0,1:T(8,128)} %bitcast.20) | data formatting | bytes 131072 | tf_op jit(solution)/shard_map/all_to_all | solution.py:245
  21.0 12.0 %all-to-all-start.1 = ((f32[64,1,256]{2,1,0:T(1,128)}), f32[64,1,256]{2,1,0:T(1,128)S(1)}, u32[]{:S(2)}, u32[]{:S(2)}) async-start(f32[64,1,256]{2,1,0:T(1,128)} %copy.10), calls=%async_computation.1 | async-start | bytes 131072 | tf_op jit(solution)/shard_map/all_to_all | solution.py:245
  33.1 1.8 %slot_table.1 = s32[96,128]{1,0:T(8,128)} custom-call(s32[1]{0:T(128)} %bitcast.refs_0_, s32[64]{0:T(128)} %refs_1_.2, s32[64,128]{1,0:T(8,128)} %refs_2_.2), custom_call_target="tpu_custom_call" | custom-call | tf_op jit(solution)/shard_map/slot_table/pallas_call | solution.py:226
  34.9 1.4 %slice_reduce_fusion.refs_0_ = s32[96]{0:T(128)} fusion(s32[96,128]{1,0:T(8,128)} %slot_table.1), kind=kLoop, calls=%fused_computation.2 | loop fusion | bytes 768 | tf_op jit(solution)/shard_map/slice | solution.py:226
  36.3 7.8 %all-to-all-done.1 = f32[64,1,256]{2,1,0:T(1,128)S(1)} async-done(((f32[64,1,256]{2,1,0:T(1,128)}), f32[64,1,256]{2,1,0:T(1,128)S(1)}, u32[]{:S(2)}, u32[]{:S(2)}) %all-to-all-start.1) | async-done | bytes 65568 | tf_op jit(solution)/shard_map/all_to_all | solution.py:245
  44.2 0.6 copy.20
  44.8 9.2 %attend.1 = f32[64,384]{1,0:T(8,128)} custom-call(s32[96]{0:T(128)} %slice_reduce_fusion.refs_0_, f32[64,256]{1,0:T(8,128)} %bitcast.21, bf16[96,128,128]{2,1,0:T(8,128)(2,1)} %bitcast.17), custom_call_target="tpu_custom_call" | custom-call | tf_op jit(solution)/shard_map/attend/pallas_call | solution.py:260
  54.0 1.6 %copy.11 = f32[64,1,384]{2,1,0:T(1,128)} copy(f32[64,1,384]{2,0,1:T(8,128)} %bitcast.18) | data formatting | bytes 196608 | tf_op jit(solution)/shard_map/all_to_all | solution.py:275
  55.6 4.6 %all-to-all-start.2 = ((f32[64,1,384]{2,1,0:T(1,128)}), f32[64,1,384]{2,1,0:T(1,128)S(1)}, u32[]{:S(2)}, u32[]{:S(2)}) async-start(f32[64,1,384]{2,1,0:T(1,128)} %copy.11), calls=%async_computation.2 | async-start | bytes 196608 | tf_op jit(solution)/shard_map/all_to_all | solution.py:275
  60.2 2.1 %keyval.1 = (bf16[1,128]{1,0:T(2,128)(2,1)}, f32[8,256]{1,0:T(8,128)}, f32[8,256]{1,0:T(8,128)}) custom-call(bf16[8,256]{1,0:T(8,128)(2,1)} %get-tuple-element.8.refs_0_, bf16[2048,128]{1,0:T(8,128)(2,1)} %refs_1_.3, f32[1,256]{1,0:T(1,128)} %get-tuple-element.13.refs_3_.refs_2_, f32[1,256]{1,0:T(1,128)} %get-tuple-element.12.refs_4_.refs_3_, ...), custom_call_target="tpu_custom_call" | custom-call | tf_op jit(solution)/shard_map/keyval/pallas_call | solution.py:247
  62.3 9.2 %all-to-all-done.2 = f32[64,1,384]{2,1,0:T(1,128)S(1)} async-done(((f32[64,1,384]{2,1,0:T(1,128)}), f32[64,1,384]{2,1,0:T(1,128)S(1)}, u32[]{:S(2)}, u32[]{:S(2)}) %all-to-all-start.2) | async-done | bytes 98336 | tf_op jit(solution)/shard_map/all_to_all | solution.py:275
  71.5 0.6 copy.19
  72.2 2.3 %combine.1 = f32[8,256]{1,0:T(8,128)} custom-call(f32[64,384]{1,0:T(8,128)} %bitcast.19, f32[8,256]{1,0:T(8,128)} %get-tuple-element.9.refs_1_, f32[8,256]{1,0:T(8,128)} %get-tuple-element.10.refs_2_, bf16[256,2048]{1,0:T(8,128)(2,1)} %refs_3_.1), custom_call_target="tpu_custom_call" | custom-call | tf_op jit(solution)/shard_map/combine/pallas_call | solution.py:277
  74.5 0.7 copy.12
  75.2 11.0 %all_to_all.39 = f32[8,1,256]{2,1,0:T(1,128)S(1)} all-to-all(f32[8,1,256]{2,1,0:T(1,128)S(1)} %copy.12), channel_id=1, replica_groups=mesh['pool'=64,'mp'=8] {'mp'}, dimensions={0} | all-to-all | bytes 16384 | tf_op jit(solution)/shard_map/all_to_all | solution.py:285
  86.3 0.0 copy-done
  86.3 0.6 add.43
  (2 shorter events, 0.0 us)
Async XLA Ops:
  1.9 14.7 %all-to-all-start = ((f32[8,1,256]{2,1,0:T(1,128)}), f32[8,1,256]{2,1,0:T(1,128)S(1)}, u32[]{:S(2)}, u32[]{:S(2)}) async-start(f32[8,1,256]{2,1,0:T(1,128)} %broadcast_in_dim.2), calls=%async_computation | async-start | bytes 16384 | tf_op jit(solution)/shard_map/all_to_all | solution.py:215
  19.5 66.8 %copy-start = (f32[1,256]{1,0:T(1,128)S(1)}, f32[1,256]{1,0:T(1,128)}, u32[]{:S(2)}) copy-start(f32[1,256]{1,0:T(1,128)} %param.8) | copy-start | bytes 3076
  21.0 23.1 %all-to-all-start.1 = ((f32[64,1,256]{2,1,0:T(1,128)}), f32[64,1,256]{2,1,0:T(1,128)S(1)}, u32[]{:S(2)}, u32[]{:S(2)}) async-start(f32[64,1,256]{2,1,0:T(1,128)} %copy.10), calls=%async_computation.1 | async-start | bytes 131072 | tf_op jit(solution)/shard_map/all_to_all | solution.py:245
  55.6 15.9 %all-to-all-start.2 = ((f32[64,1,384]{2,1,0:T(1,128)}), f32[64,1,384]{2,1,0:T(1,128)S(1)}, u32[]{:S(2)}, u32[]{:S(2)}) async-start(f32[64,1,384]{2,1,0:T(1,128)} %copy.11), calls=%async_computation.2 | async-start | bytes 196608 | tf_op jit(solution)/shard_map/all_to_all | solution.py:275

commit v2 on v0

v2 whole, which is shorter than its diff:
```python
import functools
import math

import jax
import jax.numpy as jnp
from jax import lax
from jax.experimental import pallas as pl
from jax.experimental.pallas import tpu as pltpu
from jax.sharding import PartitionSpec as P

EPSILON = 1e-05
RESIDUAL_SCALE = 0.22
SCORE_SCALE = 0.015625
ROPE_BASE = 10000000.0
MASKED = -1e30

F32 = jnp.float32
BF16 = jnp.bfloat16
VMEM = pl.BlockSpec(memory_space=pltpu.VMEM)
SMEM = pl.BlockSpec(memory_space=pltpu.SMEM)
HBM = pl.BlockSpec(memory_space=pltpu.HBM)

GROUP = 4


def far(x):
    return pltpu.with_memory_space_constraint(x, pltpu.HBM)


def lanes(shape):
    return lax.broadcasted_iota(jnp.int32, shape, len(shape) - 1)


def subs(shape):
    return lax.broadcasted_iota(jnp.int32, shape, len(shape) - 2)


def call(body, name, out_shape, in_specs, scratch=(), limit=4 << 20):
    many = isinstance(out_shape, tuple)
    return pl.pallas_call(
        body,
        out_shape=out_shape,
        in_specs=in_specs,
        out_specs=(VMEM,) * len(out_shape) if many else VMEM,
        scratch_shapes=list(scratch),
        compiler_params=pltpu.CompilerParams(vmem_limit_bytes=limit),
        name=name,
    )


def sine_cosine(angle):
    turn = jnp.floor(angle * (2.0 / math.pi) + 0.5)
    x = ((angle - turn * 1.5703125) - turn * 4.837512969970703e-4) - turn * 7.54978995489188e-8
    z = x * x
    sine = ((-1.9515295891e-4 * z + 8.3321608736e-3) * z - 1.6666654611e-1) * z * x + x
    cosine = ((2.443315711809948e-5 * z - 1.388731625493765e-3) * z + 4.166664568298827e-2) * z * z
    cosine = cosine - 0.5 * z + 1.0
    quadrant = turn.astype(jnp.int32) & 3
    odd = (quadrant & 1) == 1
    out_sine = jnp.where(odd, cosine, sine)
    out_cosine = jnp.where(odd, sine, cosine)
    out_sine = jnp.where(quadrant >= 2, -out_sine, out_sine)
    out_cosine = jnp.where((quadrant == 1) | (quadrant == 2), -out_cosine, out_cosine)
    return out_sine, out_cosine


def rotation(position, head_dim, width):
    half = head_dim // 2
    lane = lanes((8, width))
    pair = lane % half
    inverse = jnp.zeros((8, width), F32)
    for i in range(half):
        inverse = jnp.where(pair == i, ROPE_BASE ** (-2.0 * i / head_dim), inverse)
    sine, cosine = sine_cosine(position.astype(F32) * inverse)
    return cosine, jnp.where(lane % head_dim < half, -sine, sine)


def rope(x, cosine, sine, half):
    ahead = pltpu.roll(x, x.shape[1] - half, 1)
    behind = pltpu.roll(x, half, 1)
    first = lanes(x.shape) % (2 * half) < half
    return x * cosine + jnp.where(first, ahead, behind) * sine


def normalise(rows_ref, gain_ref):
    count = rows_ref.shape[0]
    x = rows_ref[...]
    total = jnp.sum(jnp.sum(x * x, axis=0, keepdims=True), axis=1, keepdims=True)
    scale = lax.rsqrt(total * (1.0 / x.size) + EPSILON)
    half = count // 2
    even = pl.ds(0, half, stride=2)
    odd = pl.ds(1, half, stride=2)
    left = rows_ref[even, :] * scale * gain_ref[even, :]
    right = rows_ref[odd, :] * scale * gain_ref[odd, :]
    return jnp.concatenate([left, right], axis=1)


def project(normed, weight_ref):
    chunks, wide = normed.shape
    row = subs(normed.shape)
    out = None
    for j in range(chunks):
        part = jnp.dot(
            jnp.where(row == j, normed, 0.0).astype(BF16),
            weight_ref[pl.ds(j * wide, wide), :],
            preferred_element_type=F32,
        )
        out = part if out is None else out + part
    return jnp.broadcast_to(jnp.sum(out, axis=0, keepdims=True), out.shape)


def fetch(sources, targets, sems):
    copies = [pltpu.make_async_copy(s, t, sems.at[i]) for i, (s, t) in enumerate(zip(sources, targets))]
    for copy in copies:
        copy.start()
    return copies


def prepare_kernel(
    head_dim, place_ref, lengths_ref, w_ref, gain_ref, held_w_ref, held_gain_ref, cos_ref, sin_ref, sems
):
    copies = fetch((w_ref, gain_ref), (held_w_ref, held_gain_ref), sems)
    cos_ref[...], sin_ref[...] = rotation(lengths_ref[place_ref[0]], head_dim, 2 * head_dim)
    for copy in copies:
        copy.wait()


def query_kernel(head_dim, rows_ref, gain_ref, w_ref, cos_ref, sin_ref, out_ref):
    wide = 2 * head_dim
    cosine, sine = cos_ref[...], sin_ref[...]
    query = project(normalise(rows_ref, gain_ref), w_ref)
    row = subs((8, wide)) % GROUP
    tile = jnp.zeros((8, wide), F32)
    for c in range(GROUP // 2):
        part = rope(query[:, c * wide : (c + 1) * wide], cosine, sine, head_dim // 2)
        tile = jnp.where(row == 2 * c, part, tile)
        tile = jnp.where(row == 2 * c + 1, pltpu.roll(part, head_dim, 1), tile)
    tile = tile.astype(BF16).astype(F32) * SCORE_SCALE
    tile = jnp.where(lanes(tile.shape) < head_dim, tile, 0.0)
    for v in range(out_ref.shape[0] // 8):
        out_ref[pl.ds(8 * v, 8), :] = tile


def keyval_kernel(head_dim, rows_ref, gain_ref, cos_ref, sin_ref, query_ref, w_ref, w_out_ref, *rest):
    kv_ref, own_ref, held_ref, near_ref, sems = rest
    copies = fetch((w_ref, w_out_ref), (near_ref, held_ref), sems)
    normed = normalise(rows_ref, gain_ref)
    copies[0].wait()
    keyval = project(normed, near_ref)
    is_key = lanes(keyval.shape) < head_dim
    turned = rope(keyval, cos_ref[...], sin_ref[...], head_dim // 2)
    both = jnp.where(is_key, turned, keyval).astype(BF16)
    kv_ref[...] = both[:1]
    both = both.astype(F32)
    score = jnp.sum(query_ref[:8, :] * both, axis=1, keepdims=True)
    own_ref[...] = jnp.where(is_key, score, both)
    copies[1].wait()


def table_kernel(
    slots_here, block_len, place_ref, lengths_ref, slot_ref, *rest
):
    kv_ref, out_ref, held_ref, sems = rest
    copies = fetch((kv_ref,), (held_ref,), sems)
    requests, blocks = slot_ref.shape
    base = place_ref[0] * slots_here
    sub = subs((8, blocks))
    lane = lanes((8, blocks))
    wanted, payload = [], []
    for v in range(requests // 8):
        length = jnp.zeros((8, blocks), jnp.int32)
        for i in range(8):
            length = jnp.where(sub == i, lengths_ref[8 * v + i], length)
        limit = length - lane * block_len
        here = slot_ref[pl.ds(8 * v, 8), :] - base
        wanted.append(jnp.where(limit > 0, here, -1))
        payload.append((sub + 8 * v) * 256 + jnp.minimum(limit, block_len))
    for tile in range(slots_here // 8):
        picked = jnp.zeros((8, blocks), jnp.int32)
        for i in range(8):
            found = jnp.zeros((8, blocks), jnp.int32)
            for w, p in zip(wanted, payload):
                found = jnp.where(w == 8 * tile + i, p, found)
            picked = jnp.where(sub == i, jnp.max(found, axis=0, keepdims=True), picked)
        out_ref[pl.ds(8 * tile, 8), :] = jnp.broadcast_to(
            jnp.max(picked.astype(F32), axis=1, keepdims=True), (8, blocks)
        ).astype(jnp.int32)
    for copy in copies:
        copy.wait()


def attend_kernel(tab_ref, query_ref, kv_ref, out_ref, q_s, score_s, max_s, sum_s, acc_s):
    slots_here, block_len, wide = kv_ref.shape
    requests = query_ref.shape[0] // GROUP
    low = subs((8, wide)) < GROUP
    token = lanes((8, block_len))
    lane = lanes((8, wide))
    for v in range(requests // 2):
        tile = query_ref[pl.ds(8 * v, 8), :]
        other = pltpu.roll(tile, GROUP, 0)
        q_s[2 * v] = jnp.where(low, tile, other)
        q_s[2 * v + 1] = jnp.where(low, other, tile)
    max_s[...] = jnp.full_like(max_s, MASKED)
    sum_s[...] = jnp.zeros_like(sum_s)
    acc_s[...] = jnp.zeros_like(acc_s)

    def pair(p):
        a, b = tab_ref[2 * p], tab_ref[2 * p + 1]
        live = token < jnp.where(low, a & 255, b & 255)
        keys = kv_ref[pl.ds(2 * p, 2)].reshape(2 * block_len, wide)
        return lax.shift_right_logical(a, 8), lax.shift_right_logical(b, 8), live, keys

    for p in range(slots_here // 2):
        ra, rb, live, keys = pair(p)
        query = jnp.where(low, q_s[ra], q_s[rb]).astype(BF16)
        scores = lax.dot_general(
            query, keys, (((1,), (1,)), ((), ())), preferred_element_type=F32
        )
        scores = jnp.where(low, scores[:, :block_len], scores[:, block_len:])
        scores = jnp.where(live, scores, MASKED)
        score_s[p] = scores
        top = jnp.broadcast_to(jnp.max(scores, axis=1, keepdims=True), scores.shape)
        max_s[ra] = jnp.maximum(max_s[ra], jnp.where(low, top, MASKED))
        max_s[rb] = jnp.maximum(max_s[rb], jnp.where(low, MASKED, top))

    for r in range(requests):
        top = max_s[r]
        max_s[r] = jnp.maximum(top, pltpu.roll(top, GROUP, 0))

    for p in range(slots_here // 2):
        ra, rb, live, values = pair(p)
        top = jnp.where(low, max_s[ra], max_s[rb])
        weight = jnp.where(live, jnp.exp(score_s[p] - top), 0.0).astype(BF16).astype(F32)
        both = jnp.concatenate(
            [jnp.where(low, weight, 0.0), jnp.where(low, 0.0, weight)], axis=1
        ).astype(BF16)
        out = jnp.dot(both, values, preferred_element_type=F32)
        total = jnp.broadcast_to(jnp.sum(weight, axis=1, keepdims=True), out.shape)
        acc_s[ra] = acc_s[ra] + jnp.where(low, out, 0.0)
        acc_s[rb] = acc_s[rb] + jnp.where(low, 0.0, out)
        sum_s[ra] = sum_s[ra] + jnp.where(low, total, 0.0)
        sum_s[rb] = sum_s[rb] + jnp.where(low, 0.0, total)

    for v in range(requests // 2):
        tiles = []
        for r in (2 * v, 2 * v + 1):
            out = acc_s[r] + pltpu.roll(acc_s[r], GROUP, 0)
            total = sum_s[r] + pltpu.roll(sum_s[r], GROUP, 0)
            tiles.append(
                jnp.where(lane < wide // 4, max_s[r], jnp.where(lane < wide // 2, total, out))
            )
        out_ref[pl.ds(8 * v, 8), :] = jnp.where(low, tiles[0], tiles[1])


def combine_kernel(got_ref, own_ref, w_ref, out_ref):
    rows, wide = got_ref.shape
    lane = lanes((8, wide))
    row = subs((8, wide))
    parts = [got_ref[pl.ds(8 * v, 8), :] for v in range(rows // 8)]
    top = parts[0]
    for part in parts[1:]:
        top = jnp.maximum(top, part)
    own = own_ref[...]
    top = jnp.maximum(jnp.maximum(top, pltpu.roll(top, GROUP, 0)), own)
    mixed = jnp.zeros((8, wide), F32)
    for part in parts:
        weight = jnp.exp(part - top)
        mixed = mixed + jnp.broadcast_to(weight[:, :1], part.shape) * part
    mixed = mixed + pltpu.roll(mixed, GROUP, 0)
    own_weight = jnp.exp(own - top)
    mixed = mixed + jnp.broadcast_to(own_weight[:, :1], own.shape) * jnp.where(
        lane < wide // 2, 1.0, own
    )
    attended = mixed / jnp.broadcast_to(mixed[:, wide // 4 : wide // 4 + 1], mixed.shape)
    swapped = pltpu.roll(attended, wide // 2, 1)
    placed = jnp.where(
        row % 2 == 0,
        jnp.where(lane < wide // 2, swapped, 0.0),
        jnp.where(lane < wide // 2, 0.0, attended),
    )
    chunks = [
        jnp.sum(jnp.where(row // 2 == c, placed, 0.0), axis=0, keepdims=True)
        for c in range(GROUP // 2)
    ]
    line = jnp.broadcast_to(jnp.concatenate(chunks, axis=1), (8, GROUP // 2 * wide)).astype(BF16)
    for v in range(out_ref.shape[0] // 8):
        part = jnp.dot(
            line, w_ref[:, pl.ds(8 * v * wide, 8 * wide)], preferred_element_type=F32
        )
        tile = jnp.zeros((8, wide), F32)
        for k in range(8):
            tile = jnp.where(row == k, part[:, k * wide : (k + 1) * wide], tile)
        out_ref[pl.ds(8 * v, 8), :] = tile


def exchange(x, axis, parts):
    shape = x.shape
    x = x.reshape(parts, shape[0] // parts, shape[1])
    return lax.all_to_all(x, axis, split_axis=0, concat_axis=0, tiled=True).reshape(shape)


def per_device(hidden, norm_gain, w_query, w_keyval, w_out, kv_cache, block_slot, lengths):
    slots_here, _, block_len, wide = kv_cache.shape
    head_dim = wide // 2
    requests = block_slot.shape[0]
    shards = lax.axis_size("mp")
    pools = lax.axis_size("pool")
    features = hidden.shape[1]
    lines = features // wide
    place = lax.axis_index("pool").astype(jnp.int32).reshape(1)
    rows = exchange(
        jnp.broadcast_to(hidden.reshape(1, lines, wide), (shards, lines, wide)).reshape(-1, wide),
        "mp",
        shards,
    )
    gain = norm_gain.reshape(shards * lines, wide)

    turn = jax.ShapeDtypeStruct((8, wide), F32)
    w_query, w_keyval, w_out, gain = (far(x) for x in (w_query, w_keyval, w_out, gain))
    held_query, held_gain, cosine, sine = call(
        functools.partial(prepare_kernel, head_dim),
        "prepare",
        (
            jax.ShapeDtypeStruct(w_query.shape, BF16),
            jax.ShapeDtypeStruct(gain.shape, F32),
            turn,
            turn,
        ),
        [SMEM, SMEM, HBM, HBM],
        [pltpu.SemaphoreType.DMA((2,))],
    )(place, lengths, w_query, gain)

    query = call(
        functools.partial(query_kernel, head_dim),
        "query",
        jax.ShapeDtypeStruct((requests * GROUP, wide), F32),
        [VMEM] * 5,
    )(rows, held_gain, held_query, cosine, sine)

    queries = exchange(query, "pool", pools)

    cache = far(kv_cache.reshape(slots_here, block_len, wide))
    table, held_cache = call(
        functools.partial(table_kernel, slots_here, block_len),
        "slot_table",
        (
            jax.ShapeDtypeStruct((slots_here, block_slot.shape[1]), jnp.int32),
            jax.ShapeDtypeStruct(cache.shape, BF16),
        ),
        [SMEM, SMEM, VMEM, HBM],
        [pltpu.SemaphoreType.DMA((1,))],
        limit=8 << 20,
    )(place, lengths, block_slot, cache)
    table = table[:, 0]

    new_kv, own, held_out = call(
        functools.partial(keyval_kernel, head_dim),
        "keyval",
        (
            jax.ShapeDtypeStruct((1, wide), BF16),
            turn,
            jax.ShapeDtypeStruct(w_out.shape, BF16),
        ),
        [VMEM] * 5 + [HBM] * 2,
        [pltpu.VMEM(w_keyval.shape, BF16), pltpu.SemaphoreType.DMA((2,))],
    )(rows, held_gain, cosine, sine, query, w_keyval, w_out)

    per_request = pltpu.VMEM((requests, 8, wide), F32)
    partial = call(
        attend_kernel,
        "attend",
        jax.ShapeDtypeStruct((requests * GROUP, wide), F32),
        [SMEM, VMEM, VMEM],
        [
            per_request,
            pltpu.VMEM((slots_here // 2, 8, block_len), F32),
            per_request,
            per_request,
            per_request,
        ],
        limit=12 << 20,
    )(table, queries, held_cache)

    got = exchange(partial, "pool", pools)

    mixed = call(
        combine_kernel,
        "combine",
        jax.ShapeDtypeStruct((shards * lines, wide), F32),
        [VMEM, VMEM, VMEM],
    )(got, own, held_out)

    spread = exchange(mixed, "mp", shards)
    total = jnp.sum(spread.reshape(shards, features), axis=0, keepdims=True)
    return (hidden + RESIDUAL_SCALE * total, new_kv)


def solution(mesh):
    return jax.shard_map(
        per_device,
        mesh=mesh,
        in_specs=(
            P("pool", "mp"),
            P(),
            P(None, "mp"),
            P(None, "mp"),
            P("mp", None),
            P("pool", "mp", None, None),
            P(),
            P(),
        ),
        out_specs=(P("pool", "mp"), P("pool", "mp")),
        check_vma=False,
    )
```

time: 184 us -> 72.4 us (0.39)
  waiting for transfers between devices: 64.6 us -> 18.5 us
  blocking collectives: 56.2 us -> 10.3 us
  between operations: 15.6 us -> 0.7 us
  Pallas kernels: 0 us -> 11.7 us
  matrix products: 10.1 us -> 0 us
  starting transfers between devices: 19.4 us -> 26.7 us
  local copies, waits for them, and re-layouts: 10.2 us -> 3.45 us
  other arithmetic: 6.91 us -> 0.59 us
    all_gather x2 -> x0, blocking collectives: 56.2 us -> none  [the longest x1 41.4 us: per_device(): lax.all_gather(queries.reshape(local_rows, q_heads * head_dim), 'pool', a...]
    unnamed x2 -> x0, waiting for transfers between devices: 39 us -> none
    pallas_call x0 -> x6, Pallas kernels: none -> 11.7 us  [the longest x1 3.01 us: per_device(): call(attend_kernel, 'attend', jax.ShapeDtypeStruct((requests * GROUP, wid...]
    all_to_all x0 -> x1, blocking collectives: none -> 10.3 us  [exchange(): lax.all_to_all(x, axis, split_axis=0, concat_axis=0, tiled=True)]
    dot_general x5 -> x0, matrix products: 8.55 us -> none  [the longest x1 3.71 us: per_device(): jnp.einsum('skgd,sktd->skgt', slot_query, cache_keys, preferred_element_t...]
    all_to_all x3, starting transfers between devices: 19.3 us -> 26.7 us  [exchange(): lax.all_to_all(x, axis, split_axis=0, concat_axis=0, tiled=True)]
    all_to_all x3, waiting for transfers between devices: 25.7 us -> 18.5 us  [exchange(): lax.all_to_all(x, axis, split_axis=0, concat_axis=0, tiled=True)]
    reduce_sum x7 -> x1, other arithmetic: 3.3 us -> 0.02 us  [per_device(): total = jnp.sum(spread.reshape(shards, features), axis=0, keepdims=True)]
  transfers between devices with their start and end apart: 4 -> 3, of which waited for: 4 -> 3; matrix products, arithmetic and copies ran while one was open for 4% -> 0% of each run, Pallas kernels for 0% -> 10%
where the time goes in v2:
time: 72.4 us; the launch traced here: 71.9 us
  starting transfers between devices  26.7 us (37%)
  waiting for transfers between devices  18.5 us (26%)
  Pallas kernels  11.7 us (16%)
  blocking collectives  10.3 us (14%)
  local copies, waits for them, and re-layouts  3.45 us (5%)
    all_to_all x3, starting transfers between devices, exchange(): lax.all_to_all(x, axis, split_axis=0, concat_axis=0, tiled=True)  26.7 us
    all_to_all x3, waiting for transfers between devices, exchange(): lax.all_to_all(x, axis, split_axis=0, concat_axis=0, tiled=True)  18.5 us
    all_to_all x1, blocking collectives, exchange(): lax.all_to_all(x, axis, split_axis=0, concat_axis=0, tiled=True)  10.3 us
    pallas_call x1, Pallas kernels, per_device(): call(attend_kernel, 'attend', jax.ShapeDtypeStruct((requests * GROUP, wid...  3.01 us
    pallas_call x1, Pallas kernels, per_device(): call(functools.partial(keyval_kernel, head_dim), 'keyval', (jax.ShapeDtyp...  2.82 us
    pallas_call x1, Pallas kernels, per_device(): call(functools.partial(table_kernel, slots_here, block_len), 'slot_table'...  2.46 us
    unnamed x8, local copies, waits for them, and re-layouts  2.07 us
    pallas_call x1, Pallas kernels, per_device(): call(functools.partial(prepare_kernel, head_dim), 'prepare', (jax.ShapeDt...  1.78 us
  transfers between devices with their start and end apart: 3, of which 3 were waited for; matrix products, arithmetic and copies ran while one was open for 0% of the time, Pallas kernels for 10%

profile of v2, /device:TPU:1, one launch (start us, length us, event | category | flops | bytes accessed | tf_op | source)
XLA Modules:
  0.0 71.9 jit_solution(16954120432650955447)
XLA Ops:
  0.6 1.3 %broadcast_in_dim.9 = f32[8,2,128]{2,1,0:T(2,128)} broadcast(f32[2,128]{1,0:T(2,128)} %bitcast.18), dimensions={1,2} | broadcast | bytes 9216 | tf_op jit(solution)/shard_map/broadcast_in_dim | solution.py:312
  1.9 10.1 %all-to-all-start = ((f32[8,2,128]{2,1,0:T(2,128)}), f32[8,2,128]{2,1,0:T(2,128)S(1)}, u32[]{:S(2)}, u32[]{:S(2)}) async-start(f32[8,2,128]{2,1,0:T(2,128)} %broadcast_in_dim.9), calls=%async_computation | async-start | bytes 16384 | tf_op jit(solution)/shard_map/all_to_all | solution.py:299
  12.0 0.0 copy-start.1
  12.0 0.7 copy-done.1
  12.7 1.8 %prepare.1 = (bf16[2048,256]{1,0:T(8,128)(2,1)S(1)}, f32[16,128]{1,0:T(8,128)S(1)}, f32[8,128]{1,0:T(8,128)S(1)}, f32[8,128]{1,0:T(8,128)S(1)}) custom-call(s32[1]{0:T(128)} %bitcast.place_ref, s32[64]{0:T(128)S(1)} %copy-done.1, bf16[2048,256]{1,0:T(8,128)(2,1)} %w_ref.2, f32[16,128]{1,0:T(8,128)} %bitcast.17), custom_call_target="tpu_custom_call" | custom-call | tf_op jit(solution)/shard_map/prepare/pallas_call | solution.py:320
  14.4 2.2 %all-to-all-done = f32[8,2,128]{2,1,0:T(2,128)S(1)} async-done(((f32[8,2,128]{2,1,0:T(2,128)}), f32[8,2,128]{2,1,0:T(2,128)S(1)}, u32[]{:S(2)}, u32[]{:S(2)}) %all-to-all-start) | async-done | bytes 8224 | tf_op jit(solution)/shard_map/all_to_all | solution.py:299
  16.6 1.1 %query.1.query_ref = f32[256,128]{1,0:T(8,128)} custom-call(f32[16,128]{1,0:T(8,128)S(1)} %bitcast.13, f32[16,128]{1,0:T(8,128)S(1)} %get-tuple-element.12.gain_ref, bf16[2048,256]{1,0:T(8,128)(2,1)S(1)} %get-tuple-element.13.w_ref, f32[8,128]{1,0:T(8,128)S(1)} %get-tuple-element.14.cos_ref, f32[8,128]{1,0:T(8,128)S(1)} %get-tuple-element.15.sin_ref), custom_call_target="tpu_custom_call" | custom-call | tf_op jit(solution)/shard_map/query/pallas_call | solution.py:333
  17.8 12.0 %all-to-all-start.1 = ((f32[64,4,128]{2,1,0:T(4,128)}), f32[64,4,128]{2,1,0:T(4,128)S(1)}, u32[]{:S(2)}, u32[]{:S(2)}) async-start(f32[64,4,128]{2,1,0:T(4,128)} %bitcast.5), calls=%async_computation.1 | async-start | bytes 262144 | tf_op jit(solution)/shard_map/all_to_all | solution.py:299
  29.8 0.0 copy-start
  29.8 0.7 %copy-done = s32[64,128]{1,0:T(8,128)S(1)} copy-done((s32[64,128]{1,0:T(8,128)S(1)}, s32[64,128]{1,0:T(8,128)}, u32[]{:S(2)}) %copy-start) | copy-done | bytes 32792
  30.5 0.0 copy-start.2
  30.5 0.7 copy-done.2
  31.2 2.5 %slot_table.1 = (s32[96,128]{1,0:T(8,128)S(1)}, bf16[96,128,128]{2,1,0:T(8,128)(2,1)S(1)}) custom-call(s32[1]{0:T(128)} %bitcast.place_ref, s32[64]{0:T(128)S(1)} %copy-done.2, s32[64,128]{1,0:T(8,128)S(1)} %copy-done, bf16[96,128,128]{2,1,0:T(8,128)(2,1)} %bitcast.16), custom_call_target="tpu_custom_call" | custom-call | tf_op jit(solution)/shard_map/slot_table/pallas_call | solution.py:343
  33.6 0.1 slice_reduce_fusion.tab_ref
  33.8 7.6 %all-to-all-done.1 = f32[64,4,128]{2,1,0:T(4,128)S(1)} async-done(((f32[64,4,128]{2,1,0:T(4,128)}), f32[64,4,128]{2,1,0:T(4,128)S(1)}, u32[]{:S(2)}, u32[]{:S(2)}) %all-to-all-start.1) | async-done | bytes 131104 | tf_op jit(solution)/shard_map/all_to_all | solution.py:299
  41.3 0.0 copy-start.3
  41.3 3.0 %attend.1 = f32[256,128]{1,0:T(8,128)} custom-call(s32[96]{0:T(128)S(1)} %slice_reduce_fusion.tab_ref, f32[256,128]{1,0:T(8,128)S(1)} %bitcast.12, bf16[96,128,128]{2,1,0:T(8,128)(2,1)S(1)} %get-tuple-element.16.kv_ref), custom_call_target="tpu_custom_call" | custom-call | tf_op jit(solution)/shard_map/attend/pallas_call | solution.py:369
  44.3 4.6 %all-to-all-start.2 = ((f32[64,4,128]{2,1,0:T(4,128)}), f32[64,4,128]{2,1,0:T(4,128)S(1)}, u32[]{:S(2)}, u32[]{:S(2)}) async-start(f32[64,4,128]{2,1,0:T(4,128)} %bitcast.7), calls=%async_computation.2 | async-start | bytes 262144 | tf_op jit(solution)/shard_map/all_to_all | solution.py:299
  48.9 2.8 %keyval.1 = (bf16[1,128]{1,0:T(2,128)(2,1)}, f32[8,128]{1,0:T(8,128)S(1)}, bf16[256,2048]{1,0:T(8,128)(2,1)S(1)}) custom-call(f32[16,128]{1,0:T(8,128)S(1)} %bitcast.14, f32[16,128]{1,0:T(8,128)S(1)} %get-tuple-element.12.gain_ref, f32[8,128]{1,0:T(8,128)S(1)} %get-tuple-element.14.cos_ref, f32[8,128]{1,0:T(8,128)S(1)} %get-tuple-element.15.sin_ref, ...), custom_call_target="tpu_custom_call" | custom-call | tf_op jit(solution)/shard_map/keyval/pallas_call | solution.py:356
  51.8 8.7 %all-to-all-done.2 = f32[64,4,128]{2,1,0:T(4,128)S(1)} async-done(((f32[64,4,128]{2,1,0:T(4,128)}), f32[64,4,128]{2,1,0:T(4,128)S(1)}, u32[]{:S(2)}, u32[]{:S(2)}) %all-to-all-start.2) | async-done | bytes 131104 | tf_op jit(solution)/shard_map/all_to_all | solution.py:299
  60.5 0.5 combine.1
  61.0 10.3 %all_to_all.20 = f32[8,2,128]{2,1,0:T(2,128)S(1)} all-to-all(f32[8,2,128]{2,1,0:T(2,128)S(1)} %bitcast.15), channel_id=1, replica_groups=mesh['pool'=64,'mp'=8] {'mp'}, dimensions={0} | all-to-all | bytes 16384 | tf_op jit(solution)/shard_map/all_to_all | solution.py:299
  71.3 0.0 copy-done.3
  71.3 0.6 add.3
  (2 shorter events, 0.0 us)
Async XLA Ops:
  1.9 14.7 %all-to-all-start = ((f32[8,2,128]{2,1,0:T(2,128)}), f32[8,2,128]{2,1,0:T(2,128)S(1)}, u32[]{:S(2)}, u32[]{:S(2)}) async-start(f32[8,2,128]{2,1,0:T(2,128)} %broadcast_in_dim.9), calls=%async_computation | async-start | bytes 16384 | tf_op jit(solution)/shard_map/all_to_all | solution.py:299
  12.0 0.7 copy-start.1
  17.8 23.6 %all-to-all-start.1 = ((f32[64,4,128]{2,1,0:T(4,128)}), f32[64,4,128]{2,1,0:T(4,128)S(1)}, u32[]{:S(2)}, u32[]{:S(2)}) async-start(f32[64,4,128]{2,1,0:T(4,128)} %bitcast.5), calls=%async_computation.1 | async-start | bytes 262144 | tf_op jit(solution)/shard_map/all_to_all | solution.py:299
  29.8 0.8 %copy-start = (s32[64,128]{1,0:T(8,128)S(1)}, s32[64,128]{1,0:T(8,128)}, u32[]{:S(2)}) copy-start(s32[64,128]{1,0:T(8,128)} %slot_ref.1) | copy-start | bytes 98308
  30.5 0.7 copy-start.2
  41.3 30.0 %copy-start.3 = (f32[1,256]{1,0:T(1,128)S(1)}, f32[1,256]{1,0:T(1,128)}, u32[]{:S(2)}) copy-start(f32[1,256]{1,0:T(1,128)} %param.8) | copy-start | bytes 3076
  44.3 16.2 %all-to-all-start.2 = ((f32[64,4,128]{2,1,0:T(4,128)}), f32[64,4,128]{2,1,0:T(4,128)S(1)}, u32[]{:S(2)}, u32[]{:S(2)}) async-start(f32[64,4,128]{2,1,0:T(4,128)} %bitcast.7), calls=%async_computation.2 | async-start | bytes 262144 | tf_op jit(solution)/shard_map/all_to_all | solution.py:299

commit v3 on v2

--- a/solution.py
+++ b/solution.py
@@ -117,9 +117,11 @@
 
 
 def prepare_kernel(
-    head_dim, place_ref, lengths_ref, w_ref, gain_ref, held_w_ref, held_gain_ref, cos_ref, sin_ref, sems
+    head_dim, place_ref, lengths_ref, w_ref, gain_ref, cache_ref, *rest
 ):
-    copies = fetch((w_ref, gain_ref), (held_w_ref, held_gain_ref), sems)
+    held_w_ref, held_gain_ref, held_cache_ref, cos_ref, sin_ref, sems = rest
+    first = cache_ref.at[pl.ds(0, held_cache_ref.shape[0])]
+    copies = fetch((w_ref, gain_ref, first), (held_w_ref, held_gain_ref, held_cache_ref), sems)
     cos_ref[...], sin_ref[...] = rotation(lengths_ref[place_ref[0]], head_dim, 2 * head_dim)
     for copy in copies:
         copy.wait()
@@ -136,32 +138,29 @@
         tile = jnp.where(row == 2 * c, part, tile)
         tile = jnp.where(row == 2 * c + 1, pltpu.roll(part, head_dim, 1), tile)
     tile = tile.astype(BF16).astype(F32) * SCORE_SCALE
-    tile = jnp.where(lanes(tile.shape) < head_dim, tile, 0.0)
+    tile = jnp.where(lanes(tile.shape) < head_dim, tile, 0.0).astype(BF16)
     for v in range(out_ref.shape[0] // 8):
         out_ref[pl.ds(8 * v, 8), :] = tile
 
 
-def keyval_kernel(head_dim, rows_ref, gain_ref, cos_ref, sin_ref, query_ref, w_ref, w_out_ref, *rest):
-    kv_ref, own_ref, held_ref, near_ref, sems = rest
-    copies = fetch((w_ref, w_out_ref), (near_ref, held_ref), sems)
-    normed = normalise(rows_ref, gain_ref)
-    copies[0].wait()
-    keyval = project(normed, near_ref)
+def keyval_kernel(
+    head_dim, rows_ref, gain_ref, cos_ref, sin_ref, query_ref, w_ref, kv_ref, own_ref
+):
+    keyval = project(normalise(rows_ref, gain_ref), w_ref)
     is_key = lanes(keyval.shape) < head_dim
     turned = rope(keyval, cos_ref[...], sin_ref[...], head_dim // 2)
     both = jnp.where(is_key, turned, keyval).astype(BF16)
     kv_ref[...] = both[:1]
     both = both.astype(F32)
-    score = jnp.sum(query_ref[:8, :] * both, axis=1, keepdims=True)
+    score = jnp.sum(query_ref[:8, :].astype(F32) * both, axis=1, keepdims=True)
     own_ref[...] = jnp.where(is_key, score, both)
-    copies[1].wait()
 
 
 def table_kernel(
-    slots_here, block_len, place_ref, lengths_ref, slot_ref, *rest
+    slots_here, block_len, place_ref, lengths_ref, slot_ref, cache_ref, out_ref, held_ref, sems
 ):
-    kv_ref, out_ref, held_ref, sems = rest
-    copies = fetch((kv_ref,), (held_ref,), sems)
+    count = held_ref.shape[0]
+    copies = fetch((cache_ref.at[pl.ds(slots_here - count, count)],), (held_ref,), sems)
     requests, blocks = slot_ref.shape
     base = place_ref[0] * slots_here
     sub = subs((8, blocks))
@@ -185,18 +184,21 @@
         out_ref[pl.ds(8 * tile, 8), :] = jnp.broadcast_to(
             jnp.max(picked.astype(F32), axis=1, keepdims=True), (8, blocks)
         ).astype(jnp.int32)
-    for copy in copies:
-        copy.wait()
-
-
-def attend_kernel(tab_ref, query_ref, kv_ref, out_ref, q_s, score_s, max_s, sum_s, acc_s):
-    slots_here, block_len, wide = kv_ref.shape
+    copies[0].wait()
+
+
+def attend_kernel(
+    tab_ref, query_ref, first_ref, second_ref, w_ref, out_ref, held_ref, q_s, score_s, max_s, sum_s, acc_s, sems
+):
+    copies = fetch((w_ref,), (held_ref,), sems)
+    half, block_len, wide = first_ref.shape
+    slots_here = 2 * half
     requests = query_ref.shape[0] // GROUP
     low = subs((8, wide)) < GROUP
     token = lanes((8, block_len))
     lane = lanes((8, wide))
     for v in range(requests // 2):
-        tile = query_ref[pl.ds(8 * v, 8), :]
+        tile = query_ref[pl.ds(8 * v, 8), :].astype(F32)
         other = pltpu.roll(tile, GROUP, 0)
         q_s[2 * v] = jnp.where(low, tile, other)
         q_s[2 * v + 1] = jnp.where(low, other, tile)
@@ -207,7 +209,8 @@
     def pair(p):
         a, b = tab_ref[2 * p], tab_ref[2 * p + 1]
         live = token < jnp.where(low, a & 255, b & 255)
-        keys = kv_ref[pl.ds(2 * p, 2)].reshape(2 * block_len, wide)
+        held, at = (first_ref, 2 * p) if 2 * p < half else (second_ref, 2 * p - half)
+        keys = held[pl.ds(at, 2)].reshape(2 * block_len, wide)
         return lax.shift_right_logical(a, 8), lax.shift_right_logical(b, 8), live, keys
 
     for p in range(slots_here // 2):
@@ -250,6 +253,7 @@
                 jnp.where(lane < wide // 4, max_s[r], jnp.where(lane < wide // 2, total, out))
             )
         out_ref[pl.ds(8 * v, 8), :] = jnp.where(low, tiles[0], tiles[1])
+    copies[0].wait()
 
 
 def combine_kernel(got_ref, own_ref, w_ref, out_ref):
@@ -317,69 +321,69 @@
 
     turn = jax.ShapeDtypeStruct((8, wide), F32)
     w_query, w_keyval, w_out, gain = (far(x) for x in (w_query, w_keyval, w_out, gain))
-    held_query, held_gain, cosine, sine = call(
+    cache = far(kv_cache.reshape(slots_here, block_len, wide))
+    lengths, block_slot = far(lengths), far(block_slot)
+    half_cache = jax.ShapeDtypeStruct((slots_here // 2, block_len, wide), BF16)
+    held_query, held_gain, first_cache, cosine, sine = call(
         functools.partial(prepare_kernel, head_dim),
         "prepare",
         (
             jax.ShapeDtypeStruct(w_query.shape, BF16),
             jax.ShapeDtypeStruct(gain.shape, F32),
+            half_cache,
             turn,
             turn,
         ),
-        [SMEM, SMEM, HBM, HBM],
-        [pltpu.SemaphoreType.DMA((2,))],
-    )(place, lengths, w_query, gain)
+        [SMEM, SMEM, HBM, HBM, HBM],
+        [pltpu.SemaphoreType.DMA((3,))],
+        limit=8 << 20,
+    )(place, lengths, w_query, gain, cache)
 
     query = call(
         functools.partial(query_kernel, head_dim),
         "query",
-        jax.ShapeDtypeStruct((requests * GROUP, wide), F32),
+        jax.ShapeDtypeStruct((requests * GROUP, wide), BF16),
         [VMEM] * 5,
     )(rows, held_gain, held_query, cosine, sine)
 
     queries = exchange(query, "pool", pools)
 
-    cache = far(kv_cache.reshape(slots_here, block_len, wide))
-    table, held_cache = call(
+    table, second_cache = call(
         functools.partial(table_kernel, slots_here, block_len),
         "slot_table",
-        (
-            jax.ShapeDtypeStruct((slots_here, block_slot.shape[1]), jnp.int32),
-            jax.ShapeDtypeStruct(cache.shape, BF16),
-        ),
+        (jax.ShapeDtypeStruct((slots_here, block_slot.shape[1]), jnp.int32), half_cache),
         [SMEM, SMEM, VMEM, HBM],
         [pltpu.SemaphoreType.DMA((1,))],
-        limit=8 << 20,
     )(place, lengths, block_slot, cache)
     table = table[:, 0]
 
-    new_kv, own, held_out = call(
+    new_kv, own = call(
         functools.partial(keyval_kernel, head_dim),
         "keyval",
+        (jax.ShapeDtypeStruct((1, wide), BF16), turn),
+        [VMEM] * 6,
+    )(rows, held_gain, cosine, sine, query, w_keyval)
+    table, own = lax.optimization_barrier((table, own))
+
+    per_request = pltpu.VMEM((requests, 8, wide), F32)
+    partial, held_out = call(
+        attend_kernel,
+        "attend",
         (
-            jax.ShapeDtypeStruct((1, wide), BF16),
-            turn,
+            jax.ShapeDtypeStruct((requests * GROUP, wide), F32),
             jax.ShapeDtypeStruct(w_out.shape, BF16),
         ),
-        [VMEM] * 5 + [HBM] * 2,
-        [pltpu.VMEM(w_keyval.shape, BF16), pltpu.SemaphoreType.DMA((2,))],
-    )(rows, held_gain, cosine, sine, query, w_keyval, w_out)
-
-    per_request = pltpu.VMEM((requests, 8, wide), F32)
-    partial = call(
-        attend_kernel,
-        "attend",
-        jax.ShapeDtypeStruct((requests * GROUP, wide), F32),
-        [SMEM, VMEM, VMEM],
+        [SMEM, VMEM, VMEM, VMEM, HBM],
         [
             per_request,
             pltpu.VMEM((slots_here // 2, 8, block_len), F32),
             per_request,
             per_request,
             per_request,
+            pltpu.SemaphoreType.DMA((1,)),
         ],
         limit=12 << 20,
-    )(table, queries, held_cache)
+    )(table, queries, first_cache, second_cache, w_out)
 
     got = exchange(partial, "pool", pools)
 

time: 72.4 us -> 72.3 us (level)
  blocking collectives: 10.3 us -> 26.4 us
  waiting for transfers between devices: 18.5 us -> 9 us
  starting transfers between devices: 26.7 us -> 22.1 us
  local copies, waits for them, and re-layouts: 3.45 us -> 1.38 us
    all_to_all x1 -> x2, blocking collectives: 10.3 us -> 26.4 us  [exchange(): lax.all_to_all(x, axis, split_axis=0, concat_axis=0, tiled=True)]
    all_to_all x3 -> x2, waiting for transfers between devices: 18.5 us -> 9 us  [exchange(): lax.all_to_all(x, axis, split_axis=0, concat_axis=0, tiled=True)]
    all_to_all x3 -> x2, starting transfers between devices: 26.7 us -> 22.1 us  [exchange(): lax.all_to_all(x, axis, split_axis=0, concat_axis=0, tiled=True)]
    unnamed x8 -> x2, local copies, waits for them, and re-layouts: 2.07 us -> 0.01 us
    pallas_call x1, Pallas kernels: 2.82 us -> 1.94 us  [per_device(): call(functools.partial(keyval_kernel, head_dim), 'keyval', (jax.ShapeDtyp...]
  transfers between devices with their start and end apart: 3 -> 2, of which waited for: 3 -> 2; matrix products, arithmetic and copies ran while one was open for 0% -> 0% of each run, Pallas kernels for 10% -> 9%
where the time goes in v3:
time: 72.3 us; the launch traced here: 71.8 us
  blocking collectives  26.4 us (37%)
  starting transfers between devices  22.1 us (31%)
  Pallas kernels  11.7 us (16%)
  waiting for transfers between devices  9 us (12%)
  local copies, waits for them, and re-layouts  1.38 us (2%)
    all_to_all x2, blocking collectives, exchange(): lax.all_to_all(x, axis, split_axis=0, concat_axis=0, tiled=True)  26.4 us
    all_to_all x2, starting transfers between devices, exchange(): lax.all_to_all(x, axis, split_axis=0, concat_axis=0, tiled=True)  22.1 us
    all_to_all x2, waiting for transfers between devices, exchange(): lax.all_to_all(x, axis, split_axis=0, concat_axis=0, tiled=True)  9 us
    pallas_call x1, Pallas kernels, per_device(): call(attend_kernel, 'attend', (jax.ShapeDtypeStruct((requests * GROUP, wi...  3.48 us
    pallas_call x1, Pallas kernels, per_device(): call(functools.partial(prepare_kernel, head_dim), 'prepare', (jax.ShapeDt...  2.43 us
    pallas_call x1, Pallas kernels, per_device(): call(functools.partial(table_kernel, slots_here, block_len), 'slot_table'...  2.21 us
    pallas_call x1, Pallas kernels, per_device(): call(functools.partial(keyval_kernel, head_dim), 'keyval', (jax.ShapeDtyp...  1.94 us
  transfers between devices with their start and end apart: 2, of which 2 were waited for; matrix products, arithmetic and copies ran while one was open for 0% of the time, Pallas kernels for 9%

profile of v3, /device:TPU:1, one launch (start us, length us, event | category | flops | bytes accessed | tf_op | source)
XLA Modules:
  0.0 71.8 jit_solution(1692651368149941473)
XLA Ops:
  0.6 1.3 %broadcast_in_dim.9 = f32[8,2,128]{2,1,0:T(2,128)} broadcast(f32[2,128]{1,0:T(2,128)} %bitcast.20), dimensions={1,2} | broadcast | bytes 9216 | tf_op jit(solution)/shard_map/broadcast_in_dim | solution.py:316
  1.9 10.1 %all-to-all-start = ((f32[8,2,128]{2,1,0:T(2,128)}), f32[8,2,128]{2,1,0:T(2,128)S(1)}, u32[]{:S(2)}, u32[]{:S(2)}) async-start(f32[8,2,128]{2,1,0:T(2,128)} %broadcast_in_dim.9), calls=%async_computation | async-start | bytes 16384 | tf_op jit(solution)/shard_map/all_to_all | solution.py:303
  12.0 2.4 %prepare.1 = (bf16[2048,256]{1,0:T(8,128)(2,1)S(1)}, f32[16,128]{1,0:T(8,128)S(1)}, bf16[48,128,128]{2,1,0:T(8,128)(2,1)S(1)}, f32[8,128]{1,0:T(8,128)S(1)}, f32[8,128]{1,0:T(8,128)S(1)}) custom-call(s32[1]{0:T(128)} %bitcast.place_ref, s32[64]{0:T(128)} %lengths_ref.3, bf16[2048,256]{1,0:T(8,128)(2,1)} %w_ref.3, f32[16,128]{1,0:T(8,128)} %bitcast.19, ...), custom_call_target="tpu_custom_call" | custom-call | tf_op jit(solution)/shard_map/prepare/pallas_call | solution.py:327
  14.4 2.2 %all-to-all-done = f32[8,2,128]{2,1,0:T(2,128)S(1)} async-done(((f32[8,2,128]{2,1,0:T(2,128)}), f32[8,2,128]{2,1,0:T(2,128)S(1)}, u32[]{:S(2)}, u32[]{:S(2)}) %all-to-all-start) | async-done | bytes 8224 | tf_op jit(solution)/shard_map/all_to_all | solution.py:303
  16.6 1.1 %query.1.query_ref = bf16[256,128]{1,0:T(8,128)(2,1)} custom-call(f32[16,128]{1,0:T(8,128)S(1)} %bitcast.14, f32[16,128]{1,0:T(8,128)S(1)} %get-tuple-element.16.gain_ref, bf16[2048,256]{1,0:T(8,128)(2,1)S(1)} %get-tuple-element.19.w_ref, f32[8,128]{1,0:T(8,128)S(1)} %get-tuple-element.17.cos_ref, f32[8,128]{1,0:T(8,128)S(1)} %get-tuple-element.18.sin_ref), custom_call_target="tpu_custom_call" | custom-call | tf_op jit(solution)/shard_map/query/pallas_call | solution.py:342
  17.7 12.0 %all-to-all-start.1 = ((bf16[64,4,128]{2,1,0:T(4,128)(2,1)}), bf16[64,4,128]{2,1,0:T(4,128)(2,1)S(1)}, u32[]{:S(2)}, u32[]{:S(2)}) async-start(bf16[64,4,128]{2,1,0:T(4,128)(2,1)} %bitcast.5), calls=%async_computation.1 | async-start | bytes 131072 | tf_op jit(solution)/shard_map/all_to_all | solution.py:303
  29.7 2.2 %slot_table.1 = (s32[96,128]{1,0:T(8,128)S(1)}, bf16[48,128,128]{2,1,0:T(8,128)(2,1)S(1)}) custom-call(s32[1]{0:T(128)} %bitcast.place_ref, s32[64]{0:T(128)} %lengths_ref.3, s32[64,128]{1,0:T(8,128)} %slot_ref.1, bf16[96,128,128]{2,1,0:T(8,128)(2,1)} %bitcast.18), custom_call_target="tpu_custom_call" | custom-call | tf_op jit(solution)/shard_map/slot_table/pallas_call | solution.py:351
  31.9 0.1 slice_reduce_fusion.tab_ref
  32.0 1.9 %keyval.1 = (bf16[1,128]{1,0:T(2,128)(2,1)}, f32[8,128]{1,0:T(8,128)S(1)}) custom-call(f32[16,128]{1,0:T(8,128)S(1)} %bitcast.15, f32[16,128]{1,0:T(8,128)S(1)} %get-tuple-element.16.gain_ref, f32[8,128]{1,0:T(8,128)S(1)} %get-tuple-element.17.cos_ref, f32[8,128]{1,0:T(8,128)S(1)} %get-tuple-element.18.sin_ref, bf16[256,128]{1,0:T(8,128)(2,1)} %query.1.query_ref, ...), custom_call_target="tpu_custom_call" | custom-call | tf_op jit(solution)/shard_map/keyval/pallas_call | solution.py:360
  34.0 6.8 %all-to-all-done.1 = bf16[64,4,128]{2,1,0:T(4,128)(2,1)S(1)} async-done(((bf16[64,4,128]{2,1,0:T(4,128)(2,1)}), bf16[64,4,128]{2,1,0:T(4,128)(2,1)S(1)}, u32[]{:S(2)}, u32[]{:S(2)}) %all-to-all-start.1) | async-done | bytes 65568 | tf_op jit(solution)/shard_map/all_to_all | solution.py:303
  40.8 0.0 copy-start
  40.8 3.5 %attend.1 = (f32[256,128]{1,0:T(8,128)S(1)}, bf16[256,2048]{1,0:T(8,128)(2,1)S(1)}) custom-call(s32[96]{0:T(128)S(1)} %slice_reduce_fusion.tab_ref, bf16[256,128]{1,0:T(8,128)(2,1)S(1)} %bitcast.12, bf16[48,128,128]{2,1,0:T(8,128)(2,1)S(1)} %get-tuple-element.22.first_ref, bf16[48,128,128]{2,1,0:T(8,128)(2,1)S(1)} %get-tuple-element.23.second_ref, ...), custom_call_target="tpu_custom_call" | custom-call | tf_op jit(solution)/shard_map/attend/pallas_call | solution.py:369
  44.3 16.7 %all_to_all.20 = f32[64,4,128]{2,1,0:T(4,128)S(1)} all-to-all(f32[64,4,128]{2,1,0:T(4,128)S(1)} %bitcast.13), channel_id=1, replica_groups=mesh['pool'=64,'mp'=8] {'pool'}, dimensions={0} | all-to-all | bytes 262144 | tf_op jit(solution)/shard_map/all_to_all | solution.py:303
  61.0 0.5 combine.1
  61.5 9.7 %all_to_all.21 = f32[8,2,128]{2,1,0:T(2,128)S(1)} all-to-all(f32[8,2,128]{2,1,0:T(2,128)S(1)} %bitcast.16), channel_id=1, replica_groups=mesh['pool'=64,'mp'=8] {'mp'}, dimensions={0} | all-to-all | bytes 16384 | tf_op jit(solution)/shard_map/all_to_all | solution.py:303
  71.2 0.0 copy-done
  71.2 0.6 add.3
  (2 shorter events, 0.0 us)
Async XLA Ops:
  1.9 14.7 %all-to-all-start = ((f32[8,2,128]{2,1,0:T(2,128)}), f32[8,2,128]{2,1,0:T(2,128)S(1)}, u32[]{:S(2)}, u32[]{:S(2)}) async-start(f32[8,2,128]{2,1,0:T(2,128)} %broadcast_in_dim.9), calls=%async_computation | async-start | bytes 16384 | tf_op jit(solution)/shard_map/all_to_all | solution.py:303
  17.7 23.1 %all-to-all-start.1 = ((bf16[64,4,128]{2,1,0:T(4,128)(2,1)}), bf16[64,4,128]{2,1,0:T(4,128)(2,1)S(1)}, u32[]{:S(2)}, u32[]{:S(2)}) async-start(bf16[64,4,128]{2,1,0:T(4,128)(2,1)} %bitcast.5), calls=%async_computation.1 | async-start | bytes 131072 | tf_op jit(solution)/shard_map/all_to_all | solution.py:303
  40.8 30.4 %copy-start = (f32[1,256]{1,0:T(1,128)S(1)}, f32[1,256]{1,0:T(1,128)}, u32[]{:S(2)}) copy-start(f32[1,256]{1,0:T(1,128)} %param.8) | copy-start | bytes 3076

commit v4 on v3

--- a/solution.py
+++ b/solution.py
@@ -21,6 +21,8 @@
 HBM = pl.BlockSpec(memory_space=pltpu.HBM)
 
 GROUP = 4
+
+FIRST = 44
 
 
 def far(x):
@@ -173,7 +175,9 @@
         limit = length - lane * block_len
         here = slot_ref[pl.ds(8 * v, 8), :] - base
         wanted.append(jnp.where(limit > 0, here, -1))
-        payload.append((sub + 8 * v) * 256 + jnp.minimum(limit, block_len))
+        payload.append(
+            ((sub + 8 * v + requests - FIRST) % requests) * 256 + jnp.minimum(limit, block_len)
+        )
     for tile in range(slots_here // 8):
         picked = jnp.zeros((8, blocks), jnp.int32)
         for i in range(8):
@@ -297,10 +301,13 @@
         out_ref[pl.ds(8 * v, 8), :] = tile
 
 
-def exchange(x, axis, parts):
+def exchange(x, axis, parts, first=0):
     shape = x.shape
     x = x.reshape(parts, shape[0] // parts, shape[1])
-    return lax.all_to_all(x, axis, split_axis=0, concat_axis=0, tiled=True).reshape(shape)
+    groups = [[(i + first) % parts for i in range(parts)]] if first else None
+    return lax.all_to_all(
+        x, axis, split_axis=0, concat_axis=0, tiled=True, axis_index_groups=groups
+    ).reshape(shape)
 
 
 def per_device(hidden, norm_gain, w_query, w_keyval, w_out, kv_cache, block_slot, lengths):
@@ -346,7 +353,7 @@
         [VMEM] * 5,
     )(rows, held_gain, held_query, cosine, sine)
 
-    queries = exchange(query, "pool", pools)
+    queries = exchange(query, "pool", pools, FIRST)
 
     table, second_cache = call(
         functools.partial(table_kernel, slots_here, block_len),
@@ -385,7 +392,7 @@
         limit=12 << 20,
     )(table, queries, first_cache, second_cache, w_out)
 
-    got = exchange(partial, "pool", pools)
+    got = exchange(partial, "pool", pools, FIRST)
 
     mixed = call(
         combine_kernel,

time: 72.3 us -> 66.2 us (0.916)
  waiting for transfers between devices: 9 us -> 2.2 us
  starting transfers between devices: 22.1 us -> 24.1 us
  blocking collectives: 26.4 us -> 25.1 us
    all_to_all x2, waiting for transfers between devices: 9 us -> 2.2 us  [exchange(): lax.all_to_all(x, axis, split_axis=0, concat_axis=0, tiled=True, axis_ind...]
    all_to_all x2, starting transfers between devices: 22.1 us -> 24.1 us  [exchange(): lax.all_to_all(x, axis, split_axis=0, concat_axis=0, tiled=True, axis_ind...]
    all_to_all x2, blocking collectives: 26.4 us -> 25.1 us  [exchange(): lax.all_to_all(x, axis, split_axis=0, concat_axis=0, tiled=True, axis_ind...]
  transfers between devices with their start and end apart: 2 -> 2, of which waited for: 2 -> 1; matrix products, arithmetic and copies ran while one was open for 0% -> 0% of each run, Pallas kernels for 9% -> 10%
where the time goes in v4:
time: 66.2 us; the launch traced here: 65.7 us
  blocking collectives  25.1 us (38%)
  starting transfers between devices  24.1 us (36%)
  Pallas kernels  11.7 us (18%)
  waiting for transfers between devices  2.2 us (3%)
  local copies, waits for them, and re-layouts  1.38 us (2%)
  between operations  0.68 us (1%)
    all_to_all x2, blocking collectives, exchange(): lax.all_to_all(x, axis, split_axis=0, concat_axis=0, tiled=True, axis_ind...  25.1 us
    all_to_all x2, starting transfers between devices, exchange(): lax.all_to_all(x, axis, split_axis=0, concat_axis=0, tiled=True, axis_ind...  24.1 us
    pallas_call x1, Pallas kernels, per_device(): call(attend_kernel, 'attend', (jax.ShapeDtypeStruct((requests * GROUP, wi...  3.48 us
    pallas_call x1, Pallas kernels, per_device(): call(functools.partial(prepare_kernel, head_dim), 'prepare', (jax.ShapeDt...  2.43 us
    pallas_call x1, Pallas kernels, per_device(): call(functools.partial(table_kernel, slots_here, block_len), 'slot_table'...  2.22 us
    all_to_all x2, waiting for transfers between devices, exchange(): lax.all_to_all(x, axis, split_axis=0, concat_axis=0, tiled=True, axis_ind...  2.2 us
    pallas_call x1, Pallas kernels, per_device(): call(functools.partial(keyval_kernel, head_dim), 'keyval', (jax.ShapeDtyp...  1.94 us
  transfers between devices with their start and end apart: 2, of which 1 were waited for; matrix products, arithmetic and copies ran while one was open for 0% of the time, Pallas kernels for 10%

profile of v4, /device:TPU:1, one launch (start us, length us, event | category | flops | bytes accessed | tf_op | source)
XLA Modules:
  0.0 65.7 jit_solution(12780997383995276012)
XLA Ops:
  0.6 1.3 %broadcast_in_dim.9 = f32[8,2,128]{2,1,0:T(2,128)} broadcast(f32[2,128]{1,0:T(2,128)} %bitcast.20), dimensions={1,2} | broadcast | bytes 9216 | tf_op jit(solution)/shard_map/broadcast_in_dim | solution.py:323
  1.9 10.1 %all-to-all-start = ((f32[8,2,128]{2,1,0:T(2,128)}), f32[8,2,128]{2,1,0:T(2,128)S(1)}, u32[]{:S(2)}, u32[]{:S(2)}) async-start(f32[8,2,128]{2,1,0:T(2,128)} %broadcast_in_dim.9), calls=%async_computation | async-start | bytes 16384 | tf_op jit(solution)/shard_map/all_to_all | solution.py:308
  12.0 2.4 %prepare.1 = (bf16[2048,256]{1,0:T(8,128)(2,1)S(1)}, f32[16,128]{1,0:T(8,128)S(1)}, bf16[48,128,128]{2,1,0:T(8,128)(2,1)S(1)}, f32[8,128]{1,0:T(8,128)S(1)}, f32[8,128]{1,0:T(8,128)S(1)}) custom-call(s32[1]{0:T(128)} %bitcast.place_ref, s32[64]{0:T(128)} %lengths_ref.3, bf16[2048,256]{1,0:T(8,128)(2,1)} %w_ref.3, f32[16,128]{1,0:T(8,128)} %bitcast.19, ...), custom_call_target="tpu_custom_call" | custom-call | tf_op jit(solution)/shard_map/prepare/pallas_call | solution.py:334
  14.4 2.2 %all-to-all-done = f32[8,2,128]{2,1,0:T(2,128)S(1)} async-done(((f32[8,2,128]{2,1,0:T(2,128)}), f32[8,2,128]{2,1,0:T(2,128)S(1)}, u32[]{:S(2)}, u32[]{:S(2)}) %all-to-all-start) | async-done | bytes 8224 | tf_op jit(solution)/shard_map/all_to_all | solution.py:308
  16.6 1.1 %query.1.query_ref = bf16[256,128]{1,0:T(8,128)(2,1)} custom-call(f32[16,128]{1,0:T(8,128)S(1)} %bitcast.14, f32[16,128]{1,0:T(8,128)S(1)} %get-tuple-element.16.gain_ref, bf16[2048,256]{1,0:T(8,128)(2,1)S(1)} %get-tuple-element.19.w_ref, f32[8,128]{1,0:T(8,128)S(1)} %get-tuple-element.17.cos_ref, f32[8,128]{1,0:T(8,128)S(1)} %get-tuple-element.18.sin_ref), custom_call_target="tpu_custom_call" | custom-call | tf_op jit(solution)/shard_map/query/pallas_call | solution.py:349
  17.7 14.0 %all-to-all-start.1 = ((bf16[64,4,128]{2,1,0:T(4,128)(2,1)}), bf16[64,4,128]{2,1,0:T(4,128)(2,1)S(1)}, u32[]{:S(2)}, u32[]{:S(2)}) async-start(bf16[64,4,128]{2,1,0:T(4,128)(2,1)} %bitcast.5), calls=%async_computation.1 | async-start | bytes 131072 | tf_op jit(solution)/shard_map/all_to_all | solution.py:308
  31.7 2.2 %slot_table.1 = (s32[96,128]{1,0:T(8,128)S(1)}, bf16[48,128,128]{2,1,0:T(8,128)(2,1)S(1)}) custom-call(s32[1]{0:T(128)} %bitcast.place_ref, s32[64]{0:T(128)} %lengths_ref.3, s32[64,128]{1,0:T(8,128)} %slot_ref.1, bf16[96,128,128]{2,1,0:T(8,128)(2,1)} %bitcast.18), custom_call_target="tpu_custom_call" | custom-call | tf_op jit(solution)/shard_map/slot_table/pallas_call | solution.py:358
  33.9 0.1 slice_reduce_fusion.tab_ref
  34.0 1.9 %keyval.1 = (bf16[1,128]{1,0:T(2,128)(2,1)}, f32[8,128]{1,0:T(8,128)S(1)}) custom-call(f32[16,128]{1,0:T(8,128)S(1)} %bitcast.15, f32[16,128]{1,0:T(8,128)S(1)} %get-tuple-element.16.gain_ref, f32[8,128]{1,0:T(8,128)S(1)} %get-tuple-element.17.cos_ref, f32[8,128]{1,0:T(8,128)S(1)} %get-tuple-element.18.sin_ref, bf16[256,128]{1,0:T(8,128)(2,1)} %query.1.query_ref, ...), custom_call_target="tpu_custom_call" | custom-call | tf_op jit(solution)/shard_map/keyval/pallas_call | solution.py:367
  36.0 0.0 all-to-all-done.1
  36.0 0.0 copy-start
  36.0 3.5 %attend.1 = (f32[256,128]{1,0:T(8,128)S(1)}, bf16[256,2048]{1,0:T(8,128)(2,1)S(1)}) custom-call(s32[96]{0:T(128)S(1)} %slice_reduce_fusion.tab_ref, bf16[256,128]{1,0:T(8,128)(2,1)S(1)} %bitcast.12, bf16[48,128,128]{2,1,0:T(8,128)(2,1)S(1)} %get-tuple-element.22.first_ref, bf16[48,128,128]{2,1,0:T(8,128)(2,1)S(1)} %get-tuple-element.23.second_ref, ...), custom_call_target="tpu_custom_call" | custom-call | tf_op jit(solution)/shard_map/attend/pallas_call | solution.py:376
  39.5 15.8 %all_to_all.20 = f32[64,4,128]{2,1,0:T(4,128)S(1)} all-to-all(f32[64,4,128]{2,1,0:T(4,128)S(1)} %bitcast.13), channel_id=1, replica_groups={{352,360,368,376,384,392,400,408,416,424,432,440,448,456,464,472,480,48..., dimensions={0} | all-to-all | bytes 262144 | tf_op jit(solution)/shard_map/all_to_all | solution.py:308
  55.2 0.5 combine.1
  55.7 9.4 %all_to_all.21 = f32[8,2,128]{2,1,0:T(2,128)S(1)} all-to-all(f32[8,2,128]{2,1,0:T(2,128)S(1)} %bitcast.16), channel_id=1, replica_groups=mesh['pool'=64,'mp'=8] {'mp'}, dimensions={0} | all-to-all | bytes 16384 | tf_op jit(solution)/shard_map/all_to_all | solution.py:308
  65.1 0.0 copy-done
  65.2 0.6 add.3
  (2 shorter events, 0.0 us)
Async XLA Ops:
  1.9 14.7 %all-to-all-start = ((f32[8,2,128]{2,1,0:T(2,128)}), f32[8,2,128]{2,1,0:T(2,128)S(1)}, u32[]{:S(2)}, u32[]{:S(2)}) async-start(f32[8,2,128]{2,1,0:T(2,128)} %broadcast_in_dim.9), calls=%async_computation | async-start | bytes 16384 | tf_op jit(solution)/shard_map/all_to_all | solution.py:308
  17.7 18.3 %all-to-all-start.1 = ((bf16[64,4,128]{2,1,0:T(4,128)(2,1)}), bf16[64,4,128]{2,1,0:T(4,128)(2,1)S(1)}, u32[]{:S(2)}, u32[]{:S(2)}) async-start(bf16[64,4,128]{2,1,0:T(4,128)(2,1)} %bitcast.5), calls=%async_computation.1 | async-start | bytes 131072 | tf_op jit(solution)/shard_map/all_to_all | solution.py:308
  36.0 29.2 %copy-start = (f32[1,256]{1,0:T(1,128)S(1)}, f32[1,256]{1,0:T(1,128)}, u32[]{:S(2)}) copy-start(f32[1,256]{1,0:T(1,128)} %param.8) | copy-start | bytes 3076

commit v5 on v4

--- a/solution.py
+++ b/solution.py
@@ -23,6 +23,7 @@
 GROUP = 4
 
 FIRST = 44
+FIRST_SHARD = 4
 
 
 def far(x):
@@ -92,8 +93,8 @@
     half = count // 2
     even = pl.ds(0, half, stride=2)
     odd = pl.ds(1, half, stride=2)
-    left = rows_ref[even, :] * scale * gain_ref[even, :]
-    right = rows_ref[odd, :] * scale * gain_ref[odd, :]
+    left = pltpu.roll(rows_ref[even, :], FIRST_SHARD, 0) * scale * gain_ref[even, :]
+    right = pltpu.roll(rows_ref[odd, :], FIRST_SHARD, 0) * scale * gain_ref[odd, :]
     return jnp.concatenate([left, right], axis=1)
 
 
@@ -146,8 +147,10 @@
 
 
 def keyval_kernel(
-    head_dim, rows_ref, gain_ref, cos_ref, sin_ref, query_ref, w_ref, kv_ref, own_ref
+    head_dim, rows_ref, gain_ref, cos_ref, sin_ref, query_ref, w_ref, w_out_ref, *rest
 ):
+    kv_ref, own_ref, held_ref, sems = rest
+    copies = fetch((w_out_ref,), (held_ref,), sems)
     keyval = project(normalise(rows_ref, gain_ref), w_ref)
     is_key = lanes(keyval.shape) < head_dim
     turned = rope(keyval, cos_ref[...], sin_ref[...], head_dim // 2)
@@ -156,6 +159,7 @@
     both = both.astype(F32)
     score = jnp.sum(query_ref[:8, :].astype(F32) * both, axis=1, keepdims=True)
     own_ref[...] = jnp.where(is_key, score, both)
+    copies[0].wait()
 
 
 def table_kernel(
@@ -192,9 +196,8 @@
 
 
 def attend_kernel(
-    tab_ref, query_ref, first_ref, second_ref, w_ref, out_ref, held_ref, q_s, score_s, max_s, sum_s, acc_s, sems
+    tab_ref, query_ref, first_ref, second_ref, out_ref, q_s, score_s, max_s, sum_s, acc_s
 ):
-    copies = fetch((w_ref,), (held_ref,), sems)
     half, block_len, wide = first_ref.shape
     slots_here = 2 * half
     requests = query_ref.shape[0] // GROUP
@@ -257,7 +260,6 @@
                 jnp.where(lane < wide // 4, max_s[r], jnp.where(lane < wide // 2, total, out))
             )
         out_ref[pl.ds(8 * v, 8), :] = jnp.where(low, tiles[0], tiles[1])
-    copies[0].wait()
 
 
 def combine_kernel(got_ref, own_ref, w_ref, out_ref):
@@ -291,10 +293,10 @@
         for c in range(GROUP // 2)
     ]
     line = jnp.broadcast_to(jnp.concatenate(chunks, axis=1), (8, GROUP // 2 * wide)).astype(BF16)
-    for v in range(out_ref.shape[0] // 8):
-        part = jnp.dot(
-            line, w_ref[:, pl.ds(8 * v * wide, 8 * wide)], preferred_element_type=F32
-        )
+    lines = out_ref.shape[0]
+    for v in range(lines // 8):
+        at = (8 * v + FIRST_SHARD * GROUP // 2) % lines * wide
+        part = jnp.dot(line, w_ref[:, pl.ds(at, 8 * wide)], preferred_element_type=F32)
         tile = jnp.zeros((8, wide), F32)
         for k in range(8):
             tile = jnp.where(row == k, part[:, k * wide : (k + 1) * wide], tile)
@@ -323,6 +325,7 @@
         jnp.broadcast_to(hidden.reshape(1, lines, wide), (shards, lines, wide)).reshape(-1, wide),
         "mp",
         shards,
+        FIRST_SHARD,
     )
     gain = norm_gain.reshape(shards * lines, wide)
 
@@ -364,33 +367,34 @@
     )(place, lengths, block_slot, cache)
     table = table[:, 0]
 
-    new_kv, own = call(
+    new_kv, own, held_out = call(
         functools.partial(keyval_kernel, head_dim),
         "keyval",
-        (jax.ShapeDtypeStruct((1, wide), BF16), turn),
-        [VMEM] * 6,
-    )(rows, held_gain, cosine, sine, query, w_keyval)
+        (
+            jax.ShapeDtypeStruct((1, wide), BF16),
+            turn,
+            jax.ShapeDtypeStruct(w_out.shape, BF16),
+        ),
+        [VMEM] * 6 + [HBM],
+        [pltpu.SemaphoreType.DMA((1,))],
+    )(rows, held_gain, cosine, sine, query, w_keyval, w_out)
     table, own = lax.optimization_barrier((table, own))
 
     per_request = pltpu.VMEM((requests, 8, wide), F32)
-    partial, held_out = call(
+    partial = call(
         attend_kernel,
         "attend",
-        (
-            jax.ShapeDtypeStruct((requests * GROUP, wide), F32),
-            jax.ShapeDtypeStruct(w_out.shape, BF16),
-        ),
-        [SMEM, VMEM, VMEM, VMEM, HBM],
+        jax.ShapeDtypeStruct((requests * GROUP, wide), F32),
+        [SMEM, VMEM, VMEM, VMEM],
         [
             per_request,
             pltpu.VMEM((slots_here // 2, 8, block_len), F32),
             per_request,
             per_request,
             per_request,
-            pltpu.SemaphoreType.DMA((1,)),
         ],
         limit=12 << 20,
-    )(table, queries, first_cache, second_cache, w_out)
+    )(table, queries, first_cache, second_cache)
 
     got = exchange(partial, "pool", pools, FIRST)
 
@@ -401,7 +405,7 @@
         [VMEM, VMEM, VMEM],
     )(got, own, held_out)
 
-    spread = exchange(mixed, "mp", shards)
+    spread = exchange(mixed, "mp", shards, FIRST_SHARD)
     total = jnp.sum(spread.reshape(shards, features), axis=0, keepdims=True)
     return (hidden + RESIDUAL_SCALE * total, new_kv)
 

time: 66.2 us -> 65.9 us (level)
  waiting for transfers between devices: 2.2 us -> 0.01 us
  starting transfers between devices: 24.1 us -> 25.7 us
  local copies, waits for them, and re-layouts: 1.38 us -> 2.35 us
    all_to_all x2, waiting for transfers between devices: 2.2 us -> 0.01 us  [exchange(): lax.all_to_all(x, axis, split_axis=0, concat_axis=0, tiled=True, axis_ind...]
    all_to_all x2, starting transfers between devices: 24.1 us -> 25.7 us  [exchange(): lax.all_to_all(x, axis, split_axis=0, concat_axis=0, tiled=True, axis_ind...]
    pallas_call x1, Pallas kernels: 3.48 us -> 2.35 us  [per_device(): call(attend_kernel, 'attend', jax.ShapeDtypeStruct((requests * GROUP, wid...]
    unnamed x2 -> x6, local copies, waits for them, and re-layouts: 0.01 us -> 0.97 us
    pallas_call x1, Pallas kernels: 1.94 us -> 2.83 us  [per_device(): call(functools.partial(keyval_kernel, head_dim), 'keyval', (jax.ShapeDtyp...]
  transfers between devices with their start and end apart: 2 -> 2, of which waited for: 1 -> 0; matrix products, arithmetic and copies ran while one was open for 0% -> 0% of each run, Pallas kernels for 10% -> 11%
where the time goes in v5:
time: 65.9 us; the launch traced here: 65.4 us
  starting transfers between devices  25.7 us (39%)
  blocking collectives  24.6 us (37%)
  Pallas kernels  11.4 us (17%)
  local copies, waits for them, and re-layouts  2.35 us (4%)
  between operations  0.7 us (1%)
    all_to_all x2, starting transfers between devices, exchange(): lax.all_to_all(x, axis, split_axis=0, concat_axis=0, tiled=True, axis_ind...  25.7 us
    all_to_all x2, blocking collectives, exchange(): lax.all_to_all(x, axis, split_axis=0, concat_axis=0, tiled=True, axis_ind...  24.6 us
    pallas_call x1, Pallas kernels, per_device(): call(functools.partial(keyval_kernel, head_dim), 'keyval', (jax.ShapeDtyp...  2.83 us
    pallas_call x1, Pallas kernels, per_device(): call(functools.partial(prepare_kernel, head_dim), 'prepare', (jax.ShapeDt...  2.43 us
    pallas_call x1, Pallas kernels, per_device(): call(attend_kernel, 'attend', jax.ShapeDtypeStruct((requests * GROUP, wid...  2.35 us
    pallas_call x1, Pallas kernels, per_device(): call(functools.partial(table_kernel, slots_here, block_len), 'slot_table'...  2.22 us
  transfers between devices with their start and end apart: 2, of which 0 were waited for; matrix products, arithmetic and copies ran while one was open for 0% of the time, Pallas kernels for 11%

profile of v5, /device:TPU:1, one launch (start us, length us, event | category | flops | bytes accessed | tf_op | source)
XLA Modules:
  0.0 65.4 jit_solution(16687232923929293967)
XLA Ops:
  0.6 1.3 %broadcast_in_dim.9 = f32[8,2,128]{2,1,0:T(2,128)} broadcast(f32[2,128]{1,0:T(2,128)} %bitcast.20), dimensions={1,2} | broadcast | bytes 9216 | tf_op jit(solution)/shard_map/broadcast_in_dim | solution.py:325
  1.9 11.3 %all-to-all-start = ((f32[8,2,128]{2,1,0:T(2,128)}), f32[8,2,128]{2,1,0:T(2,128)S(1)}, u32[]{:S(2)}, u32[]{:S(2)}) async-start(f32[8,2,128]{2,1,0:T(2,128)} %broadcast_in_dim.9), calls=%async_computation | async-start | bytes 16384 | tf_op jit(solution)/shard_map/all_to_all | solution.py:310
  13.2 2.4 %prepare.1 = (bf16[2048,256]{1,0:T(8,128)(2,1)S(1)}, f32[16,128]{1,0:T(8,128)S(1)}, bf16[48,128,128]{2,1,0:T(8,128)(2,1)S(1)}, f32[8,128]{1,0:T(8,128)S(1)}, f32[8,128]{1,0:T(8,128)S(1)}) custom-call(s32[1]{0:T(128)} %bitcast.place_ref, s32[64]{0:T(128)} %lengths_ref.3, bf16[2048,256]{1,0:T(8,128)(2,1)} %w_ref.2, f32[16,128]{1,0:T(8,128)} %bitcast.19, ...), custom_call_target="tpu_custom_call" | custom-call | tf_op jit(solution)/shard_map/prepare/pallas_call | solution.py:337
  15.7 0.0 all-to-all-done
  15.7 1.1 %query.1.query_ref = bf16[256,128]{1,0:T(8,128)(2,1)} custom-call(f32[16,128]{1,0:T(8,128)S(1)} %bitcast.14, f32[16,128]{1,0:T(8,128)S(1)} %get-tuple-element.15.gain_ref, bf16[2048,256]{1,0:T(8,128)(2,1)S(1)} %get-tuple-element.18.w_ref, f32[8,128]{1,0:T(8,128)S(1)} %get-tuple-element.16.cos_ref, f32[8,128]{1,0:T(8,128)S(1)} %get-tuple-element.17.sin_ref), custom_call_target="tpu_custom_call" | custom-call | tf_op jit(solution)/shard_map/query/pallas_call | solution.py:352
  16.8 14.3 %all-to-all-start.1 = ((bf16[64,4,128]{2,1,0:T(4,128)(2,1)}), bf16[64,4,128]{2,1,0:T(4,128)(2,1)S(1)}, u32[]{:S(2)}, u32[]{:S(2)}) async-start(bf16[64,4,128]{2,1,0:T(4,128)(2,1)} %bitcast.5), calls=%async_computation.1 | async-start | bytes 131072 | tf_op jit(solution)/shard_map/all_to_all | solution.py:310
  31.1 2.2 %slot_table.1 = (s32[96,128]{1,0:T(8,128)S(1)}, bf16[48,128,128]{2,1,0:T(8,128)(2,1)S(1)}) custom-call(s32[1]{0:T(128)} %bitcast.place_ref, s32[64]{0:T(128)} %lengths_ref.3, s32[64,128]{1,0:T(8,128)} %slot_ref.1, bf16[96,128,128]{2,1,0:T(8,128)(2,1)} %bitcast.18), custom_call_target="tpu_custom_call" | custom-call | tf_op jit(solution)/shard_map/slot_table/pallas_call | solution.py:361
  33.4 0.1 slice_reduce_fusion.tab_ref
  33.5 2.8 %keyval.1 = (bf16[1,128]{1,0:T(2,128)(2,1)}, f32[8,128]{1,0:T(8,128)S(1)}, bf16[256,2048]{1,0:T(8,128)(2,1)S(1)}) custom-call(f32[16,128]{1,0:T(8,128)S(1)} %bitcast.15, f32[16,128]{1,0:T(8,128)S(1)} %get-tuple-element.15.gain_ref, f32[8,128]{1,0:T(8,128)S(1)} %get-tuple-element.16.cos_ref, f32[8,128]{1,0:T(8,128)S(1)} %get-tuple-element.17.sin_ref, ...), custom_call_target="tpu_custom_call" | custom-call | tf_op jit(solution)/shard_map/keyval/pallas_call | solution.py:370
  36.3 0.0 copy-start
  36.3 1.0 %copy-done = bf16[256,2048]{1,0:T(8,128)(2,1)} copy-done((bf16[256,2048]{1,0:T(8,128)(2,1)}, bf16[256,2048]{1,0:T(8,128)(2,1)S(1)}, u32[]{:S(2)}) %copy-start) | copy-done | bytes 1048600
  37.3 0.0 all-to-all-done.1
  37.3 0.0 copy-start.1
  37.3 0.0 copy-start.2
  37.3 2.4 %attend.1 = f32[256,128]{1,0:T(8,128)S(1)} custom-call(s32[96]{0:T(128)S(1)} %slice_reduce_fusion.tab_ref, bf16[256,128]{1,0:T(8,128)(2,1)S(1)} %bitcast.13, bf16[48,128,128]{2,1,0:T(8,128)(2,1)S(1)} %get-tuple-element.21.first_ref, bf16[48,128,128]{2,1,0:T(8,128)(2,1)S(1)} %get-tuple-element.22.second_ref), custom_call_target="tpu_custom_call" | custom-call | tf_op jit(solution)/shard_map/attend/pallas_call | solution.py:384
  39.6 15.7 %all_to_all.20 = f32[64,4,128]{2,1,0:T(4,128)S(1)} all-to-all(f32[64,4,128]{2,1,0:T(4,128)S(1)} %bitcast.11), channel_id=1, replica_groups={{352,360,368,376,384,392,400,408,416,424,432,440,448,456,464,472,480,48..., dimensions={0} | all-to-all | bytes 262144 | tf_op jit(solution)/shard_map/all_to_all | solution.py:310
  55.4 0.0 copy-done.1
  55.4 0.5 combine.1
  55.9 8.9 %all_to_all.21 = f32[8,2,128]{2,1,0:T(2,128)S(1)} all-to-all(f32[8,2,128]{2,1,0:T(2,128)S(1)} %bitcast.16), channel_id=1, replica_groups={{4,5,6,7,0,1,2,3},{12,13,14,15,8,9,10,11},{20,21,22,23,16,17,18,19},{28..., dimensions={0} | all-to-all | bytes 16384 | tf_op jit(solution)/shard_map/all_to_all | solution.py:310
  64.8 0.0 copy-done.2
  64.8 0.6 add.3
  (2 shorter events, 0.0 us)
Async XLA Ops:
  1.9 13.8 %all-to-all-start = ((f32[8,2,128]{2,1,0:T(2,128)}), f32[8,2,128]{2,1,0:T(2,128)S(1)}, u32[]{:S(2)}, u32[]{:S(2)}) async-start(f32[8,2,128]{2,1,0:T(2,128)} %broadcast_in_dim.9), calls=%async_computation | async-start | bytes 16384 | tf_op jit(solution)/shard_map/all_to_all | solution.py:310
  16.8 20.5 %all-to-all-start.1 = ((bf16[64,4,128]{2,1,0:T(4,128)(2,1)}), bf16[64,4,128]{2,1,0:T(4,128)(2,1)S(1)}, u32[]{:S(2)}, u32[]{:S(2)}) async-start(bf16[64,4,128]{2,1,0:T(4,128)(2,1)} %bitcast.5), calls=%async_computation.1 | async-start | bytes 131072 | tf_op jit(solution)/shard_map/all_to_all | solution.py:310
  36.3 1.0 %copy-start = (bf16[256,2048]{1,0:T(8,128)(2,1)}, bf16[256,2048]{1,0:T(8,128)(2,1)S(1)}, u32[]{:S(2)}) copy-start(bf16[256,2048]{1,0:T(8,128)(2,1)S(1)} %get-tuple-element.24.w_ref) | copy-start | bytes 3145732
  37.3 18.1 %copy-start.1 = (bf16[256,2048]{1,0:T(8,128)(2,1)S(1)}, bf16[256,2048]{1,0:T(8,128)(2,1)}, u32[]{:S(2)}) copy-start(bf16[256,2048]{1,0:T(8,128)(2,1)} %copy-done) | copy-start | bytes 3145732
  37.3 27.5 %copy-start.2 = (f32[1,256]{1,0:T(1,128)S(1)}, f32[1,256]{1,0:T(1,128)}, u32[]{:S(2)}) copy-start(f32[1,256]{1,0:T(1,128)} %param.8) | copy-start | bytes 3076

commit v6 on v5

--- a/solution.py
+++ b/solution.py
@@ -119,14 +119,18 @@
     return copies
 
 
-def prepare_kernel(
-    head_dim, place_ref, lengths_ref, w_ref, gain_ref, cache_ref, *rest
-):
-    held_w_ref, held_gain_ref, held_cache_ref, cos_ref, sin_ref, sems = rest
+def prepare_kernel(head_dim, lengths_ref, w_ref, gain_ref, cache_ref, *rest):
+    held_w_ref, held_gain_ref, held_cache_ref, cos_ref, sin_ref, near_lengths, sems = rest
     first = cache_ref.at[pl.ds(0, held_cache_ref.shape[0])]
-    copies = fetch((w_ref, gain_ref, first), (held_w_ref, held_gain_ref, held_cache_ref), sems)
-    cos_ref[...], sin_ref[...] = rotation(lengths_ref[place_ref[0]], head_dim, 2 * head_dim)
-    for copy in copies:
+    copies = fetch(
+        (lengths_ref, w_ref, gain_ref, first),
+        (near_lengths, held_w_ref, held_gain_ref, held_cache_ref),
+        sems,
+    )
+    copies[0].wait()
+    position = near_lengths[lax.axis_index("pool")]
+    cos_ref[...], sin_ref[...] = rotation(position, head_dim, 2 * head_dim)
+    for copy in copies[1:]:
         copy.wait()
 
 
@@ -147,11 +151,12 @@
 
 
 def keyval_kernel(
-    head_dim, rows_ref, gain_ref, cos_ref, sin_ref, query_ref, w_ref, w_out_ref, *rest
+    head_dim, rows_ref, gain_ref, cos_ref, sin_ref, query_ref, w_hbm, kv_ref, own_ref, w_ref, sems
 ):
-    kv_ref, own_ref, held_ref, sems = rest
-    copies = fetch((w_out_ref,), (held_ref,), sems)
-    keyval = project(normalise(rows_ref, gain_ref), w_ref)
+    copies = fetch((w_hbm,), (w_ref,), sems)
+    normed = normalise(rows_ref, gain_ref)
+    copies[0].wait()
+    keyval = project(normed, w_ref)
     is_key = lanes(keyval.shape) < head_dim
     turned = rope(keyval, cos_ref[...], sin_ref[...], head_dim // 2)
     both = jnp.where(is_key, turned, keyval).astype(BF16)
@@ -159,16 +164,21 @@
     both = both.astype(F32)
     score = jnp.sum(query_ref[:8, :].astype(F32) * both, axis=1, keepdims=True)
     own_ref[...] = jnp.where(is_key, score, both)
-    copies[0].wait()
 
 
 def table_kernel(
-    slots_here, block_len, place_ref, lengths_ref, slot_ref, cache_ref, out_ref, held_ref, sems
+    slots_here, block_len, lengths_hbm, slot_hbm, cache_ref, out_ref, held_ref, lengths_ref, slot_ref, sems
 ):
     count = held_ref.shape[0]
-    copies = fetch((cache_ref.at[pl.ds(slots_here - count, count)],), (held_ref,), sems)
+    copies = fetch(
+        (lengths_hbm, slot_hbm, cache_ref.at[pl.ds(slots_here - count, count)]),
+        (lengths_ref, slot_ref, held_ref),
+        sems,
+    )
+    copies[0].wait()
+    copies[1].wait()
     requests, blocks = slot_ref.shape
-    base = place_ref[0] * slots_here
+    base = lax.axis_index("pool") * slots_here
     sub = subs((8, blocks))
     lane = lanes((8, blocks))
     wanted, payload = [], []
@@ -192,7 +202,7 @@
         out_ref[pl.ds(8 * tile, 8), :] = jnp.broadcast_to(
             jnp.max(picked.astype(F32), axis=1, keepdims=True), (8, blocks)
         ).astype(jnp.int32)
-    copies[0].wait()
+    copies[2].wait()
 
 
 def attend_kernel(
@@ -262,7 +272,11 @@
         out_ref[pl.ds(8 * v, 8), :] = jnp.where(low, tiles[0], tiles[1])
 
 
-def combine_kernel(got_ref, own_ref, w_ref, out_ref):
+def combine_kernel(got_ref, own_ref, w_hbm, out_ref, w_ref, sems):
+    tiles = out_ref.shape[0] // 8
+    share = w_ref.shape[1] // tiles
+    columns_of = [pl.ds((v + FIRST_SHARD * GROUP // 16) % tiles * share, share) for v in range(tiles)]
+    copies = fetch([w_hbm.at[:, c] for c in columns_of], [w_ref.at[:, c] for c in columns_of], sems)
     rows, wide = got_ref.shape
     lane = lanes((8, wide))
     row = subs((8, wide))
@@ -293,10 +307,9 @@
         for c in range(GROUP // 2)
     ]
     line = jnp.broadcast_to(jnp.concatenate(chunks, axis=1), (8, GROUP // 2 * wide)).astype(BF16)
-    lines = out_ref.shape[0]
-    for v in range(lines // 8):
-        at = (8 * v + FIRST_SHARD * GROUP // 2) % lines * wide
-        part = jnp.dot(line, w_ref[:, pl.ds(at, 8 * wide)], preferred_element_type=F32)
+    for v, columns in enumerate(columns_of):
+        copies[v].wait()
+        part = jnp.dot(line, w_ref[:, columns], preferred_element_type=F32)
         tile = jnp.zeros((8, wide), F32)
         for k in range(8):
             tile = jnp.where(row == k, part[:, k * wide : (k + 1) * wide], tile)
@@ -320,7 +333,6 @@
     pools = lax.axis_size("pool")
     features = hidden.shape[1]
     lines = features // wide
-    place = lax.axis_index("pool").astype(jnp.int32).reshape(1)
     rows = exchange(
         jnp.broadcast_to(hidden.reshape(1, lines, wide), (shards, lines, wide)).reshape(-1, wide),
         "mp",
@@ -344,10 +356,10 @@
             turn,
             turn,
         ),
-        [SMEM, SMEM, HBM, HBM, HBM],
-        [pltpu.SemaphoreType.DMA((3,))],
+        [HBM] * 4,
+        [pltpu.SMEM(lengths.shape, jnp.int32), pltpu.SemaphoreType.DMA((4,))],
         limit=8 << 20,
-    )(place, lengths, w_query, gain, cache)
+    )(lengths, w_query, gain, cache)
 
     query = call(
         functools.partial(query_kernel, head_dim),
@@ -362,22 +374,22 @@
         functools.partial(table_kernel, slots_here, block_len),
         "slot_table",
         (jax.ShapeDtypeStruct((slots_here, block_slot.shape[1]), jnp.int32), half_cache),
-        [SMEM, SMEM, VMEM, HBM],
-        [pltpu.SemaphoreType.DMA((1,))],
-    )(place, lengths, block_slot, cache)
+        [HBM] * 3,
+        [
+            pltpu.SMEM(lengths.shape, jnp.int32),
+            pltpu.VMEM(block_slot.shape, jnp.int32),
+            pltpu.SemaphoreType.DMA((3,)),
+        ],
+    )(lengths, block_slot, cache)
     table = table[:, 0]
 
-    new_kv, own, held_out = call(
+    new_kv, own = call(
         functools.partial(keyval_kernel, head_dim),
         "keyval",
-        (
-            jax.ShapeDtypeStruct((1, wide), BF16),
-            turn,
-            jax.ShapeDtypeStruct(w_out.shape, BF16),
-        ),
-        [VMEM] * 6 + [HBM],
-        [pltpu.SemaphoreType.DMA((1,))],
-    )(rows, held_gain, cosine, sine, query, w_keyval, w_out)
+        (jax.ShapeDtypeStruct((1, wide), BF16), turn),
+        [VMEM] * 5 + [HBM],
+        [pltpu.VMEM(w_keyval.shape, BF16), pltpu.SemaphoreType.DMA((1,))],
+    )(rows, held_gain, cosine, sine, query, w_keyval)
     table, own = lax.optimization_barrier((table, own))
 
     per_request = pltpu.VMEM((requests, 8, wide), F32)
@@ -402,8 +414,9 @@
         combine_kernel,
         "combine",
         jax.ShapeDtypeStruct((shards * lines, wide), F32),
-        [VMEM, VMEM, VMEM],
-    )(got, own, held_out)
+        [VMEM, VMEM, HBM],
+        [pltpu.VMEM(w_out.shape, BF16), pltpu.SemaphoreType.DMA((shards * lines // 8,))],
+    )(got, own, w_out)
 
     spread = exchange(mixed, "mp", shards, FIRST_SHARD)
     total = jnp.sum(spread.reshape(shards, features), axis=0, keepdims=True)

time: 65.9 us -> 65 us (0.986)
  local copies, waits for them, and re-layouts: 2.35 us -> 1.39 us
    unnamed x6 -> x2, local copies, waits for them, and re-layouts: 0.97 us -> 0.01 us
    pallas_call x1, Pallas kernels: 0.51 us -> 1.44 us  [per_device(): call(combine_kernel, 'combine', jax.ShapeDtypeStruct((shards * lines, wid...]
    pallas_call x1, Pallas kernels: 2.22 us -> 1.46 us  [per_device(): call(functools.partial(table_kernel, slots_here, block_len), 'slot_table'...]
  transfers between devices with their start and end apart: 2 -> 2, of which waited for: 0 -> 1; matrix products, arithmetic and copies ran while one was open for 0% -> 0% of each run, Pallas kernels for 11% -> 9%
where the time goes in v6:
time: 65 us; the launch traced here: 64.5 us
  starting transfers between devices  25.7 us (40%)
  blocking collectives  25.1 us (39%)
  Pallas kernels  10.8 us (17%)
  local copies, waits for them, and re-layouts  1.39 us (2%)
  between operations  0.71 us (1%)
    all_to_all x2, starting transfers between devices, exchange(): lax.all_to_all(x, axis, split_axis=0, concat_axis=0, tiled=True, axis_ind...  25.7 us
    all_to_all x2, blocking collectives, exchange(): lax.all_to_all(x, axis, split_axis=0, concat_axis=0, tiled=True, axis_ind...  25.1 us
    pallas_call x1, Pallas kernels, per_device(): call(functools.partial(keyval_kernel, head_dim), 'keyval', (jax.ShapeDtyp...  2.67 us
    pallas_call x1, Pallas kernels, per_device(): call(attend_kernel, 'attend', jax.ShapeDtypeStruct((requests * GROUP, wid...  2.38 us
    pallas_call x1, Pallas kernels, per_device(): call(functools.partial(prepare_kernel, head_dim), 'prepare', (jax.ShapeDt...  1.78 us
    pallas_call x1, Pallas kernels, per_device(): call(functools.partial(table_kernel, slots_here, block_len), 'slot_table'...  1.46 us
    pallas_call x1, Pallas kernels, per_device(): call(combine_kernel, 'combine', jax.ShapeDtypeStruct((shards * lines, wid...  1.44 us
  transfers between devices with their start and end apart: 2, of which 1 were waited for; matrix products, arithmetic and copies ran while one was open for 0% of the time, Pallas kernels for 9%

profile of v6, /device:TPU:1, one launch (start us, length us, event | category | flops | bytes accessed | tf_op | source)
XLA Modules:
  0.0 64.5 jit_solution(5059779281084077792)
XLA Ops:
  0.6 1.3 %broadcast_in_dim.9 = f32[8,2,128]{2,1,0:T(2,128)} broadcast(f32[2,128]{1,0:T(2,128)} %bitcast.19), dimensions={1,2} | broadcast | bytes 9216 | tf_op jit(solution)/shard_map/broadcast_in_dim | solution.py:337
  1.9 11.3 %all-to-all-start = ((f32[8,2,128]{2,1,0:T(2,128)}), f32[8,2,128]{2,1,0:T(2,128)S(1)}, u32[]{:S(2)}, u32[]{:S(2)}) async-start(f32[8,2,128]{2,1,0:T(2,128)} %broadcast_in_dim.9), calls=%async_computation | async-start | bytes 16384 | tf_op jit(solution)/shard_map/all_to_all | solution.py:323
  13.2 1.8 %prepare.1 = (bf16[2048,256]{1,0:T(8,128)(2,1)S(1)}, f32[16,128]{1,0:T(8,128)S(1)}, bf16[48,128,128]{2,1,0:T(8,128)(2,1)S(1)}, f32[8,128]{1,0:T(8,128)S(1)}, f32[8,128]{1,0:T(8,128)S(1)}) custom-call(s32[64]{0:T(128)} %lengths_ref.1, bf16[2048,256]{1,0:T(8,128)(2,1)} %w_ref.1, f32[16,128]{1,0:T(8,128)} %bitcast.18, bf16[96,128,128]{2,1,0:T(8,128)(2,1)} %bitcast.16), custom_call_target="tpu_custom_call" | custom-call | tf_op jit(solution)/shard_map/prepare/pallas_call | solution.py:349
  15.0 0.2 all-to-all-done
  15.2 1.1 %query.1.query_ref = bf16[256,128]{1,0:T(8,128)(2,1)} custom-call(f32[16,128]{1,0:T(8,128)S(1)} %bitcast.13, f32[16,128]{1,0:T(8,128)S(1)} %get-tuple-element.14.gain_ref, bf16[2048,256]{1,0:T(8,128)(2,1)S(1)} %get-tuple-element.17.w_ref, f32[8,128]{1,0:T(8,128)S(1)} %get-tuple-element.15.cos_ref, f32[8,128]{1,0:T(8,128)S(1)} %get-tuple-element.16.sin_ref), custom_call_target="tpu_custom_call" | custom-call | tf_op jit(solution)/shard_map/query/pallas_call | solution.py:364
  16.3 14.4 %all-to-all-start.1 = ((bf16[64,4,128]{2,1,0:T(4,128)(2,1)}), bf16[64,4,128]{2,1,0:T(4,128)(2,1)S(1)}, u32[]{:S(2)}, u32[]{:S(2)}) async-start(bf16[64,4,128]{2,1,0:T(4,128)(2,1)} %bitcast.4), calls=%async_computation.1 | async-start | bytes 131072 | tf_op jit(solution)/shard_map/all_to_all | solution.py:323
  30.7 1.5 %slot_table.1 = (s32[96,128]{1,0:T(8,128)S(1)}, bf16[48,128,128]{2,1,0:T(8,128)(2,1)S(1)}) custom-call(s32[64]{0:T(128)} %lengths_ref.1, s32[64,128]{1,0:T(8,128)} %slot_hbm.1, bf16[96,128,128]{2,1,0:T(8,128)(2,1)} %bitcast.17), custom_call_target="tpu_custom_call" | custom-call | tf_op jit(solution)/shard_map/slot_table/pallas_call | solution.py:373
  32.1 0.1 slice_reduce_fusion.tab_ref
  32.2 2.7 %keyval.1 = (bf16[1,128]{1,0:T(2,128)(2,1)}, f32[8,128]{1,0:T(8,128)S(1)}) custom-call(f32[16,128]{1,0:T(8,128)S(1)} %bitcast.14, f32[16,128]{1,0:T(8,128)S(1)} %get-tuple-element.14.gain_ref, f32[8,128]{1,0:T(8,128)S(1)} %get-tuple-element.15.cos_ref, f32[8,128]{1,0:T(8,128)S(1)} %get-tuple-element.16.sin_ref, bf16[256,128]{1,0:T(8,128)(2,1)} %query.1.query_ref, ...), custom_call_target="tpu_custom_call" | custom-call | tf_op jit(solution)/shard_map/keyval/pallas_call | solution.py:386
  34.9 0.0 all-to-all-done.1
  34.9 0.0 copy-start
  35.0 2.4 %attend.1 = f32[256,128]{1,0:T(8,128)S(1)} custom-call(s32[96]{0:T(128)S(1)} %slice_reduce_fusion.tab_ref, bf16[256,128]{1,0:T(8,128)(2,1)S(1)} %bitcast.12, bf16[48,128,128]{2,1,0:T(8,128)(2,1)S(1)} %get-tuple-element.20.first_ref, bf16[48,128,128]{2,1,0:T(8,128)(2,1)S(1)} %get-tuple-element.21.second_ref), custom_call_target="tpu_custom_call" | custom-call | tf_op jit(solution)/shard_map/attend/pallas_call | solution.py:396
  37.3 15.7 %all_to_all.20 = f32[64,4,128]{2,1,0:T(4,128)S(1)} all-to-all(f32[64,4,128]{2,1,0:T(4,128)S(1)} %bitcast.10), channel_id=1, replica_groups={{352,360,368,376,384,392,400,408,416,424,432,440,448,456,464,472,480,48..., dimensions={0} | all-to-all | bytes 262144 | tf_op jit(solution)/shard_map/all_to_all | solution.py:323
  53.1 1.4 %combine.1 = f32[16,128]{1,0:T(8,128)S(1)} custom-call(f32[256,128]{1,0:T(8,128)S(1)} %bitcast.11, f32[8,128]{1,0:T(8,128)S(1)} %get-tuple-element.22.own_ref, bf16[256,2048]{1,0:T(8,128)(2,1)} %w_hbm.3), custom_call_target="tpu_custom_call" | custom-call | tf_op jit(solution)/shard_map/combine/pallas_call | solution.py:413
  54.5 9.4 %all_to_all.21 = f32[8,2,128]{2,1,0:T(2,128)S(1)} all-to-all(f32[8,2,128]{2,1,0:T(2,128)S(1)} %bitcast.15), channel_id=1, replica_groups={{4,5,6,7,0,1,2,3},{12,13,14,15,8,9,10,11},{20,21,22,23,16,17,18,19},{28..., dimensions={0} | all-to-all | bytes 16384 | tf_op jit(solution)/shard_map/all_to_all | solution.py:323
  63.9 0.0 copy-done
  63.9 0.6 add.3
  (2 shorter events, 0.0 us)
Async XLA Ops:
  1.9 13.3 %all-to-all-start = ((f32[8,2,128]{2,1,0:T(2,128)}), f32[8,2,128]{2,1,0:T(2,128)S(1)}, u32[]{:S(2)}, u32[]{:S(2)}) async-start(f32[8,2,128]{2,1,0:T(2,128)} %broadcast_in_dim.9), calls=%async_computation | async-start | bytes 16384 | tf_op jit(solution)/shard_map/all_to_all | solution.py:323
  16.3 18.6 %all-to-all-start.1 = ((bf16[64,4,128]{2,1,0:T(4,128)(2,1)}), bf16[64,4,128]{2,1,0:T(4,128)(2,1)S(1)}, u32[]{:S(2)}, u32[]{:S(2)}) async-start(bf16[64,4,128]{2,1,0:T(4,128)(2,1)} %bitcast.4), calls=%async_computation.1 | async-start | bytes 131072 | tf_op jit(solution)/shard_map/all_to_all | solution.py:323
  34.9 29.0 %copy-start = (f32[1,256]{1,0:T(1,128)S(1)}, f32[1,256]{1,0:T(1,128)}, u32[]{:S(2)}) copy-start(f32[1,256]{1,0:T(1,128)} %param.8) | copy-start | bytes 3076

commit v7 on v6

--- a/solution.py
+++ b/solution.py
@@ -119,6 +119,14 @@
     return copies
 
 
+def spread_kernel(x_ref, out_ref, sems):
+    size = x_ref.shape[0]
+    shares = range(out_ref.shape[0] // size)
+    copies = fetch([x_ref for _ in shares], [out_ref.at[pl.ds(i * size, size)] for i in shares], sems)
+    for copy in copies:
+        copy.wait()
+
+
 def prepare_kernel(head_dim, lengths_ref, w_ref, gain_ref, cache_ref, *rest):
     held_w_ref, held_gain_ref, held_cache_ref, cos_ref, sin_ref, near_lengths, sems = rest
     first = cache_ref.at[pl.ds(0, held_cache_ref.shape[0])]
@@ -151,11 +159,12 @@
 
 
 def keyval_kernel(
-    head_dim, rows_ref, gain_ref, cos_ref, sin_ref, query_ref, w_hbm, kv_ref, own_ref, w_ref, sems
+    head_dim, rows_ref, gain_ref, cos_ref, sin_ref, query_hbm, w_hbm, kv_ref, own_ref, w_ref, query_ref, sems
 ):
-    copies = fetch((w_hbm,), (w_ref,), sems)
+    copies = fetch((w_hbm, query_hbm.at[pl.ds(0, query_ref.shape[0])]), (w_ref, query_ref), sems)
     normed = normalise(rows_ref, gain_ref)
-    copies[0].wait()
+    for copy in copies:
+        copy.wait()
     keyval = project(normed, w_ref)
     is_key = lanes(keyval.shape) < head_dim
     turned = rope(keyval, cos_ref[...], sin_ref[...], head_dim // 2)
@@ -272,11 +281,7 @@
         out_ref[pl.ds(8 * v, 8), :] = jnp.where(low, tiles[0], tiles[1])
 
 
-def combine_kernel(got_ref, own_ref, w_hbm, out_ref, w_ref, sems):
-    tiles = out_ref.shape[0] // 8
-    share = w_ref.shape[1] // tiles
-    columns_of = [pl.ds((v + FIRST_SHARD * GROUP // 16) % tiles * share, share) for v in range(tiles)]
-    copies = fetch([w_hbm.at[:, c] for c in columns_of], [w_ref.at[:, c] for c in columns_of], sems)
+def combine_kernel(got_ref, own_ref, w_ref, out_ref):
     rows, wide = got_ref.shape
     lane = lanes((8, wide))
     row = subs((8, wide))
@@ -307,9 +312,10 @@
         for c in range(GROUP // 2)
     ]
     line = jnp.broadcast_to(jnp.concatenate(chunks, axis=1), (8, GROUP // 2 * wide)).astype(BF16)
-    for v, columns in enumerate(columns_of):
-        copies[v].wait()
-        part = jnp.dot(line, w_ref[:, columns], preferred_element_type=F32)
+    lines = out_ref.shape[0]
+    for v in range(lines // 8):
+        at = (8 * v + FIRST_SHARD * GROUP // 2) % lines * wide
+        part = jnp.dot(line, w_ref[:, pl.ds(at, 8 * wide)], preferred_element_type=F32)
         tile = jnp.zeros((8, wide), F32)
         for k in range(8):
             tile = jnp.where(row == k, part[:, k * wide : (k + 1) * wide], tile)
@@ -334,7 +340,14 @@
     features = hidden.shape[1]
     lines = features // wide
     rows = exchange(
-        jnp.broadcast_to(hidden.reshape(1, lines, wide), (shards, lines, wide)).reshape(-1, wide),
+        pl.pallas_call(
+            spread_kernel,
+            out_shape=jax.ShapeDtypeStruct((shards * lines, wide), F32),
+            in_specs=[HBM],
+            out_specs=HBM,
+            scratch_shapes=[pltpu.SemaphoreType.DMA((shards,))],
+            name="spread",
+        )(far(hidden.reshape(lines, wide))),
         "mp",
         shards,
         FIRST_SHARD,
@@ -342,7 +355,7 @@
     gain = norm_gain.reshape(shards * lines, wide)
 
     turn = jax.ShapeDtypeStruct((8, wide), F32)
-    w_query, w_keyval, w_out, gain = (far(x) for x in (w_query, w_keyval, w_out, gain))
+    w_query, w_keyval, gain = (far(x) for x in (w_query, w_keyval, gain))
     cache = far(kv_cache.reshape(slots_here, block_len, wide))
     lengths, block_slot = far(lengths), far(block_slot)
     half_cache = jax.ShapeDtypeStruct((slots_here // 2, block_len, wide), BF16)
@@ -387,9 +400,13 @@
         functools.partial(keyval_kernel, head_dim),
         "keyval",
         (jax.ShapeDtypeStruct((1, wide), BF16), turn),
-        [VMEM] * 5 + [HBM],
-        [pltpu.VMEM(w_keyval.shape, BF16), pltpu.SemaphoreType.DMA((1,))],
-    )(rows, held_gain, cosine, sine, query, w_keyval)
+        [VMEM] * 4 + [HBM] * 2,
+        [
+            pltpu.VMEM(w_keyval.shape, BF16),
+            pltpu.VMEM((16, wide), BF16),
+            pltpu.SemaphoreType.DMA((2,)),
+        ],
+    )(rows, held_gain, cosine, sine, far(query), w_keyval)
     table, own = lax.optimization_barrier((table, own))
 
     per_request = pltpu.VMEM((requests, 8, wide), F32)
@@ -414,8 +431,7 @@
         combine_kernel,
         "combine",
         jax.ShapeDtypeStruct((shards * lines, wide), F32),
-        [VMEM, VMEM, HBM],
-        [pltpu.VMEM(w_out.shape, BF16), pltpu.SemaphoreType.DMA((shards * lines // 8,))],
+        [VMEM, VMEM, VMEM],
     )(got, own, w_out)
 
     spread = exchange(mixed, "mp", shards, FIRST_SHARD)

time: 65 us -> 63.3 us (0.974)
  local copies, waits for them, and re-layouts: 1.39 us -> 0.12 us
    pallas_call x0 -> x1, Pallas kernels: none -> 1.45 us  [per_device(): pl.pallas_call(spread_kernel, out_shape=jax.ShapeDtypeStruct((shards * li...]
    broadcast_in_dim x1 -> x0, local copies, waits for them, and re-layouts: 1.28 us -> none  [per_device(): jnp.broadcast_to(hidden.reshape(1, lines, wide), (shards, lines, wide))]
    pallas_call x1, Pallas kernels: 1.44 us -> 0.52 us  [per_device(): call(combine_kernel, 'combine', jax.ShapeDtypeStruct((shards * lines, wid...]
    pallas_call x1, Pallas kernels: 2.67 us -> 1.85 us  [per_device(): call(functools.partial(keyval_kernel, head_dim), 'keyval', (jax.ShapeDtyp...]
  transfers between devices with their start and end apart: 2 -> 2, of which waited for: 1 -> 1; matrix products, arithmetic and copies ran while one was open for 0% -> 0% of each run, Pallas kernels for 9% -> 8%
where the time goes in v7:
time: 63.3 us; the launch traced here: 62.9 us
  starting transfers between devices  25.7 us (41%)
  blocking collectives  25.1 us (40%)
  Pallas kernels  10.5 us (17%)
  between operations  0.72 us (1%)
    all_to_all x2, starting transfers between devices, exchange(): lax.all_to_all(x, axis, split_axis=0, concat_axis=0, tiled=True, axis_ind...  25.7 us
    all_to_all x2, blocking collectives, exchange(): lax.all_to_all(x, axis, split_axis=0, concat_axis=0, tiled=True, axis_ind...  25.1 us
    pallas_call x1, Pallas kernels, per_device(): call(attend_kernel, 'attend', jax.ShapeDtypeStruct((requests * GROUP, wid...  2.39 us
    pallas_call x1, Pallas kernels, per_device(): call(functools.partial(keyval_kernel, head_dim), 'keyval', (jax.ShapeDtyp...  1.85 us
    pallas_call x1, Pallas kernels, per_device(): call(functools.partial(prepare_kernel, head_dim), 'prepare', (jax.ShapeDt...  1.78 us
    pallas_call x1, Pallas kernels, per_device(): call(functools.partial(table_kernel, slots_here, block_len), 'slot_table'...  1.46 us
    pallas_call x1, Pallas kernels, per_device(): pl.pallas_call(spread_kernel, out_shape=jax.ShapeDtypeStruct((shards * li...  1.45 us
  transfers between devices with their start and end apart: 2, of which 1 were waited for; matrix products, arithmetic and copies ran while one was open for 0% of the time, Pallas kernels for 8%

profile of v7, /device:TPU:1, one launch (start us, length us, event | category | flops | bytes accessed | tf_op | source)
XLA Modules:
  0.0 62.9 jit_solution(7210698675219453763)
XLA Ops:
  0.6 1.5 %spread.1 = f32[16,128]{1,0:T(8,128)} custom-call(f32[2,128]{1,0:T(2,128)} %bitcast.21), custom_call_target="tpu_custom_call" | custom-call | tf_op jit(solution)/shard_map/spread/pallas_call | solution.py:343
  2.1 11.3 %all-to-all-start = ((f32[8,2,128]{2,1,0:T(2,128)}), f32[8,2,128]{2,1,0:T(2,128)S(1)}, u32[]{:S(2)}, u32[]{:S(2)}) async-start(f32[8,2,128]{2,1,0:T(2,128)} %bitcast.19), calls=%async_computation | async-start | bytes 16384 | tf_op jit(solution)/shard_map/all_to_all | solution.py:329
  13.4 1.8 %prepare.1 = (bf16[2048,256]{1,0:T(8,128)(2,1)S(1)}, f32[16,128]{1,0:T(8,128)S(1)}, bf16[48,128,128]{2,1,0:T(8,128)(2,1)S(1)}, f32[8,128]{1,0:T(8,128)S(1)}, f32[8,128]{1,0:T(8,128)S(1)}) custom-call(s32[64]{0:T(128)} %lengths_ref.1, bf16[2048,256]{1,0:T(8,128)(2,1)} %w_ref.2, f32[16,128]{1,0:T(8,128)} %bitcast.20, bf16[96,128,128]{2,1,0:T(8,128)(2,1)} %bitcast.17), custom_call_target="tpu_custom_call" | custom-call | tf_op jit(solution)/shard_map/prepare/pallas_call | solution.py:362
  15.2 0.2 all-to-all-done
  15.4 1.1 %query.1.query_hbm = bf16[256,128]{1,0:T(8,128)(2,1)} custom-call(f32[16,128]{1,0:T(8,128)S(1)} %bitcast.14, f32[16,128]{1,0:T(8,128)S(1)} %get-tuple-element.14.gain_ref, bf16[2048,256]{1,0:T(8,128)(2,1)S(1)} %get-tuple-element.17.w_ref, f32[8,128]{1,0:T(8,128)S(1)} %get-tuple-element.15.cos_ref, f32[8,128]{1,0:T(8,128)S(1)} %get-tuple-element.16.sin_ref), custom_call_target="tpu_custom_call" | custom-call | tf_op jit(solution)/shard_map/query/pallas_call | solution.py:377
  16.5 14.3 %all-to-all-start.1 = ((bf16[64,4,128]{2,1,0:T(4,128)(2,1)}), bf16[64,4,128]{2,1,0:T(4,128)(2,1)S(1)}, u32[]{:S(2)}, u32[]{:S(2)}) async-start(bf16[64,4,128]{2,1,0:T(4,128)(2,1)} %bitcast.5), calls=%async_computation.1 | async-start | bytes 131072 | tf_op jit(solution)/shard_map/all_to_all | solution.py:329
  30.8 1.5 %slot_table.1 = (s32[96,128]{1,0:T(8,128)S(1)}, bf16[48,128,128]{2,1,0:T(8,128)(2,1)S(1)}) custom-call(s32[64]{0:T(128)} %lengths_ref.1, s32[64,128]{1,0:T(8,128)} %slot_hbm.1, bf16[96,128,128]{2,1,0:T(8,128)(2,1)} %bitcast.18), custom_call_target="tpu_custom_call" | custom-call | tf_op jit(solution)/shard_map/slot_table/pallas_call | solution.py:386
  32.3 0.1 slice_reduce_fusion.tab_ref
  32.4 1.8 %keyval.1 = (bf16[1,128]{1,0:T(2,128)(2,1)}, f32[8,128]{1,0:T(8,128)S(1)}) custom-call(f32[16,128]{1,0:T(8,128)S(1)} %bitcast.15, f32[16,128]{1,0:T(8,128)S(1)} %get-tuple-element.14.gain_ref, f32[8,128]{1,0:T(8,128)S(1)} %get-tuple-element.15.cos_ref, f32[8,128]{1,0:T(8,128)S(1)} %get-tuple-element.16.sin_ref, bf16[256,128]{1,0:T(8,128)(2,1)} %query.1.query_hbm, ...), custom_call_target="tpu_custom_call" | custom-call | tf_op jit(solution)/shard_map/keyval/pallas_call | solution.py:399
  34.3 0.0 all-to-all-done.1
  34.3 0.0 copy-start
  34.3 0.0 copy-start.1
  34.3 2.4 %attend.1 = f32[256,128]{1,0:T(8,128)S(1)} custom-call(s32[96]{0:T(128)S(1)} %slice_reduce_fusion.tab_ref, bf16[256,128]{1,0:T(8,128)(2,1)S(1)} %bitcast.13, bf16[48,128,128]{2,1,0:T(8,128)(2,1)S(1)} %get-tuple-element.20.first_ref, bf16[48,128,128]{2,1,0:T(8,128)(2,1)S(1)} %get-tuple-element.21.second_ref), custom_call_target="tpu_custom_call" | custom-call | tf_op jit(solution)/shard_map/attend/pallas_call | solution.py:413
  36.7 15.7 %all_to_all.20 = f32[64,4,128]{2,1,0:T(4,128)S(1)} all-to-all(f32[64,4,128]{2,1,0:T(4,128)S(1)} %bitcast.11), channel_id=1, replica_groups={{352,360,368,376,384,392,400,408,416,424,432,440,448,456,464,472,480,48..., dimensions={0} | all-to-all | bytes 262144 | tf_op jit(solution)/shard_map/all_to_all | solution.py:329
  52.4 0.0 copy-done
  52.4 0.5 combine.1
  52.9 9.4 %all_to_all.21 = f32[8,2,128]{2,1,0:T(2,128)S(1)} all-to-all(f32[8,2,128]{2,1,0:T(2,128)S(1)} %bitcast.16), channel_id=1, replica_groups={{4,5,6,7,0,1,2,3},{12,13,14,15,8,9,10,11},{20,21,22,23,16,17,18,19},{28..., dimensions={0} | all-to-all | bytes 16384 | tf_op jit(solution)/shard_map/all_to_all | solution.py:329
  62.3 0.0 copy-done.1
  62.4 0.6 add.3
  (2 shorter events, 0.0 us)
Async XLA Ops:
  2.1 13.3 %all-to-all-start = ((f32[8,2,128]{2,1,0:T(2,128)}), f32[8,2,128]{2,1,0:T(2,128)S(1)}, u32[]{:S(2)}, u32[]{:S(2)}) async-start(f32[8,2,128]{2,1,0:T(2,128)} %bitcast.19), calls=%async_computation | async-start | bytes 16384 | tf_op jit(solution)/shard_map/all_to_all | solution.py:329
  16.5 17.8 %all-to-all-start.1 = ((bf16[64,4,128]{2,1,0:T(4,128)(2,1)}), bf16[64,4,128]{2,1,0:T(4,128)(2,1)S(1)}, u32[]{:S(2)}, u32[]{:S(2)}) async-start(bf16[64,4,128]{2,1,0:T(4,128)(2,1)} %bitcast.5), calls=%async_computation.1 | async-start | bytes 131072 | tf_op jit(solution)/shard_map/all_to_all | solution.py:329
  34.3 18.1 %copy-start = (bf16[256,2048]{1,0:T(8,128)(2,1)S(1)}, bf16[256,2048]{1,0:T(8,128)(2,1)}, u32[]{:S(2)}) copy-start(bf16[256,2048]{1,0:T(8,128)(2,1)} %w_ref.3) | copy-start | bytes 3145732
  34.3 28.1 %copy-start.1 = (f32[1,256]{1,0:T(1,128)S(1)}, f32[1,256]{1,0:T(1,128)}, u32[]{:S(2)}) copy-start(f32[1,256]{1,0:T(1,128)} %param.8) | copy-start | bytes 3076

commit v8 on v7

--- a/solution.py
+++ b/solution.py
@@ -119,27 +119,22 @@
     return copies
 
 
-def spread_kernel(x_ref, out_ref, sems):
-    size = x_ref.shape[0]
-    shares = range(out_ref.shape[0] // size)
-    copies = fetch([x_ref for _ in shares], [out_ref.at[pl.ds(i * size, size)] for i in shares], sems)
-    for copy in copies:
-        copy.wait()
-
-
-def prepare_kernel(head_dim, lengths_ref, w_ref, gain_ref, cache_ref, *rest):
-    held_w_ref, held_gain_ref, held_cache_ref, cos_ref, sin_ref, near_lengths, sems = rest
-    first = cache_ref.at[pl.ds(0, held_cache_ref.shape[0])]
+def prepare_kernel(head_dim, x_ref, lengths_ref, w_ref, gain_ref, *rest):
+    spread_ref, held_w_ref, held_gain_ref, cos_ref, sin_ref, near_x, near_lengths, sems = rest
     copies = fetch(
-        (lengths_ref, w_ref, gain_ref, first),
-        (near_lengths, held_w_ref, held_gain_ref, held_cache_ref),
+        (x_ref, lengths_ref, w_ref, gain_ref),
+        (near_x, near_lengths, held_w_ref, held_gain_ref),
         sems,
     )
-    copies[0].wait()
+    copies[1].wait()
     position = near_lengths[lax.axis_index("pool")]
     cos_ref[...], sin_ref[...] = rotation(position, head_dim, 2 * head_dim)
-    for copy in copies[1:]:
-        copy.wait()
+    copies[0].wait()
+    size = near_x.shape[0]
+    for i in range(spread_ref.shape[0] // size):
+        spread_ref[pl.ds(i * size, size), :] = near_x[...]
+    copies[2].wait()
+    copies[3].wait()
 
 
 def query_kernel(head_dim, rows_ref, gain_ref, w_ref, cos_ref, sin_ref, out_ref):
@@ -178,12 +173,7 @@
 def table_kernel(
     slots_here, block_len, lengths_hbm, slot_hbm, cache_ref, out_ref, held_ref, lengths_ref, slot_ref, sems
 ):
-    count = held_ref.shape[0]
-    copies = fetch(
-        (lengths_hbm, slot_hbm, cache_ref.at[pl.ds(slots_here - count, count)]),
-        (lengths_ref, slot_ref, held_ref),
-        sems,
-    )
+    copies = fetch((lengths_hbm, slot_hbm, cache_ref), (lengths_ref, slot_ref, held_ref), sems)
     copies[0].wait()
     copies[1].wait()
     requests, blocks = slot_ref.shape
@@ -215,10 +205,9 @@
 
 
 def attend_kernel(
-    tab_ref, query_ref, first_ref, second_ref, out_ref, q_s, score_s, max_s, sum_s, acc_s
+    tab_ref, query_ref, kv_ref, out_ref, q_s, score_s, max_s, sum_s, acc_s
 ):
-    half, block_len, wide = first_ref.shape
-    slots_here = 2 * half
+    slots_here, block_len, wide = kv_ref.shape
     requests = query_ref.shape[0] // GROUP
     low = subs((8, wide)) < GROUP
     token = lanes((8, block_len))
@@ -235,8 +224,7 @@
     def pair(p):
         a, b = tab_ref[2 * p], tab_ref[2 * p + 1]
         live = token < jnp.where(low, a & 255, b & 255)
-        held, at = (first_ref, 2 * p) if 2 * p < half else (second_ref, 2 * p - half)
-        keys = held[pl.ds(at, 2)].reshape(2 * block_len, wide)
+        keys = kv_ref[pl.ds(2 * p, 2)].reshape(2 * block_len, wide)
         return lax.shift_right_logical(a, 8), lax.shift_right_logical(b, 8), live, keys
 
     for p in range(slots_here // 2):
@@ -339,40 +327,32 @@
     pools = lax.axis_size("pool")
     features = hidden.shape[1]
     lines = features // wide
-    rows = exchange(
-        pl.pallas_call(
-            spread_kernel,
-            out_shape=jax.ShapeDtypeStruct((shards * lines, wide), F32),
-            in_specs=[HBM],
-            out_specs=HBM,
-            scratch_shapes=[pltpu.SemaphoreType.DMA((shards,))],
-            name="spread",
-        )(far(hidden.reshape(lines, wide))),
-        "mp",
-        shards,
-        FIRST_SHARD,
-    )
-    gain = norm_gain.reshape(shards * lines, wide)
-
+    gain = far(norm_gain.reshape(shards * lines, wide))
+    cache = far(kv_cache.reshape(slots_here, block_len, wide))
+    line = far(hidden.reshape(lines, wide))
+    w_query, w_keyval, lengths, block_slot = (
+        far(x) for x in (w_query, w_keyval, lengths, block_slot)
+    )
     turn = jax.ShapeDtypeStruct((8, wide), F32)
-    w_query, w_keyval, gain = (far(x) for x in (w_query, w_keyval, gain))
-    cache = far(kv_cache.reshape(slots_here, block_len, wide))
-    lengths, block_slot = far(lengths), far(block_slot)
-    half_cache = jax.ShapeDtypeStruct((slots_here // 2, block_len, wide), BF16)
-    held_query, held_gain, first_cache, cosine, sine = call(
+    spread_rows, held_query, held_gain, cosine, sine = call(
         functools.partial(prepare_kernel, head_dim),
         "prepare",
         (
+            jax.ShapeDtypeStruct((shards * lines, wide), F32),
             jax.ShapeDtypeStruct(w_query.shape, BF16),
             jax.ShapeDtypeStruct(gain.shape, F32),
-            half_cache,
             turn,
             turn,
         ),
         [HBM] * 4,
-        [pltpu.SMEM(lengths.shape, jnp.int32), pltpu.SemaphoreType.DMA((4,))],
-        limit=8 << 20,
-    )(lengths, w_query, gain, cache)
+        [
+            pltpu.VMEM((lines, wide), F32),
+            pltpu.SMEM(lengths.shape, jnp.int32),
+            pltpu.SemaphoreType.DMA((4,)),
+        ],
+    )(line, lengths, w_query, gain)
+
+    rows = exchange(spread_rows, "mp", shards, FIRST_SHARD)
 
     query = call(
         functools.partial(query_kernel, head_dim),
@@ -383,17 +363,21 @@
 
     queries = exchange(query, "pool", pools, FIRST)
 
-    table, second_cache = call(
+    lengths, block_slot, rows = lax.optimization_barrier((lengths, block_slot, rows))
+    table, held_cache = call(
         functools.partial(table_kernel, slots_here, block_len),
         "slot_table",
-        (jax.ShapeDtypeStruct((slots_here, block_slot.shape[1]), jnp.int32), half_cache),
+        (
+            jax.ShapeDtypeStruct((slots_here, block_slot.shape[1]), jnp.int32),
+            jax.ShapeDtypeStruct(cache.shape, BF16),
+        ),
         [HBM] * 3,
         [
             pltpu.SMEM(lengths.shape, jnp.int32),
             pltpu.VMEM(block_slot.shape, jnp.int32),
             pltpu.SemaphoreType.DMA((3,)),
         ],
-    )(lengths, block_slot, cache)
+    )(far(lengths), far(block_slot), cache)
     table = table[:, 0]
 
     new_kv, own = call(
@@ -414,7 +398,7 @@
         attend_kernel,
         "attend",
         jax.ShapeDtypeStruct((requests * GROUP, wide), F32),
-        [SMEM, VMEM, VMEM, VMEM],
+        [SMEM, VMEM, VMEM],
         [
             per_request,
             pltpu.VMEM((slots_here // 2, 8, block_len), F32),
@@ -423,7 +407,7 @@
             per_request,
         ],
         limit=12 << 20,
-    )(table, queries, first_cache, second_cache)
+    )(table, queries, held_cache)
 
     got = exchange(partial, "pool", pools, FIRST)
 

time: 63.3 us -> 62.7 us (level)
  blocking collectives: 25.1 us -> 38.3 us
  starting transfers between devices: 25.7 us -> 13.7 us
  Pallas kernels: 10.5 us -> 9.02 us
    all_to_all x2 -> x3, blocking collectives: 25.1 us -> 38.3 us  [exchange(): lax.all_to_all(x, axis, split_axis=0, concat_axis=0, tiled=True, axis_ind...]
    all_to_all x2 -> x1, starting transfers between devices: 25.7 us -> 13.7 us  [exchange(): lax.all_to_all(x, axis, split_axis=0, concat_axis=0, tiled=True, axis_ind...]
    pallas_call x1 -> x0, Pallas kernels: 1.45 us -> none  [per_device(): pl.pallas_call(spread_kernel, out_shape=jax.ShapeDtypeStruct((shards * li...]
  transfers between devices with their start and end apart: 2 -> 1, of which waited for: 1 -> 0; matrix products, arithmetic and copies ran while one was open for 0% -> 0% of each run, Pallas kernels for 8% -> 6%
where the time goes in v8:
time: 62.7 us; the launch traced here: 62.4 us
  blocking collectives  38.3 us (61%)
  starting transfers between devices  13.7 us (22%)
  Pallas kernels  9.02 us (14%)
  between operations  0.71 us (1%)
    all_to_all x3, blocking collectives, exchange(): lax.all_to_all(x, axis, split_axis=0, concat_axis=0, tiled=True, axis_ind...  38.3 us
    all_to_all x1, starting transfers between devices, exchange(): lax.all_to_all(x, axis, split_axis=0, concat_axis=0, tiled=True, axis_ind...  13.7 us
    pallas_call x1, Pallas kernels, per_device(): call(attend_kernel, 'attend', jax.ShapeDtypeStruct((requests * GROUP, wid...  2.36 us
    pallas_call x1, Pallas kernels, per_device(): call(functools.partial(table_kernel, slots_here, block_len), 'slot_table'...  1.94 us
    pallas_call x1, Pallas kernels, per_device(): call(functools.partial(keyval_kernel, head_dim), 'keyval', (jax.ShapeDtyp...  1.84 us
    pallas_call x1, Pallas kernels, per_device(): call(functools.partial(prepare_kernel, head_dim), 'prepare', (jax.ShapeDt...  1.28 us
  transfers between devices with their start and end apart: 1, of which 0 were waited for; matrix products, arithmetic and copies ran while one was open for 0% of the time, Pallas kernels for 6%

profile of v8, /device:TPU:1, one launch (start us, length us, event | category | flops | bytes accessed | tf_op | source)
XLA Modules:
  0.0 62.4 jit_solution(60479724590936850)
XLA Ops:
  0.6 1.3 %prepare.1 = (f32[16,128]{1,0:T(8,128)S(1)}, bf16[2048,256]{1,0:T(8,128)(2,1)S(1)}, f32[16,128]{1,0:T(8,128)S(1)}, f32[8,128]{1,0:T(8,128)S(1)}, f32[8,128]{1,0:T(8,128)S(1)}) custom-call(f32[2,128]{1,0:T(2,128)} %bitcast.20, s32[64]{0:T(128)} %lengths_hbm, bf16[2048,256]{1,0:T(8,128)(2,1)} %w_ref.2, f32[16,128]{1,0:T(8,128)} %bitcast.19), custom_call_target="tpu_custom_call" | custom-call | tf_op jit(solution)/shard_map/prepare/pallas_call | solution.py:337
  1.9 13.1 %all_to_all.20 = f32[8,2,128]{2,1,0:T(2,128)S(1)} all-to-all(f32[8,2,128]{2,1,0:T(2,128)S(1)} %bitcast.17), channel_id=1, replica_groups={{4,5,6,7,0,1,2,3},{12,13,14,15,8,9,10,11},{20,21,22,23,16,17,18,19},{28..., dimensions={0} | all-to-all | bytes 16384 | tf_op jit(solution)/shard_map/all_to_all | solution.py:317
  15.0 1.1 %query.1.query_hbm = bf16[256,128]{1,0:T(8,128)(2,1)} custom-call(f32[16,128]{1,0:T(8,128)S(1)} %bitcast.14, f32[16,128]{1,0:T(8,128)S(1)} %get-tuple-element.21.gain_ref, bf16[2048,256]{1,0:T(8,128)(2,1)S(1)} %get-tuple-element.24.w_ref, f32[8,128]{1,0:T(8,128)S(1)} %get-tuple-element.22.cos_ref, f32[8,128]{1,0:T(8,128)S(1)} %get-tuple-element.23.sin_ref), custom_call_target="tpu_custom_call" | custom-call | tf_op jit(solution)/shard_map/query/pallas_call | solution.py:357
  16.1 13.7 %all-to-all-start.1 = ((bf16[64,4,128]{2,1,0:T(4,128)(2,1)}), bf16[64,4,128]{2,1,0:T(4,128)(2,1)S(1)}, u32[]{:S(2)}, u32[]{:S(2)}) async-start(bf16[64,4,128]{2,1,0:T(4,128)(2,1)} %bitcast.5), calls=%async_computation.1 | async-start | bytes 131072 | tf_op jit(solution)/shard_map/all_to_all | solution.py:317
  29.8 1.8 %keyval.1 = (bf16[1,128]{1,0:T(2,128)(2,1)}, f32[8,128]{1,0:T(8,128)S(1)}) custom-call(f32[16,128]{1,0:T(8,128)S(1)} %bitcast.15, f32[16,128]{1,0:T(8,128)S(1)} %get-tuple-element.21.gain_ref, f32[8,128]{1,0:T(8,128)S(1)} %get-tuple-element.22.cos_ref, f32[8,128]{1,0:T(8,128)S(1)} %get-tuple-element.23.sin_ref, bf16[256,128]{1,0:T(8,128)(2,1)} %query.1.query_hbm, ...), custom_call_target="tpu_custom_call" | custom-call | tf_op jit(solution)/shard_map/keyval/pallas_call | solution.py:383
  31.6 1.9 %slot_table.1 = (s32[96,128]{1,0:T(8,128)S(1)}, bf16[96,128,128]{2,1,0:T(8,128)(2,1)S(1)}) custom-call(s32[64]{0:T(128)} %lengths_hbm, s32[64,128]{1,0:T(8,128)} %slot_hbm, bf16[96,128,128]{2,1,0:T(8,128)(2,1)} %bitcast.18), custom_call_target="tpu_custom_call" | custom-call | tf_op jit(solution)/shard_map/slot_table/pallas_call | solution.py:367
  33.6 0.0 copy-start.1
  33.6 0.1 slice_reduce_fusion.tab_ref
  33.7 0.0 all-to-all-done.1
  33.7 0.0 copy-start
  33.7 2.4 %attend.1 = f32[256,128]{1,0:T(8,128)S(1)} custom-call(s32[96]{0:T(128)S(1)} %slice_reduce_fusion.tab_ref, bf16[256,128]{1,0:T(8,128)(2,1)S(1)} %bitcast.13, bf16[96,128,128]{2,1,0:T(8,128)(2,1)S(1)} %get-tuple-element.27.kv_ref), custom_call_target="tpu_custom_call" | custom-call | tf_op jit(solution)/shard_map/attend/pallas_call | solution.py:397
  36.1 15.8 %all_to_all.21 = f32[64,4,128]{2,1,0:T(4,128)S(1)} all-to-all(f32[64,4,128]{2,1,0:T(4,128)S(1)} %bitcast.11), channel_id=1, replica_groups={{352,360,368,376,384,392,400,408,416,424,432,440,448,456,464,472,480,48..., dimensions={0} | all-to-all | bytes 262144 | tf_op jit(solution)/shard_map/all_to_all | solution.py:317
  51.9 0.0 copy-done
  51.9 0.5 combine.1
  52.4 9.4 %all_to_all.22 = f32[8,2,128]{2,1,0:T(2,128)S(1)} all-to-all(f32[8,2,128]{2,1,0:T(2,128)S(1)} %bitcast.16), channel_id=1, replica_groups={{4,5,6,7,0,1,2,3},{12,13,14,15,8,9,10,11},{20,21,22,23,16,17,18,19},{28..., dimensions={0} | all-to-all | bytes 16384 | tf_op jit(solution)/shard_map/all_to_all | solution.py:317
  61.8 0.0 copy-done.1
  61.8 0.6 add.3
  (2 shorter events, 0.0 us)
Async XLA Ops:
  16.1 17.6 %all-to-all-start.1 = ((bf16[64,4,128]{2,1,0:T(4,128)(2,1)}), bf16[64,4,128]{2,1,0:T(4,128)(2,1)S(1)}, u32[]{:S(2)}, u32[]{:S(2)}) async-start(bf16[64,4,128]{2,1,0:T(4,128)(2,1)} %bitcast.5), calls=%async_computation.1 | async-start | bytes 131072 | tf_op jit(solution)/shard_map/all_to_all | solution.py:317
  33.6 28.2 %copy-start.1 = (f32[1,256]{1,0:T(1,128)S(1)}, f32[1,256]{1,0:T(1,128)}, u32[]{:S(2)}) copy-start(f32[1,256]{1,0:T(1,128)} %param.8) | copy-start | bytes 3076
  33.7 18.2 %copy-start = (bf16[256,2048]{1,0:T(8,128)(2,1)S(1)}, bf16[256,2048]{1,0:T(8,128)(2,1)}, u32[]{:S(2)}) copy-start(bf16[256,2048]{1,0:T(8,128)(2,1)} %w_ref.3) | copy-start | bytes 3145732

commit v9 on v8

--- a/solution.py
+++ b/solution.py
@@ -22,7 +22,7 @@
 
 GROUP = 4
 
-FIRST = 44
+FIRST = 36
 FIRST_SHARD = 4
 
 

time: 62.7 us -> 62.7 us (level)
  blocking collectives: 38.3 us -> 37.3 us
  starting transfers between devices: 13.7 us -> 14.6 us
    all_to_all x3, blocking collectives: 38.3 us -> 37.3 us  [exchange(): lax.all_to_all(x, axis, split_axis=0, concat_axis=0, tiled=True, axis_ind...]
    all_to_all x1, starting transfers between devices: 13.7 us -> 14.6 us  [exchange(): lax.all_to_all(x, axis, split_axis=0, concat_axis=0, tiled=True, axis_ind...]
where the time goes in v9:
time: 62.7 us; the launch traced here: 62.4 us
  blocking collectives  37.3 us (59%)
  starting transfers between devices  14.6 us (23%)
  Pallas kernels  9.02 us (14%)
  between operations  0.71 us (1%)
    all_to_all x3, blocking collectives, exchange(): lax.all_to_all(x, axis, split_axis=0, concat_axis=0, tiled=True, axis_ind...  37.3 us
    all_to_all x1, starting transfers between devices, exchange(): lax.all_to_all(x, axis, split_axis=0, concat_axis=0, tiled=True, axis_ind...  14.6 us
    pallas_call x1, Pallas kernels, per_device(): call(attend_kernel, 'attend', jax.ShapeDtypeStruct((requests * GROUP, wid...  2.36 us
    pallas_call x1, Pallas kernels, per_device(): call(functools.partial(table_kernel, slots_here, block_len), 'slot_table'...  1.94 us
    pallas_call x1, Pallas kernels, per_device(): call(functools.partial(keyval_kernel, head_dim), 'keyval', (jax.ShapeDtyp...  1.84 us
    pallas_call x1, Pallas kernels, per_device(): call(functools.partial(prepare_kernel, head_dim), 'prepare', (jax.ShapeDt...  1.28 us
  transfers between devices with their start and end apart: 1, of which 0 were waited for; matrix products, arithmetic and copies ran while one was open for 0% of the time, Pallas kernels for 6%

profile of v9, /device:TPU:1, one launch (start us, length us, event | category | flops | bytes accessed | tf_op | source)
XLA Modules:
  0.0 62.4 jit_solution(7093226623258396767)
XLA Ops:
  0.6 1.3 %prepare.1 = (f32[16,128]{1,0:T(8,128)S(1)}, bf16[2048,256]{1,0:T(8,128)(2,1)S(1)}, f32[16,128]{1,0:T(8,128)S(1)}, f32[8,128]{1,0:T(8,128)S(1)}, f32[8,128]{1,0:T(8,128)S(1)}) custom-call(f32[2,128]{1,0:T(2,128)} %bitcast.20, s32[64]{0:T(128)} %lengths_hbm, bf16[2048,256]{1,0:T(8,128)(2,1)} %w_ref.2, f32[16,128]{1,0:T(8,128)} %bitcast.19), custom_call_target="tpu_custom_call" | custom-call | tf_op jit(solution)/shard_map/prepare/pallas_call | solution.py:337
  1.9 13.1 %all_to_all.20 = f32[8,2,128]{2,1,0:T(2,128)S(1)} all-to-all(f32[8,2,128]{2,1,0:T(2,128)S(1)} %bitcast.17), channel_id=1, replica_groups={{4,5,6,7,0,1,2,3},{12,13,14,15,8,9,10,11},{20,21,22,23,16,17,18,19},{28..., dimensions={0} | all-to-all | bytes 16384 | tf_op jit(solution)/shard_map/all_to_all | solution.py:317
  15.0 1.1 %query.1.query_hbm = bf16[256,128]{1,0:T(8,128)(2,1)} custom-call(f32[16,128]{1,0:T(8,128)S(1)} %bitcast.14, f32[16,128]{1,0:T(8,128)S(1)} %get-tuple-element.21.gain_ref, bf16[2048,256]{1,0:T(8,128)(2,1)S(1)} %get-tuple-element.24.w_ref, f32[8,128]{1,0:T(8,128)S(1)} %get-tuple-element.22.cos_ref, f32[8,128]{1,0:T(8,128)S(1)} %get-tuple-element.23.sin_ref), custom_call_target="tpu_custom_call" | custom-call | tf_op jit(solution)/shard_map/query/pallas_call | solution.py:357
  16.1 14.6 %all-to-all-start.1 = ((bf16[64,4,128]{2,1,0:T(4,128)(2,1)}), bf16[64,4,128]{2,1,0:T(4,128)(2,1)S(1)}, u32[]{:S(2)}, u32[]{:S(2)}) async-start(bf16[64,4,128]{2,1,0:T(4,128)(2,1)} %bitcast.5), calls=%async_computation.1 | async-start | bytes 131072 | tf_op jit(solution)/shard_map/all_to_all | solution.py:317
  30.8 1.8 %keyval.1 = (bf16[1,128]{1,0:T(2,128)(2,1)}, f32[8,128]{1,0:T(8,128)S(1)}) custom-call(f32[16,128]{1,0:T(8,128)S(1)} %bitcast.15, f32[16,128]{1,0:T(8,128)S(1)} %get-tuple-element.21.gain_ref, f32[8,128]{1,0:T(8,128)S(1)} %get-tuple-element.22.cos_ref, f32[8,128]{1,0:T(8,128)S(1)} %get-tuple-element.23.sin_ref, bf16[256,128]{1,0:T(8,128)(2,1)} %query.1.query_hbm, ...), custom_call_target="tpu_custom_call" | custom-call | tf_op jit(solution)/shard_map/keyval/pallas_call | solution.py:383
  32.6 1.9 %slot_table.1 = (s32[96,128]{1,0:T(8,128)S(1)}, bf16[96,128,128]{2,1,0:T(8,128)(2,1)S(1)}) custom-call(s32[64]{0:T(128)} %lengths_hbm, s32[64,128]{1,0:T(8,128)} %slot_hbm, bf16[96,128,128]{2,1,0:T(8,128)(2,1)} %bitcast.18), custom_call_target="tpu_custom_call" | custom-call | tf_op jit(solution)/shard_map/slot_table/pallas_call | solution.py:367
  34.6 0.0 copy-start.1
  34.6 0.1 slice_reduce_fusion.tab_ref
  34.7 0.0 all-to-all-done.1
  34.7 0.0 copy-start
  34.7 2.4 %attend.1 = f32[256,128]{1,0:T(8,128)S(1)} custom-call(s32[96]{0:T(128)S(1)} %slice_reduce_fusion.tab_ref, bf16[256,128]{1,0:T(8,128)(2,1)S(1)} %bitcast.13, bf16[96,128,128]{2,1,0:T(8,128)(2,1)S(1)} %get-tuple-element.27.kv_ref), custom_call_target="tpu_custom_call" | custom-call | tf_op jit(solution)/shard_map/attend/pallas_call | solution.py:397
  37.1 14.8 %all_to_all.21 = f32[64,4,128]{2,1,0:T(4,128)S(1)} all-to-all(f32[64,4,128]{2,1,0:T(4,128)S(1)} %bitcast.11), channel_id=1, replica_groups={{288,296,304,312,320,328,336,344,352,360,368,376,384,392,400,408,416,42..., dimensions={0} | all-to-all | bytes 262144 | tf_op jit(solution)/shard_map/all_to_all | solution.py:317
  51.9 0.0 copy-done
  51.9 0.5 combine.1
  52.4 9.4 %all_to_all.22 = f32[8,2,128]{2,1,0:T(2,128)S(1)} all-to-all(f32[8,2,128]{2,1,0:T(2,128)S(1)} %bitcast.16), channel_id=1, replica_groups={{4,5,6,7,0,1,2,3},{12,13,14,15,8,9,10,11},{20,21,22,23,16,17,18,19},{28..., dimensions={0} | all-to-all | bytes 16384 | tf_op jit(solution)/shard_map/all_to_all | solution.py:317
  61.8 0.0 copy-done.1
  61.8 0.6 add.3
  (2 shorter events, 0.0 us)
Async XLA Ops:
  16.1 18.6 %all-to-all-start.1 = ((bf16[64,4,128]{2,1,0:T(4,128)(2,1)}), bf16[64,4,128]{2,1,0:T(4,128)(2,1)S(1)}, u32[]{:S(2)}, u32[]{:S(2)}) async-start(bf16[64,4,128]{2,1,0:T(4,128)(2,1)} %bitcast.5), calls=%async_computation.1 | async-start | bytes 131072 | tf_op jit(solution)/shard_map/all_to_all | solution.py:317
  34.6 27.3 %copy-start.1 = (f32[1,256]{1,0:T(1,128)S(1)}, f32[1,256]{1,0:T(1,128)}, u32[]{:S(2)}) copy-start(f32[1,256]{1,0:T(1,128)} %param.8) | copy-start | bytes 3076
  34.7 17.2 %copy-start = (bf16[256,2048]{1,0:T(8,128)(2,1)S(1)}, bf16[256,2048]{1,0:T(8,128)(2,1)}, u32[]{:S(2)}) copy-start(bf16[256,2048]{1,0:T(8,128)(2,1)} %w_ref.3) | copy-start | bytes 3145732

commit v10 on v9

--- a/solution.py
+++ b/solution.py
@@ -38,13 +38,13 @@
     return lax.broadcasted_iota(jnp.int32, shape, len(shape) - 2)
 
 
-def call(body, name, out_shape, in_specs, scratch=(), limit=4 << 20):
+def call(body, name, out_shape, in_specs, scratch=(), limit=4 << 20, out_specs=None):
     many = isinstance(out_shape, tuple)
     return pl.pallas_call(
         body,
         out_shape=out_shape,
         in_specs=in_specs,
-        out_specs=(VMEM,) * len(out_shape) if many else VMEM,
+        out_specs=out_specs or ((VMEM,) * len(out_shape) if many else VMEM),
         scratch_shapes=list(scratch),
         compiler_params=pltpu.CompilerParams(vmem_limit_bytes=limit),
         name=name,
@@ -119,13 +119,10 @@
     return copies
 
 
-def prepare_kernel(head_dim, x_ref, lengths_ref, w_ref, gain_ref, *rest):
-    spread_ref, held_w_ref, held_gain_ref, cos_ref, sin_ref, near_x, near_lengths, sems = rest
-    copies = fetch(
-        (x_ref, lengths_ref, w_ref, gain_ref),
-        (near_x, near_lengths, held_w_ref, held_gain_ref),
-        sems,
-    )
+def prepare_kernel(head_dim, x_ref, lengths_ref, *rest):
+    sources, (spread_ref, *targets) = rest[:3], rest[3:7]
+    cos_ref, sin_ref, near_x, near_lengths, sems = rest[7:]
+    copies = fetch((x_ref, lengths_ref, *sources), (near_x, near_lengths, *targets), sems)
     copies[1].wait()
     position = near_lengths[lax.axis_index("pool")]
     cos_ref[...], sin_ref[...] = rotation(position, head_dim, 2 * head_dim)
@@ -133,41 +130,36 @@
     size = near_x.shape[0]
     for i in range(spread_ref.shape[0] // size):
         spread_ref[pl.ds(i * size, size), :] = near_x[...]
-    copies[2].wait()
-    copies[3].wait()
-
-
-def query_kernel(head_dim, rows_ref, gain_ref, w_ref, cos_ref, sin_ref, out_ref):
+    for copy in copies[2:]:
+        copy.wait()
+
+
+def query_kernel(head_dim, rows_ref, gain_ref, w_ref, w_keyval_ref, cos_ref, sin_ref, *rest):
+    out_ref, kv_ref, own_ref, tiles_ref, sem = rest
     wide = 2 * head_dim
     cosine, sine = cos_ref[...], sin_ref[...]
-    query = project(normalise(rows_ref, gain_ref), w_ref)
+    normed = normalise(rows_ref, gain_ref)
+    query = project(normed, w_ref)
     row = subs((8, wide)) % GROUP
     tile = jnp.zeros((8, wide), F32)
     for c in range(GROUP // 2):
         part = rope(query[:, c * wide : (c + 1) * wide], cosine, sine, head_dim // 2)
         tile = jnp.where(row == 2 * c, part, tile)
         tile = jnp.where(row == 2 * c + 1, pltpu.roll(part, head_dim, 1), tile)
-    tile = tile.astype(BF16).astype(F32) * SCORE_SCALE
-    tile = jnp.where(lanes(tile.shape) < head_dim, tile, 0.0).astype(BF16)
-    for v in range(out_ref.shape[0] // 8):
-        out_ref[pl.ds(8 * v, 8), :] = tile
-
-
-def keyval_kernel(
-    head_dim, rows_ref, gain_ref, cos_ref, sin_ref, query_hbm, w_hbm, kv_ref, own_ref, w_ref, query_ref, sems
-):
-    copies = fetch((w_hbm, query_hbm.at[pl.ds(0, query_ref.shape[0])]), (w_ref, query_ref), sems)
-    normed = normalise(rows_ref, gain_ref)
-    for copy in copies:
-        copy.wait()
-    keyval = project(normed, w_ref)
-    is_key = lanes(keyval.shape) < head_dim
-    turned = rope(keyval, cos_ref[...], sin_ref[...], head_dim // 2)
+    is_key = lanes(tile.shape) < head_dim
+    tile = jnp.where(is_key, tile.astype(BF16).astype(F32) * SCORE_SCALE, 0.0)
+    for v in range(tiles_ref.shape[0] // 8):
+        tiles_ref[pl.ds(8 * v, 8), :] = tile.astype(BF16)
+    copy = pltpu.make_async_copy(tiles_ref, out_ref, sem)
+    copy.start()
+    keyval = project(normed, w_keyval_ref)
+    turned = rope(keyval, cosine, sine, head_dim // 2)
     both = jnp.where(is_key, turned, keyval).astype(BF16)
     kv_ref[...] = both[:1]
     both = both.astype(F32)
-    score = jnp.sum(query_ref[:8, :].astype(F32) * both, axis=1, keepdims=True)
+    score = jnp.sum(tile * both, axis=1, keepdims=True)
     own_ref[...] = jnp.where(is_key, score, both)
+    copy.wait()
 
 
 def table_kernel(
@@ -205,7 +197,7 @@
 
 
 def attend_kernel(
-    tab_ref, query_ref, kv_ref, out_ref, q_s, score_s, max_s, sum_s, acc_s
+    tab_ref, query_ref, kv_ref, out_ref, q_s, score_s, max_s, acc_s
 ):
     slots_here, block_len, wide = kv_ref.shape
     requests = query_ref.shape[0] // GROUP
@@ -218,7 +210,6 @@
         q_s[2 * v] = jnp.where(low, tile, other)
         q_s[2 * v + 1] = jnp.where(low, other, tile)
     max_s[...] = jnp.full_like(max_s, MASKED)
-    sum_s[...] = jnp.zeros_like(sum_s)
     acc_s[...] = jnp.zeros_like(acc_s)
 
     def pair(p):
@@ -237,12 +228,9 @@
         scores = jnp.where(live, scores, MASKED)
         score_s[p] = scores
         top = jnp.broadcast_to(jnp.max(scores, axis=1, keepdims=True), scores.shape)
-        max_s[ra] = jnp.maximum(max_s[ra], jnp.where(low, top, MASKED))
-        max_s[rb] = jnp.maximum(max_s[rb], jnp.where(low, MASKED, top))
-
-    for r in range(requests):
-        top = max_s[r]
-        max_s[r] = jnp.maximum(top, pltpu.roll(top, GROUP, 0))
+        other = pltpu.roll(top, GROUP, 0)
+        max_s[ra] = jnp.maximum(max_s[ra], jnp.where(low, top, other))
+        max_s[rb] = jnp.maximum(max_s[rb], jnp.where(low, other, top))
 
     for p in range(slots_here // 2):
         ra, rb, live, values = pair(p)
@@ -252,21 +240,16 @@
             [jnp.where(low, weight, 0.0), jnp.where(low, 0.0, weight)], axis=1
         ).astype(BF16)
         out = jnp.dot(both, values, preferred_element_type=F32)
-        total = jnp.broadcast_to(jnp.sum(weight, axis=1, keepdims=True), out.shape)
-        acc_s[ra] = acc_s[ra] + jnp.where(low, out, 0.0)
-        acc_s[rb] = acc_s[rb] + jnp.where(low, 0.0, out)
-        sum_s[ra] = sum_s[ra] + jnp.where(low, total, 0.0)
-        sum_s[rb] = sum_s[rb] + jnp.where(low, 0.0, total)
+        total = jnp.sum(weight, axis=1, keepdims=True)
+        out = jnp.where(lane < wide // 2, total, out)
+        other = pltpu.roll(out, GROUP, 0)
+        acc_s[ra] = acc_s[ra] + jnp.where(low, out, other)
+        acc_s[rb] = acc_s[rb] + jnp.where(low, other, out)
 
     for v in range(requests // 2):
-        tiles = []
-        for r in (2 * v, 2 * v + 1):
-            out = acc_s[r] + pltpu.roll(acc_s[r], GROUP, 0)
-            total = sum_s[r] + pltpu.roll(sum_s[r], GROUP, 0)
-            tiles.append(
-                jnp.where(lane < wide // 4, max_s[r], jnp.where(lane < wide // 2, total, out))
-            )
-        out_ref[pl.ds(8 * v, 8), :] = jnp.where(low, tiles[0], tiles[1])
+        top = jnp.where(low, max_s[2 * v], max_s[2 * v + 1])
+        out = jnp.where(low, acc_s[2 * v], acc_s[2 * v + 1])
+        out_ref[pl.ds(8 * v, 8), :] = jnp.where(lane < wide // 4, top, out)
 
 
 def combine_kernel(got_ref, own_ref, w_ref, out_ref):
@@ -334,36 +317,40 @@
         far(x) for x in (w_query, w_keyval, lengths, block_slot)
     )
     turn = jax.ShapeDtypeStruct((8, wide), F32)
-    spread_rows, held_query, held_gain, cosine, sine = call(
+    spread_rows, held_query, held_keyval, held_gain, cosine, sine = call(
         functools.partial(prepare_kernel, head_dim),
         "prepare",
         (
             jax.ShapeDtypeStruct((shards * lines, wide), F32),
             jax.ShapeDtypeStruct(w_query.shape, BF16),
+            jax.ShapeDtypeStruct(w_keyval.shape, BF16),
             jax.ShapeDtypeStruct(gain.shape, F32),
             turn,
             turn,
         ),
-        [HBM] * 4,
+        [HBM] * 5,
         [
             pltpu.VMEM((lines, wide), F32),
             pltpu.SMEM(lengths.shape, jnp.int32),
-            pltpu.SemaphoreType.DMA((4,)),
+            pltpu.SemaphoreType.DMA((5,)),
         ],
-    )(line, lengths, w_query, gain)
+    )(line, lengths, w_query, w_keyval, gain)
 
     rows = exchange(spread_rows, "mp", shards, FIRST_SHARD)
 
-    query = call(
+    tiles = jax.ShapeDtypeStruct((requests * GROUP, wide), BF16)
+    query, new_kv, own = call(
         functools.partial(query_kernel, head_dim),
         "query",
-        jax.ShapeDtypeStruct((requests * GROUP, wide), BF16),
-        [VMEM] * 5,
-    )(rows, held_gain, held_query, cosine, sine)
+        (tiles, jax.ShapeDtypeStruct((1, wide), BF16), turn),
+        [VMEM] * 6,
+        [pltpu.VMEM(tiles.shape, BF16), pltpu.SemaphoreType.DMA],
+        out_specs=(HBM, VMEM, VMEM),
+    )(rows, held_gain, held_query, held_keyval, cosine, sine)
 
     queries = exchange(query, "pool", pools, FIRST)
 
-    lengths, block_slot, rows = lax.optimization_barrier((lengths, block_slot, rows))
+    lengths, block_slot, own = lax.optimization_barrier((lengths, block_slot, own))
     table, held_cache = call(
         functools.partial(table_kernel, slots_here, block_len),
         "slot_table",
@@ -380,19 +367,6 @@
     )(far(lengths), far(block_slot), cache)
     table = table[:, 0]
 
-    new_kv, own = call(
-        functools.partial(keyval_kernel, head_dim),
-        "keyval",
-        (jax.ShapeDtypeStruct((1, wide), BF16), turn),
-        [VMEM] * 4 + [HBM] * 2,
-        [
-            pltpu.VMEM(w_keyval.shape, BF16),
-            pltpu.VMEM((16, wide), BF16),
-            pltpu.SemaphoreType.DMA((2,)),
-        ],
-    )(rows, held_gain, cosine, sine, far(query), w_keyval)
-    table, own = lax.optimization_barrier((table, own))
-
     per_request = pltpu.VMEM((requests, 8, wide), F32)
     partial = call(
         attend_kernel,
@@ -402,7 +376,6 @@
         [
             per_request,
             pltpu.VMEM((slots_here // 2, 8, block_len), F32),
-            per_request,
             per_request,
             per_request,
         ],

time: 62.7 us -> 62.6 us (level)
  Pallas kernels: 9.02 us -> 7.8 us
  blocking collectives: 37.3 us -> 38.2 us
    pallas_call x2 -> x1, Pallas kernels: 2.92 us -> 1.67 us  [per_device(): call(functools.partial(query_kernel, head_dim), 'query', (tiles, jax.Shap...]
    all_to_all x3, blocking collectives: 37.3 us -> 38.2 us  [exchange(): lax.all_to_all(x, axis, split_axis=0, concat_axis=0, tiled=True, axis_ind...]
  transfers between devices with their start and end apart: 1 -> 1, of which waited for: 0 -> 1; matrix products, arithmetic and copies ran while one was open for 0% -> 0% of each run, Pallas kernels for 6% -> 3%
where the time goes in v10:
time: 62.6 us; the launch traced here: 62.3 us
  blocking collectives  38.2 us (61%)
  starting transfers between devices  14.7 us (23%)
  Pallas kernels  7.8 us (12%)
  between operations  0.69 us (1%)
    all_to_all x3, blocking collectives, exchange(): lax.all_to_all(x, axis, split_axis=0, concat_axis=0, tiled=True, axis_ind...  38.2 us
    all_to_all x1, starting transfers between devices, exchange(): lax.all_to_all(x, axis, split_axis=0, concat_axis=0, tiled=True, axis_ind...  14.7 us
    pallas_call x1, Pallas kernels, per_device(): call(attend_kernel, 'attend', jax.ShapeDtypeStruct((requests * GROUP, wid...  2.26 us
    pallas_call x1, Pallas kernels, per_device(): call(functools.partial(table_kernel, slots_here, block_len), 'slot_table'...  1.94 us
    pallas_call x1, Pallas kernels, per_device(): call(functools.partial(query_kernel, head_dim), 'query', (tiles, jax.Shap...  1.67 us
    pallas_call x1, Pallas kernels, per_device(): call(functools.partial(prepare_kernel, head_dim), 'prepare', (jax.ShapeDt...  1.42 us
  transfers between devices with their start and end apart: 1, of which 1 were waited for; matrix products, arithmetic and copies ran while one was open for 0% of the time, Pallas kernels for 3%

profile of v10, /device:TPU:1, one launch (start us, length us, event | category | flops | bytes accessed | tf_op | source)
XLA Modules:
  0.0 62.3 jit_solution(15700326286876561308)
XLA Ops:
  0.6 1.4 %prepare.1 = (f32[16,128]{1,0:T(8,128)S(1)}, bf16[2048,256]{1,0:T(8,128)(2,1)S(1)}, bf16[2048,128]{1,0:T(8,128)(2,1)S(1)}, f32[16,128]{1,0:T(8,128)S(1)}, f32[8,128]{1,0:T(8,128)S(1)}, /*index=5*/f32[8,128]{1,0:T(8,128)S(1)}) custom-call(f32[2,128]{1,0:T(2,128)} %bitcast.19, s32[64]{0:T(128)} %lengths_hbm, bf16[2048,256]{1,0:T(8,128)(2,1)} %rest_0_.1, ...), custom_call_target="tpu_custom_call" | custom-call | tf_op jit(solution)/shard_map/prepare/pallas_call | solution.py:320
  2.1 13.1 %all_to_all.20 = f32[8,2,128]{2,1,0:T(2,128)S(1)} all-to-all(f32[8,2,128]{2,1,0:T(2,128)S(1)} %bitcast.16), channel_id=1, replica_groups={{4,5,6,7,0,1,2,3},{12,13,14,15,8,9,10,11},{20,21,22,23,16,17,18,19},{28..., dimensions={0} | all-to-all | bytes 16384 | tf_op jit(solution)/shard_map/all_to_all | solution.py:300
  15.2 1.7 %query.1 = (bf16[256,128]{1,0:T(8,128)(2,1)}, bf16[1,128]{1,0:T(2,128)(2,1)}, f32[8,128]{1,0:T(8,128)S(1)}) custom-call(f32[16,128]{1,0:T(8,128)S(1)} %bitcast.14, f32[16,128]{1,0:T(8,128)S(1)} %get-tuple-element.17.gain_ref, bf16[2048,256]{1,0:T(8,128)(2,1)S(1)} %get-tuple-element.18.w_ref, bf16[2048,128]{1,0:T(8,128)(2,1)S(1)} %get-tuple-element.19.w_keyval_ref, ...), custom_call_target="tpu_custom_call" | custom-call | tf_op jit(solution)/shard_map/query/pallas_call | solution.py:342
  16.8 14.7 %all-to-all-start.1 = ((bf16[64,4,128]{2,1,0:T(4,128)(2,1)}), bf16[64,4,128]{2,1,0:T(4,128)(2,1)S(1)}, u32[]{:S(2)}, u32[]{:S(2)}) async-start(bf16[64,4,128]{2,1,0:T(4,128)(2,1)} %bitcast.5), calls=%async_computation.1 | async-start | bytes 131072 | tf_op jit(solution)/shard_map/all_to_all | solution.py:300
  31.5 1.9 %slot_table.1 = (s32[96,128]{1,0:T(8,128)S(1)}, bf16[96,128,128]{2,1,0:T(8,128)(2,1)S(1)}) custom-call(s32[64]{0:T(128)} %lengths_hbm, s32[64,128]{1,0:T(8,128)} %slot_hbm, bf16[96,128,128]{2,1,0:T(8,128)(2,1)} %bitcast.17), custom_call_target="tpu_custom_call" | custom-call | tf_op jit(solution)/shard_map/slot_table/pallas_call | solution.py:354
  33.4 0.0 copy-start.1
  33.5 0.1 slice_reduce_fusion.tab_ref
  33.6 0.2 all-to-all-done.1
  33.8 0.0 copy-start
  33.8 2.3 %attend.1 = f32[256,128]{1,0:T(8,128)S(1)} custom-call(s32[96]{0:T(128)S(1)} %slice_reduce_fusion.tab_ref, bf16[256,128]{1,0:T(8,128)(2,1)S(1)} %bitcast.13, bf16[96,128,128]{2,1,0:T(8,128)(2,1)S(1)} %get-tuple-element.27.kv_ref), custom_call_target="tpu_custom_call" | custom-call | tf_op jit(solution)/shard_map/attend/pallas_call | solution.py:371
  36.0 15.2 %all_to_all.21 = f32[64,4,128]{2,1,0:T(4,128)S(1)} all-to-all(f32[64,4,128]{2,1,0:T(4,128)S(1)} %bitcast.11), channel_id=1, replica_groups={{288,296,304,312,320,328,336,344,352,360,368,376,384,392,400,408,416,42..., dimensions={0} | all-to-all | bytes 262144 | tf_op jit(solution)/shard_map/all_to_all | solution.py:300
  51.2 0.0 copy-done
  51.2 0.5 combine.1
  51.7 10.0 %all_to_all.22 = f32[8,2,128]{2,1,0:T(2,128)S(1)} all-to-all(f32[8,2,128]{2,1,0:T(2,128)S(1)} %bitcast.15), channel_id=1, replica_groups={{4,5,6,7,0,1,2,3},{12,13,14,15,8,9,10,11},{20,21,22,23,16,17,18,19},{28..., dimensions={0} | all-to-all | bytes 16384 | tf_op jit(solution)/shard_map/all_to_all | solution.py:300
  61.7 0.0 copy-done.1
  61.7 0.6 add.3
  (2 shorter events, 0.0 us)
Async XLA Ops:
  16.8 16.9 %all-to-all-start.1 = ((bf16[64,4,128]{2,1,0:T(4,128)(2,1)}), bf16[64,4,128]{2,1,0:T(4,128)(2,1)S(1)}, u32[]{:S(2)}, u32[]{:S(2)}) async-start(bf16[64,4,128]{2,1,0:T(4,128)(2,1)} %bitcast.5), calls=%async_computation.1 | async-start | bytes 131072 | tf_op jit(solution)/shard_map/all_to_all | solution.py:300
  33.4 28.3 %copy-start.1 = (f32[1,256]{1,0:T(1,128)S(1)}, f32[1,256]{1,0:T(1,128)}, u32[]{:S(2)}) copy-start(f32[1,256]{1,0:T(1,128)} %param.8) | copy-start | bytes 3076
  33.8 17.4 %copy-start = (bf16[256,2048]{1,0:T(8,128)(2,1)S(1)}, bf16[256,2048]{1,0:T(8,128)(2,1)}, u32[]{:S(2)}) copy-start(bf16[256,2048]{1,0:T(8,128)(2,1)} %w_ref.1) | copy-start | bytes 3145732

commit v11 on v10

--- a/solution.py
+++ b/solution.py
@@ -21,6 +21,8 @@
 HBM = pl.BlockSpec(memory_space=pltpu.HBM)
 
 GROUP = 4
+
+SPLIT = 4
 
 FIRST = 36
 FIRST_SHARD = 4
@@ -113,25 +115,42 @@
 
 
 def fetch(sources, targets, sems):
-    copies = [pltpu.make_async_copy(s, t, sems.at[i]) for i, (s, t) in enumerate(zip(sources, targets))]
-    for copy in copies:
-        copy.start()
-    return copies
+    lists = []
+    for i, (source, target) in enumerate(zip(sources, targets)):
+        parts = SPLIT if source.size >= 1 << 18 else 1
+        size = source.shape[0] // parts
+        copies = []
+        for j in range(parts):
+            rows = pl.ds(j * size, size)
+            copy = pltpu.make_async_copy(
+                source.at[rows] if parts > 1 else source,
+                target.at[rows] if parts > 1 else target,
+                sems.at[i, j],
+            )
+            copy.start()
+            copies.append(copy)
+        lists.append(copies)
+    return lists
+
+
+def wait(lists):
+    for copies in lists:
+        for copy in copies:
+            copy.wait()
 
 
 def prepare_kernel(head_dim, x_ref, lengths_ref, *rest):
     sources, (spread_ref, *targets) = rest[:3], rest[3:7]
     cos_ref, sin_ref, near_x, near_lengths, sems = rest[7:]
     copies = fetch((x_ref, lengths_ref, *sources), (near_x, near_lengths, *targets), sems)
-    copies[1].wait()
+    wait(copies[1:2])
     position = near_lengths[lax.axis_index("pool")]
     cos_ref[...], sin_ref[...] = rotation(position, head_dim, 2 * head_dim)
-    copies[0].wait()
+    wait(copies[:1])
     size = near_x.shape[0]
     for i in range(spread_ref.shape[0] // size):
         spread_ref[pl.ds(i * size, size), :] = near_x[...]
-    for copy in copies[2:]:
-        copy.wait()
+    wait(copies[2:])
 
 
 def query_kernel(head_dim, rows_ref, gain_ref, w_ref, w_keyval_ref, cos_ref, sin_ref, *rest):
@@ -155,8 +174,8 @@
     keyval = project(normed, w_keyval_ref)
     turned = rope(keyval, cosine, sine, head_dim // 2)
     both = jnp.where(is_key, turned, keyval).astype(BF16)
-    kv_ref[...] = both[:1]
     both = both.astype(F32)
+    kv_ref[...] = both
     score = jnp.sum(tile * both, axis=1, keepdims=True)
     own_ref[...] = jnp.where(is_key, score, both)
     copy.wait()
@@ -166,8 +185,7 @@
     slots_here, block_len, lengths_hbm, slot_hbm, cache_ref, out_ref, held_ref, lengths_ref, slot_ref, sems
 ):
     copies = fetch((lengths_hbm, slot_hbm, cache_ref), (lengths_ref, slot_ref, held_ref), sems)
-    copies[0].wait()
-    copies[1].wait()
+    wait(copies[:2])
     requests, blocks = slot_ref.shape
     base = lax.axis_index("pool") * slots_here
     sub = subs((8, blocks))
@@ -193,7 +211,7 @@
         out_ref[pl.ds(8 * tile, 8), :] = jnp.broadcast_to(
             jnp.max(picked.astype(F32), axis=1, keepdims=True), (8, blocks)
         ).astype(jnp.int32)
-    copies[2].wait()
+    wait(copies[2:])
 
 
 def attend_kernel(
@@ -332,17 +350,17 @@
         [
             pltpu.VMEM((lines, wide), F32),
             pltpu.SMEM(lengths.shape, jnp.int32),
-            pltpu.SemaphoreType.DMA((5,)),
+            pltpu.SemaphoreType.DMA((5, SPLIT)),
         ],
     )(line, lengths, w_query, w_keyval, gain)
 
     rows = exchange(spread_rows, "mp", shards, FIRST_SHARD)
 
     tiles = jax.ShapeDtypeStruct((requests * GROUP, wide), BF16)
-    query, new_kv, own = call(
+    query, new_tile, own = call(
         functools.partial(query_kernel, head_dim),
         "query",
-        (tiles, jax.ShapeDtypeStruct((1, wide), BF16), turn),
+        (tiles, turn, turn),
         [VMEM] * 6,
         [pltpu.VMEM(tiles.shape, BF16), pltpu.SemaphoreType.DMA],
         out_specs=(HBM, VMEM, VMEM),
@@ -350,7 +368,10 @@
 
     queries = exchange(query, "pool", pools, FIRST)
 
-    lengths, block_slot, own = lax.optimization_barrier((lengths, block_slot, own))
+    lengths, block_slot, own, new_tile = lax.optimization_barrier(
+        (lengths, block_slot, own, new_tile)
+    )
+    new_kv = new_tile[:1].astype(BF16)
     table, held_cache = call(
         functools.partial(table_kernel, slots_here, block_len),
         "slot_table",
@@ -362,10 +383,10 @@
         [
             pltpu.SMEM(lengths.shape, jnp.int32),
             pltpu.VMEM(block_slot.shape, jnp.int32),
-            pltpu.SemaphoreType.DMA((3,)),
+            pltpu.SemaphoreType.DMA((3, SPLIT)),
         ],
     )(far(lengths), far(block_slot), cache)
-    table = table[:, 0]
+    table, new_kv = lax.optimization_barrier((table[:, 0], new_kv))
 
     per_request = pltpu.VMEM((requests, 8, wide), F32)
     partial = call(

time: 62.6 us -> 62.2 us (level)
  transfers between devices with their start and end apart: 1 -> 1, of which waited for: 1 -> 0; matrix products, arithmetic and copies ran while one was open for 0% -> 1% of each run, Pallas kernels for 3% -> 3%
where the time goes in v11:
time: 62.2 us; the launch traced here: 61.9 us
  blocking collectives  37.8 us (61%)
  starting transfers between devices  14.7 us (24%)
  Pallas kernels  7.46 us (12%)
  between operations  0.72 us (1%)
  local copies, waits for them, and re-layouts  0.63 us (1%)
    all_to_all x3, blocking collectives, exchange(): lax.all_to_all(x, axis, split_axis=0, concat_axis=0, tiled=True, axis_ind...  37.8 us
    all_to_all x1, starting transfers between devices, exchange(): lax.all_to_all(x, axis, split_axis=0, concat_axis=0, tiled=True, axis_ind...  14.7 us
    pallas_call x1, Pallas kernels, per_device(): call(attend_kernel, 'attend', jax.ShapeDtypeStruct((requests * GROUP, wid...  2.29 us
    pallas_call x1, Pallas kernels, per_device(): call(functools.partial(table_kernel, slots_here, block_len), 'slot_table'...  1.97 us
    pallas_call x1, Pallas kernels, per_device(): call(functools.partial(prepare_kernel, head_dim), 'prepare', (jax.ShapeDt...  1.54 us
  transfers between devices with their start and end apart: 1, of which 0 were waited for; matrix products, arithmetic and copies ran while one was open for 1% of the time, Pallas kernels for 3%

profile of v11, /device:TPU:1, one launch (start us, length us, event | category | flops | bytes accessed | tf_op | source)
XLA Modules:
  0.0 61.9 jit_solution(12250707631010583051)
XLA Ops:
  0.6 1.5 %prepare.1 = (f32[16,128]{1,0:T(8,128)S(1)}, bf16[2048,256]{1,0:T(8,128)(2,1)S(1)}, bf16[2048,128]{1,0:T(8,128)(2,1)S(1)}, f32[16,128]{1,0:T(8,128)S(1)}, f32[8,128]{1,0:T(8,128)S(1)}, /*index=5*/f32[8,128]{1,0:T(8,128)S(1)}) custom-call(f32[2,128]{1,0:T(2,128)} %bitcast.19, s32[64]{0:T(128)} %lengths_hbm, bf16[2048,256]{1,0:T(8,128)(2,1)} %rest_0_.1, ...), custom_call_target="tpu_custom_call" | custom-call | tf_op jit(solution)/shard_map/prepare/pallas_call | solution.py:338
  2.2 13.1 %all_to_all.20 = f32[8,2,128]{2,1,0:T(2,128)S(1)} all-to-all(f32[8,2,128]{2,1,0:T(2,128)S(1)} %bitcast.16), channel_id=1, replica_groups={{4,5,6,7,0,1,2,3},{12,13,14,15,8,9,10,11},{20,21,22,23,16,17,18,19},{28..., dimensions={0} | all-to-all | bytes 16384 | tf_op jit(solution)/shard_map/all_to_all | solution.py:318
  15.3 1.2 %query.1 = (bf16[256,128]{1,0:T(8,128)(2,1)}, f32[8,128]{1,0:T(8,128)S(1)}, f32[8,128]{1,0:T(8,128)S(1)}) custom-call(f32[16,128]{1,0:T(8,128)S(1)} %bitcast.14, f32[16,128]{1,0:T(8,128)S(1)} %get-tuple-element.20.gain_ref, bf16[2048,256]{1,0:T(8,128)(2,1)S(1)} %get-tuple-element.21.w_ref, bf16[2048,128]{1,0:T(8,128)(2,1)S(1)} %get-tuple-element.22.w_keyval_ref, ...), custom_call_target="tpu_custom_call" | custom-call | tf_op jit(solution)/shard_map/query/pallas_call | solution.py:360
  16.4 14.7 %all-to-all-start.1 = ((bf16[64,4,128]{2,1,0:T(4,128)(2,1)}), bf16[64,4,128]{2,1,0:T(4,128)(2,1)S(1)}, u32[]{:S(2)}, u32[]{:S(2)}) async-start(bf16[64,4,128]{2,1,0:T(4,128)(2,1)} %bitcast.5), calls=%async_computation.1 | async-start | bytes 131072 | tf_op jit(solution)/shard_map/all_to_all | solution.py:318
  31.1 0.5 slice.8
  31.6 2.0 %slot_table.1 = (s32[96,128]{1,0:T(8,128)S(1)}, bf16[96,128,128]{2,1,0:T(8,128)(2,1)S(1)}) custom-call(s32[64]{0:T(128)} %lengths_hbm, s32[64,128]{1,0:T(8,128)} %slot_hbm, bf16[96,128,128]{2,1,0:T(8,128)(2,1)} %bitcast.17), custom_call_target="tpu_custom_call" | custom-call | tf_op jit(solution)/shard_map/slot_table/pallas_call | solution.py:375
  33.6 0.0 copy-start.1
  33.6 0.1 slice_reduce_fusion.tab_ref
  33.7 0.0 all-to-all-done.1
  33.7 0.0 copy-start
  33.7 2.3 %attend.1 = f32[256,128]{1,0:T(8,128)S(1)} custom-call(s32[96]{0:T(128)S(1)} %slice_reduce_fusion.tab_ref, bf16[256,128]{1,0:T(8,128)(2,1)S(1)} %bitcast.13, bf16[96,128,128]{2,1,0:T(8,128)(2,1)S(1)} %get-tuple-element.33.kv_ref), custom_call_target="tpu_custom_call" | custom-call | tf_op jit(solution)/shard_map/attend/pallas_call | solution.py:392
  36.0 14.8 %all_to_all.21 = f32[64,4,128]{2,1,0:T(4,128)S(1)} all-to-all(f32[64,4,128]{2,1,0:T(4,128)S(1)} %bitcast.11), channel_id=1, replica_groups={{288,296,304,312,320,328,336,344,352,360,368,376,384,392,400,408,416,42..., dimensions={0} | all-to-all | bytes 262144 | tf_op jit(solution)/shard_map/all_to_all | solution.py:318
  50.9 0.0 copy-done
  50.9 0.5 combine.1
  51.4 9.9 %all_to_all.22 = f32[8,2,128]{2,1,0:T(2,128)S(1)} all-to-all(f32[8,2,128]{2,1,0:T(2,128)S(1)} %bitcast.15), channel_id=1, replica_groups={{4,5,6,7,0,1,2,3},{12,13,14,15,8,9,10,11},{20,21,22,23,16,17,18,19},{28..., dimensions={0} | all-to-all | bytes 16384 | tf_op jit(solution)/shard_map/all_to_all | solution.py:318
  61.3 0.0 copy-done.1
  61.3 0.6 add.3
  (3 shorter events, 0.0 us)
Async XLA Ops:
  16.4 17.3 %all-to-all-start.1 = ((bf16[64,4,128]{2,1,0:T(4,128)(2,1)}), bf16[64,4,128]{2,1,0:T(4,128)(2,1)S(1)}, u32[]{:S(2)}, u32[]{:S(2)}) async-start(bf16[64,4,128]{2,1,0:T(4,128)(2,1)} %bitcast.5), calls=%async_computation.1 | async-start | bytes 131072 | tf_op jit(solution)/shard_map/all_to_all | solution.py:318
  33.6 27.7 %copy-start.1 = (f32[1,256]{1,0:T(1,128)S(1)}, f32[1,256]{1,0:T(1,128)}, u32[]{:S(2)}) copy-start(f32[1,256]{1,0:T(1,128)} %param.8) | copy-start | bytes 3076
  33.7 17.2 %copy-start = (bf16[256,2048]{1,0:T(8,128)(2,1)S(1)}, bf16[256,2048]{1,0:T(8,128)(2,1)}, u32[]{:S(2)}) copy-start(bf16[256,2048]{1,0:T(8,128)(2,1)} %w_ref.1) | copy-start | bytes 3145732

commit v12 on v10

--- a/solution.py
+++ b/solution.py
@@ -21,6 +21,7 @@
 HBM = pl.BlockSpec(memory_space=pltpu.HBM)
 
 GROUP = 4
+TERM = 8
 
 FIRST = 36
 FIRST_SHARD = 4
@@ -119,23 +120,29 @@
     return copies
 
 
+def wait(copies):
+    for copy in copies:
+        copy.wait()
+
+
 def prepare_kernel(head_dim, x_ref, lengths_ref, *rest):
-    sources, (spread_ref, *targets) = rest[:3], rest[3:7]
-    cos_ref, sin_ref, near_x, near_lengths, sems = rest[7:]
+    sources, (spread_ref, *targets) = rest[:2], rest[2:5]
+    cos_ref, sin_ref, near_x, near_lengths, sems = rest[5:]
     copies = fetch((x_ref, lengths_ref, *sources), (near_x, near_lengths, *targets), sems)
-    copies[1].wait()
+    wait(copies[1:2])
     position = near_lengths[lax.axis_index("pool")]
     cos_ref[...], sin_ref[...] = rotation(position, head_dim, 2 * head_dim)
-    copies[0].wait()
+    wait(copies[:1])
     size = near_x.shape[0]
     for i in range(spread_ref.shape[0] // size):
         spread_ref[pl.ds(i * size, size), :] = near_x[...]
-    for copy in copies[2:]:
-        copy.wait()
-
-
-def query_kernel(head_dim, rows_ref, gain_ref, w_ref, w_keyval_ref, cos_ref, sin_ref, *rest):
-    out_ref, kv_ref, own_ref, tiles_ref, sem = rest
+    wait(copies[2:])
+
+
+def query_kernel(head_dim, rows_ref, gain_ref, w_ref, cos_ref, sin_ref, w_keyval_hbm, *rest):
+    out_ref, kv_ref, own_ref, tiles_ref, w_keyval_ref, sems = rest
+    weight = pltpu.make_async_copy(w_keyval_hbm, w_keyval_ref, sems.at[1])
+    weight.start()
     wide = 2 * head_dim
     cosine, sine = cos_ref[...], sin_ref[...]
     normed = normalise(rows_ref, gain_ref)
@@ -150,13 +157,14 @@
     tile = jnp.where(is_key, tile.astype(BF16).astype(F32) * SCORE_SCALE, 0.0)
     for v in range(tiles_ref.shape[0] // 8):
         tiles_ref[pl.ds(8 * v, 8), :] = tile.astype(BF16)
-    copy = pltpu.make_async_copy(tiles_ref, out_ref, sem)
+    copy = pltpu.make_async_copy(tiles_ref, out_ref, sems.at[0])
     copy.start()
+    weight.wait()
     keyval = project(normed, w_keyval_ref)
     turned = rope(keyval, cosine, sine, head_dim // 2)
     both = jnp.where(is_key, turned, keyval).astype(BF16)
-    kv_ref[...] = both[:1]
     both = both.astype(F32)
+    kv_ref[...] = both
     score = jnp.sum(tile * both, axis=1, keepdims=True)
     own_ref[...] = jnp.where(is_key, score, both)
     copy.wait()
@@ -166,8 +174,7 @@
     slots_here, block_len, lengths_hbm, slot_hbm, cache_ref, out_ref, held_ref, lengths_ref, slot_ref, sems
 ):
     copies = fetch((lengths_hbm, slot_hbm, cache_ref), (lengths_ref, slot_ref, held_ref), sems)
-    copies[0].wait()
-    copies[1].wait()
+    wait(copies[:2])
     requests, blocks = slot_ref.shape
     base = lax.axis_index("pool") * slots_here
     sub = subs((8, blocks))
@@ -193,7 +200,7 @@
         out_ref[pl.ds(8 * tile, 8), :] = jnp.broadcast_to(
             jnp.max(picked.astype(F32), axis=1, keepdims=True), (8, blocks)
         ).astype(jnp.int32)
-    copies[2].wait()
+    wait(copies[2:])
 
 
 def attend_kernel(
@@ -249,14 +256,29 @@
     for v in range(requests // 2):
         top = jnp.where(low, max_s[2 * v], max_s[2 * v + 1])
         out = jnp.where(low, acc_s[2 * v], acc_s[2 * v + 1])
-        out_ref[pl.ds(8 * v, 8), :] = jnp.where(lane < wide // 4, top, out)
+        out = jnp.where(lane < wide // 4, top, out)
+        terms = []
+        for _ in range(3):
+            terms.append(out.astype(BF16).astype(F32))
+            out = out - terms[-1]
+        third = (lane % (wide // 4)) // TERM
+        out = jnp.where(
+            (lane >= wide // 2) | (third == 0),
+            terms[0],
+            jnp.where(third == 1, terms[1], terms[2]),
+        )
+        out_ref[pl.ds(8 * v, 8), :] = out.astype(BF16)
 
 
 def combine_kernel(got_ref, own_ref, w_ref, out_ref):
     rows, wide = got_ref.shape
     lane = lanes((8, wide))
     row = subs((8, wide))
-    parts = [got_ref[pl.ds(8 * v, 8), :] for v in range(rows // 8)]
+    parts = []
+    for v in range(rows // 8):
+        part = got_ref[pl.ds(8 * v, 8), :].astype(F32)
+        whole = part + pltpu.roll(part, wide - TERM, 1) + pltpu.roll(part, wide - 2 * TERM, 1)
+        parts.append(jnp.where(lane < wide // 2, whole, part))
     top = parts[0]
     for part in parts[1:]:
         top = jnp.maximum(top, part)
@@ -317,40 +339,46 @@
         far(x) for x in (w_query, w_keyval, lengths, block_slot)
     )
     turn = jax.ShapeDtypeStruct((8, wide), F32)
-    spread_rows, held_query, held_keyval, held_gain, cosine, sine = call(
+    spread_rows, held_query, held_gain, cosine, sine = call(
         functools.partial(prepare_kernel, head_dim),
         "prepare",
         (
             jax.ShapeDtypeStruct((shards * lines, wide), F32),
             jax.ShapeDtypeStruct(w_query.shape, BF16),
-            jax.ShapeDtypeStruct(w_keyval.shape, BF16),
             jax.ShapeDtypeStruct(gain.shape, F32),
             turn,
             turn,
         ),
-        [HBM] * 5,
+        [HBM] * 4,
         [
             pltpu.VMEM((lines, wide), F32),
             pltpu.SMEM(lengths.shape, jnp.int32),
-            pltpu.SemaphoreType.DMA((5,)),
+            pltpu.SemaphoreType.DMA((4,)),
         ],
-    )(line, lengths, w_query, w_keyval, gain)
+    )(line, lengths, w_query, gain)
 
     rows = exchange(spread_rows, "mp", shards, FIRST_SHARD)
 
     tiles = jax.ShapeDtypeStruct((requests * GROUP, wide), BF16)
-    query, new_kv, own = call(
+    query, new_tile, own = call(
         functools.partial(query_kernel, head_dim),
         "query",
-        (tiles, jax.ShapeDtypeStruct((1, wide), BF16), turn),
-        [VMEM] * 6,
-        [pltpu.VMEM(tiles.shape, BF16), pltpu.SemaphoreType.DMA],
+        (tiles, turn, turn),
+        [VMEM] * 5 + [HBM],
+        [
+            pltpu.VMEM(tiles.shape, BF16),
+            pltpu.VMEM(w_keyval.shape, BF16),
+            pltpu.SemaphoreType.DMA((2,)),
+        ],
         out_specs=(HBM, VMEM, VMEM),
-    )(rows, held_gain, held_query, held_keyval, cosine, sine)
+    )(rows, held_gain, held_query, cosine, sine, w_keyval)
 
     queries = exchange(query, "pool", pools, FIRST)
 
-    lengths, block_slot, own = lax.optimization_barrier((lengths, block_slot, own))
+    lengths, block_slot, own, new_tile = lax.optimization_barrier(
+        (lengths, block_slot, own, new_tile)
+    )
+    new_kv = new_tile[:1].astype(BF16)
     table, held_cache = call(
         functools.partial(table_kernel, slots_here, block_len),
         "slot_table",
@@ -365,13 +393,13 @@
             pltpu.SemaphoreType.DMA((3,)),
         ],
     )(far(lengths), far(block_slot), cache)
-    table = table[:, 0]
+    table, new_kv = lax.optimization_barrier((table[:, 0], new_kv))
 
     per_request = pltpu.VMEM((requests, 8, wide), F32)
     partial = call(
         attend_kernel,
         "attend",
-        jax.ShapeDtypeStruct((requests * GROUP, wide), F32),
+        tiles,
         [SMEM, VMEM, VMEM],
         [
             per_request,

time: 62.6 us -> 62 us (level)
  blocking collectives: 38.2 us -> 37.2 us
    all_to_all x3, blocking collectives: 38.2 us -> 37.2 us  [exchange(): lax.all_to_all(x, axis, split_axis=0, concat_axis=0, tiled=True, axis_ind...]
  transfers between devices with their start and end apart: 1 -> 1, of which waited for: 1 -> 0; matrix products, arithmetic and copies ran while one was open for 0% -> 1% of each run, Pallas kernels for 3% -> 3%
where the time goes in v12:
time: 62 us; the launch traced here: 61.6 us
  blocking collectives  37.2 us (60%)
  starting transfers between devices  14.7 us (24%)
  Pallas kernels  7.82 us (13%)
  between operations  0.71 us (1%)
  local copies, waits for them, and re-layouts  0.63 us (1%)
    all_to_all x3, blocking collectives, exchange(): lax.all_to_all(x, axis, split_axis=0, concat_axis=0, tiled=True, axis_ind...  37.2 us
    all_to_all x1, starting transfers between devices, exchange(): lax.all_to_all(x, axis, split_axis=0, concat_axis=0, tiled=True, axis_ind...  14.7 us
    pallas_call x1, Pallas kernels, per_device(): call(attend_kernel, 'attend', tiles, [SMEM, VMEM, VMEM], [per_request, pl...  2.3 us
    pallas_call x1, Pallas kernels, per_device(): call(functools.partial(table_kernel, slots_here, block_len), 'slot_table'...  1.95 us
    pallas_call x1, Pallas kernels, per_device(): call(functools.partial(query_kernel, head_dim), 'query', (tiles, turn, tu...  1.71 us
    pallas_call x1, Pallas kernels, per_device(): call(functools.partial(prepare_kernel, head_dim), 'prepare', (jax.ShapeDt...  1.28 us
  transfers between devices with their start and end apart: 1, of which 0 were waited for; matrix products, arithmetic and copies ran while one was open for 1% of the time, Pallas kernels for 3%

profile of v12, /device:TPU:1, one launch (start us, length us, event | category | flops | bytes accessed | tf_op | source)
XLA Modules:
  0.0 61.6 jit_solution(11335588908790746444)
XLA Ops:
  0.6 1.3 %prepare.1 = (f32[16,128]{1,0:T(8,128)S(1)}, bf16[2048,256]{1,0:T(8,128)(2,1)S(1)}, f32[16,128]{1,0:T(8,128)S(1)}, f32[8,128]{1,0:T(8,128)S(1)}, f32[8,128]{1,0:T(8,128)S(1)}) custom-call(f32[2,128]{1,0:T(2,128)} %bitcast.19, s32[64]{0:T(128)} %lengths_hbm, bf16[2048,256]{1,0:T(8,128)(2,1)} %rest_0_.1, f32[16,128]{1,0:T(8,128)} %bitcast.18), custom_call_target="tpu_custom_call" | custom-call | tf_op jit(solution)/shard_map/prepare/pallas_call | solution.py:342
  1.9 13.1 %all_to_all.20 = f32[8,2,128]{2,1,0:T(2,128)S(1)} all-to-all(f32[8,2,128]{2,1,0:T(2,128)S(1)} %bitcast.16), channel_id=1, replica_groups={{4,5,6,7,0,1,2,3},{12,13,14,15,8,9,10,11},{20,21,22,23,16,17,18,19},{28..., dimensions={0} | all-to-all | bytes 16384 | tf_op jit(solution)/shard_map/all_to_all | solution.py:322
  15.0 1.7 %query.1 = (bf16[256,128]{1,0:T(8,128)(2,1)}, f32[8,128]{1,0:T(8,128)S(1)}, f32[8,128]{1,0:T(8,128)S(1)}) custom-call(f32[16,128]{1,0:T(8,128)S(1)} %bitcast.14, f32[16,128]{1,0:T(8,128)S(1)} %get-tuple-element.19.gain_ref, bf16[2048,256]{1,0:T(8,128)(2,1)S(1)} %get-tuple-element.20.w_ref, f32[8,128]{1,0:T(8,128)S(1)} %get-tuple-element.21.cos_ref, ...), custom_call_target="tpu_custom_call" | custom-call | tf_op jit(solution)/shard_map/query/pallas_call | solution.py:363
  16.7 14.7 %all-to-all-start.1 = ((bf16[64,4,128]{2,1,0:T(4,128)(2,1)}), bf16[64,4,128]{2,1,0:T(4,128)(2,1)S(1)}, u32[]{:S(2)}, u32[]{:S(2)}) async-start(bf16[64,4,128]{2,1,0:T(4,128)(2,1)} %bitcast.5), calls=%async_computation.1 | async-start | bytes 131072 | tf_op jit(solution)/shard_map/all_to_all | solution.py:322
  31.4 0.5 slice.8
  31.9 0.0 copy-start.1
  31.9 1.9 %slot_table.1 = (s32[96,128]{1,0:T(8,128)S(1)}, bf16[96,128,128]{2,1,0:T(8,128)(2,1)S(1)}) custom-call(s32[64]{0:T(128)} %lengths_hbm, s32[64,128]{1,0:T(8,128)} %slot_hbm, bf16[96,128,128]{2,1,0:T(8,128)(2,1)} %bitcast.17), custom_call_target="tpu_custom_call" | custom-call | tf_op jit(solution)/shard_map/slot_table/pallas_call | solution.py:382
  33.9 0.1 slice_reduce_fusion.tab_ref
  34.0 0.0 all-to-all-done.1
  34.0 0.0 copy-start
  34.0 2.3 %attend.1 = bf16[256,128]{1,0:T(8,128)(2,1)S(1)} custom-call(s32[96]{0:T(128)S(1)} %slice_reduce_fusion.tab_ref, bf16[256,128]{1,0:T(8,128)(2,1)S(1)} %bitcast.11, bf16[96,128,128]{2,1,0:T(8,128)(2,1)S(1)} %get-tuple-element.31.kv_ref), custom_call_target="tpu_custom_call" | custom-call | tf_op jit(solution)/shard_map/attend/pallas_call | solution.py:399
  36.3 14.2 %all_to_all.21 = bf16[64,4,128]{2,1,0:T(4,128)(2,1)S(1)} all-to-all(bf16[64,4,128]{2,1,0:T(4,128)(2,1)S(1)} %bitcast.12), channel_id=1, replica_groups={{288,296,304,312,320,328,336,344,352,360,368,376,384,392,400,408,416,42..., dimensions={0} | all-to-all | bytes 131072 | tf_op jit(solution)/shard_map/all_to_all | solution.py:322
  50.5 0.0 copy-done
  50.5 0.6 combine.1
  51.1 9.9 %all_to_all.22 = f32[8,2,128]{2,1,0:T(2,128)S(1)} all-to-all(f32[8,2,128]{2,1,0:T(2,128)S(1)} %bitcast.15), channel_id=1, replica_groups={{4,5,6,7,0,1,2,3},{12,13,14,15,8,9,10,11},{20,21,22,23,16,17,18,19},{28..., dimensions={0} | all-to-all | bytes 16384 | tf_op jit(solution)/shard_map/all_to_all | solution.py:322
  61.0 0.0 copy-done.1
  61.1 0.6 add.3
  (3 shorter events, 0.0 us)
Async XLA Ops:
  16.7 17.3 %all-to-all-start.1 = ((bf16[64,4,128]{2,1,0:T(4,128)(2,1)}), bf16[64,4,128]{2,1,0:T(4,128)(2,1)S(1)}, u32[]{:S(2)}, u32[]{:S(2)}) async-start(bf16[64,4,128]{2,1,0:T(4,128)(2,1)} %bitcast.5), calls=%async_computation.1 | async-start | bytes 131072 | tf_op jit(solution)/shard_map/all_to_all | solution.py:322
  31.9 29.1 %copy-start.1 = (f32[1,256]{1,0:T(1,128)S(1)}, f32[1,256]{1,0:T(1,128)}, u32[]{:S(2)}) copy-start(f32[1,256]{1,0:T(1,128)} %param.8) | copy-start | bytes 3076
  34.0 16.5 %copy-start = (bf16[256,2048]{1,0:T(8,128)(2,1)S(1)}, bf16[256,2048]{1,0:T(8,128)(2,1)}, u32[]{:S(2)}) copy-start(bf16[256,2048]{1,0:T(8,128)(2,1)} %w_ref.1) | copy-start | bytes 3145732

commit v13 on v12

--- a/solution.py
+++ b/solution.py
@@ -139,42 +139,23 @@
     wait(copies[2:])
 
 
-def query_kernel(head_dim, rows_ref, gain_ref, w_ref, cos_ref, sin_ref, w_keyval_hbm, *rest):
-    out_ref, kv_ref, own_ref, tiles_ref, w_keyval_ref, sems = rest
-    weight = pltpu.make_async_copy(w_keyval_hbm, w_keyval_ref, sems.at[1])
-    weight.start()
+def query_kernel(head_dim, rows_ref, gain_ref, w_ref, cos_ref, sin_ref, out_ref):
     wide = 2 * head_dim
     cosine, sine = cos_ref[...], sin_ref[...]
-    normed = normalise(rows_ref, gain_ref)
-    query = project(normed, w_ref)
+    query = project(normalise(rows_ref, gain_ref), w_ref)
     row = subs((8, wide)) % GROUP
     tile = jnp.zeros((8, wide), F32)
     for c in range(GROUP // 2):
         part = rope(query[:, c * wide : (c + 1) * wide], cosine, sine, head_dim // 2)
         tile = jnp.where(row == 2 * c, part, tile)
         tile = jnp.where(row == 2 * c + 1, pltpu.roll(part, head_dim, 1), tile)
-    is_key = lanes(tile.shape) < head_dim
-    tile = jnp.where(is_key, tile.astype(BF16).astype(F32) * SCORE_SCALE, 0.0)
-    for v in range(tiles_ref.shape[0] // 8):
-        tiles_ref[pl.ds(8 * v, 8), :] = tile.astype(BF16)
-    copy = pltpu.make_async_copy(tiles_ref, out_ref, sems.at[0])
-    copy.start()
-    weight.wait()
-    keyval = project(normed, w_keyval_ref)
-    turned = rope(keyval, cosine, sine, head_dim // 2)
-    both = jnp.where(is_key, turned, keyval).astype(BF16)
-    both = both.astype(F32)
-    kv_ref[...] = both
-    score = jnp.sum(tile * both, axis=1, keepdims=True)
-    own_ref[...] = jnp.where(is_key, score, both)
-    copy.wait()
-
-
-def table_kernel(
-    slots_here, block_len, lengths_hbm, slot_hbm, cache_ref, out_ref, held_ref, lengths_ref, slot_ref, sems
-):
-    copies = fetch((lengths_hbm, slot_hbm, cache_ref), (lengths_ref, slot_ref, held_ref), sems)
-    wait(copies[:2])
+    tile = tile.astype(BF16).astype(F32) * SCORE_SCALE
+    tile = jnp.where(lanes(tile.shape) < head_dim, tile, 0.0).astype(BF16)
+    for v in range(out_ref.shape[0] // 8):
+        out_ref[pl.ds(8 * v, 8), :] = tile
+
+
+def find_slots(slots_here, block_len, lengths_ref, slot_ref, out_ref):
     requests, blocks = slot_ref.shape
     base = lax.axis_index("pool") * slots_here
     sub = subs((8, blocks))
@@ -200,7 +181,29 @@
         out_ref[pl.ds(8 * tile, 8), :] = jnp.broadcast_to(
             jnp.max(picked.astype(F32), axis=1, keepdims=True), (8, blocks)
         ).astype(jnp.int32)
-    wait(copies[2:])
+
+
+def window_kernel(slots_here, block_len, head_dim, rows_ref, gain_ref, cos_ref, sin_ref, *rest):
+    sources, (table_ref, held_ref, kv_ref, own_ref) = rest[:5], rest[5:9]
+    lengths_ref, slot_ref, query_ref, w_ref, sems = rest[9:]
+    lengths_hbm, slot_hbm, query_hbm, w_hbm, cache_ref = sources
+    copies = fetch(
+        (lengths_hbm, slot_hbm, query_hbm.at[pl.ds(0, query_ref.shape[0])], w_hbm, cache_ref),
+        (lengths_ref, slot_ref, query_ref, w_ref, held_ref),
+        sems,
+    )
+    normed = normalise(rows_ref, gain_ref)
+    wait(copies[:4])
+    keyval = project(normed, w_ref)
+    is_key = lanes(keyval.shape) < head_dim
+    turned = rope(keyval, cos_ref[...], sin_ref[...], head_dim // 2)
+    both = jnp.where(is_key, turned, keyval).astype(BF16)
+    kv_ref[...] = both[:1]
+    both = both.astype(F32)
+    score = jnp.sum(query_ref[:8, :].astype(F32) * both, axis=1, keepdims=True)
+    own_ref[...] = jnp.where(is_key, score, both)
+    find_slots(slots_here, block_len, lengths_ref, slot_ref, table_ref)
+    wait(copies[4:])
 
 
 def attend_kernel(
@@ -360,40 +363,32 @@
     rows = exchange(spread_rows, "mp", shards, FIRST_SHARD)
 
     tiles = jax.ShapeDtypeStruct((requests * GROUP, wide), BF16)
-    query, new_tile, own = call(
-        functools.partial(query_kernel, head_dim),
-        "query",
-        (tiles, turn, turn),
-        [VMEM] * 5 + [HBM],
-        [
-            pltpu.VMEM(tiles.shape, BF16),
-            pltpu.VMEM(w_keyval.shape, BF16),
-            pltpu.SemaphoreType.DMA((2,)),
-        ],
-        out_specs=(HBM, VMEM, VMEM),
-    )(rows, held_gain, held_query, cosine, sine, w_keyval)
+    query = call(
+        functools.partial(query_kernel, head_dim), "query", tiles, [VMEM] * 5
+    )(rows, held_gain, held_query, cosine, sine)
 
     queries = exchange(query, "pool", pools, FIRST)
 
-    lengths, block_slot, own, new_tile = lax.optimization_barrier(
-        (lengths, block_slot, own, new_tile)
-    )
-    new_kv = new_tile[:1].astype(BF16)
-    table, held_cache = call(
-        functools.partial(table_kernel, slots_here, block_len),
-        "slot_table",
+    table, held_cache, new_kv, own = call(
+        functools.partial(window_kernel, slots_here, block_len, head_dim),
+        "window",
         (
             jax.ShapeDtypeStruct((slots_here, block_slot.shape[1]), jnp.int32),
             jax.ShapeDtypeStruct(cache.shape, BF16),
+            jax.ShapeDtypeStruct((1, wide), BF16),
+            turn,
         ),
-        [HBM] * 3,
+        [VMEM] * 4 + [HBM] * 5,
         [
             pltpu.SMEM(lengths.shape, jnp.int32),
             pltpu.VMEM(block_slot.shape, jnp.int32),
-            pltpu.SemaphoreType.DMA((3,)),
+            pltpu.VMEM((16, wide), BF16),
+            pltpu.VMEM(w_keyval.shape, BF16),
+            pltpu.SemaphoreType.DMA((5,)),
         ],
-    )(far(lengths), far(block_slot), cache)
-    table, new_kv = lax.optimization_barrier((table[:, 0], new_kv))
+        limit=8 << 20,
+    )(rows, held_gain, cosine, sine, lengths, block_slot, far(query), w_keyval, cache)
+    table = table[:, 0]
 
     per_request = pltpu.VMEM((requests, 8, wide), F32)
     partial = call(

time: 62 us -> 61.3 us (0.989)
  transfers between devices with their start and end apart: 1 -> 1, of which waited for: 0 -> 0; matrix products, arithmetic and copies ran while one was open for 1% -> 0% of each run, Pallas kernels for 3% -> 4%
where the time goes in v13:
time: 61.3 us; the launch traced here: 61 us
  blocking collectives  37 us (60%)
  starting transfers between devices  14.6 us (24%)
  Pallas kernels  7.88 us (13%)
  between operations  0.7 us (1%)
    all_to_all x3, blocking collectives, exchange(): lax.all_to_all(x, axis, split_axis=0, concat_axis=0, tiled=True, axis_ind...  37 us
    all_to_all x1, starting transfers between devices, exchange(): lax.all_to_all(x, axis, split_axis=0, concat_axis=0, tiled=True, axis_ind...  14.6 us
    pallas_call x1, Pallas kernels, per_device(): call(functools.partial(window_kernel, slots_here, block_len, head_dim), '...  2.64 us
    pallas_call x1, Pallas kernels, per_device(): call(attend_kernel, 'attend', tiles, [SMEM, VMEM, VMEM], [per_request, pl...  2.29 us
    pallas_call x1, Pallas kernels, per_device(): call(functools.partial(prepare_kernel, head_dim), 'prepare', (jax.ShapeDt...  1.28 us
  transfers between devices with their start and end apart: 1, of which 0 were waited for; matrix products, arithmetic and copies ran while one was open for 0% of the time, Pallas kernels for 4%

profile of v13, /device:TPU:1, one launch (start us, length us, event | category | flops | bytes accessed | tf_op | source)
XLA Modules:
  0.0 61.0 jit_solution(10411820866078850720)
XLA Ops:
  0.6 1.3 %prepare.1 = (f32[16,128]{1,0:T(8,128)S(1)}, bf16[2048,256]{1,0:T(8,128)(2,1)S(1)}, f32[16,128]{1,0:T(8,128)S(1)}, f32[8,128]{1,0:T(8,128)S(1)}, f32[8,128]{1,0:T(8,128)S(1)}) custom-call(f32[2,128]{1,0:T(2,128)} %bitcast.20, s32[64]{0:T(128)} %rest_0_.3, bf16[2048,256]{1,0:T(8,128)(2,1)} %rest_0_.2, f32[16,128]{1,0:T(8,128)} %bitcast.19), custom_call_target="tpu_custom_call" | custom-call | tf_op jit(solution)/shard_map/prepare/pallas_call | solution.py:345
  1.9 13.1 %all_to_all.20 = f32[8,2,128]{2,1,0:T(2,128)S(1)} all-to-all(f32[8,2,128]{2,1,0:T(2,128)S(1)} %bitcast.17), channel_id=1, replica_groups={{4,5,6,7,0,1,2,3},{12,13,14,15,8,9,10,11},{20,21,22,23,16,17,18,19},{28..., dimensions={0} | all-to-all | bytes 16384 | tf_op jit(solution)/shard_map/all_to_all | solution.py:325
  15.0 1.1 %query.1.rest_2_ = bf16[256,128]{1,0:T(8,128)(2,1)} custom-call(f32[16,128]{1,0:T(8,128)S(1)} %bitcast.14, f32[16,128]{1,0:T(8,128)S(1)} %get-tuple-element.12.gain_ref, bf16[2048,256]{1,0:T(8,128)(2,1)S(1)} %get-tuple-element.15.w_ref, f32[8,128]{1,0:T(8,128)S(1)} %get-tuple-element.13.cos_ref, f32[8,128]{1,0:T(8,128)S(1)} %get-tuple-element.14.sin_ref), custom_call_target="tpu_custom_call" | custom-call | tf_op jit(solution)/shard_map/query/pallas_call | solution.py:366
  16.1 14.6 %all-to-all-start.1 = ((bf16[64,4,128]{2,1,0:T(4,128)(2,1)}), bf16[64,4,128]{2,1,0:T(4,128)(2,1)S(1)}, u32[]{:S(2)}, u32[]{:S(2)}) async-start(bf16[64,4,128]{2,1,0:T(4,128)(2,1)} %bitcast.5), calls=%async_computation.1 | async-start | bytes 131072 | tf_op jit(solution)/shard_map/all_to_all | solution.py:325
  30.8 2.6 %window.1 = (s32[96,128]{1,0:T(8,128)S(1)}, bf16[96,128,128]{2,1,0:T(8,128)(2,1)S(1)}, bf16[1,128]{1,0:T(2,128)(2,1)}, f32[8,128]{1,0:T(8,128)S(1)}) custom-call(f32[16,128]{1,0:T(8,128)S(1)} %bitcast.15, f32[16,128]{1,0:T(8,128)S(1)} %get-tuple-element.12.gain_ref, f32[8,128]{1,0:T(8,128)S(1)} %get-tuple-element.13.cos_ref, ...), custom_call_target="tpu_custom_call" | custom-call | tf_op jit(solution)/shard_map/window/pallas_call | solution.py:372
  33.4 0.0 copy-start.1
  33.4 0.1 slice_reduce_fusion.tab_ref
  33.5 0.0 all-to-all-done.1
  33.5 0.0 copy-start
  33.6 2.3 %attend.1 = bf16[256,128]{1,0:T(8,128)(2,1)S(1)} custom-call(s32[96]{0:T(128)S(1)} %slice_reduce_fusion.tab_ref, bf16[256,128]{1,0:T(8,128)(2,1)S(1)} %bitcast.11, bf16[96,128,128]{2,1,0:T(8,128)(2,1)S(1)} %get-tuple-element.17.kv_ref), custom_call_target="tpu_custom_call" | custom-call | tf_op jit(solution)/shard_map/attend/pallas_call | solution.py:394
  35.8 14.2 %all_to_all.21 = bf16[64,4,128]{2,1,0:T(4,128)(2,1)S(1)} all-to-all(bf16[64,4,128]{2,1,0:T(4,128)(2,1)S(1)} %bitcast.12), channel_id=1, replica_groups={{288,296,304,312,320,328,336,344,352,360,368,376,384,392,400,408,416,42..., dimensions={0} | all-to-all | bytes 131072 | tf_op jit(solution)/shard_map/all_to_all | solution.py:325
  50.0 0.0 copy-done
  50.0 0.6 combine.1
  50.6 9.8 %all_to_all.22 = f32[8,2,128]{2,1,0:T(2,128)S(1)} all-to-all(f32[8,2,128]{2,1,0:T(2,128)S(1)} %bitcast.16), channel_id=1, replica_groups={{4,5,6,7,0,1,2,3},{12,13,14,15,8,9,10,11},{20,21,22,23,16,17,18,19},{28..., dimensions={0} | all-to-all | bytes 16384 | tf_op jit(solution)/shard_map/all_to_all | solution.py:325
  60.4 0.0 copy-done.1
  60.4 0.6 add.3
  (2 shorter events, 0.0 us)
Async XLA Ops:
  16.1 17.4 %all-to-all-start.1 = ((bf16[64,4,128]{2,1,0:T(4,128)(2,1)}), bf16[64,4,128]{2,1,0:T(4,128)(2,1)S(1)}, u32[]{:S(2)}, u32[]{:S(2)}) async-start(bf16[64,4,128]{2,1,0:T(4,128)(2,1)} %bitcast.5), calls=%async_computation.1 | async-start | bytes 131072 | tf_op jit(solution)/shard_map/all_to_all | solution.py:325
  33.4 27.0 %copy-start.1 = (f32[1,256]{1,0:T(1,128)S(1)}, f32[1,256]{1,0:T(1,128)}, u32[]{:S(2)}) copy-start(f32[1,256]{1,0:T(1,128)} %param.8) | copy-start | bytes 3076
  33.5 16.5 %copy-start = (bf16[256,2048]{1,0:T(8,128)(2,1)S(1)}, bf16[256,2048]{1,0:T(8,128)(2,1)}, u32[]{:S(2)}) copy-start(bf16[256,2048]{1,0:T(8,128)(2,1)} %w_ref.1) | copy-start | bytes 3145732

commit v14 on v13

--- a/solution.py
+++ b/solution.py
@@ -23,7 +23,8 @@
 GROUP = 4
 TERM = 8
 
-FIRST = 36
+FIRST_QUERY = 62
+FIRST_PARTIAL = 36
 FIRST_SHARD = 4
 
 
@@ -169,7 +170,7 @@
         here = slot_ref[pl.ds(8 * v, 8), :] - base
         wanted.append(jnp.where(limit > 0, here, -1))
         payload.append(
-            ((sub + 8 * v + requests - FIRST) % requests) * 256 + jnp.minimum(limit, block_len)
+            ((sub + 8 * v + requests - FIRST_QUERY) % requests) * 256 + jnp.minimum(limit, block_len)
         )
     for tile in range(slots_here // 8):
         picked = jnp.zeros((8, blocks), jnp.int32)
@@ -270,7 +271,8 @@
             terms[0],
             jnp.where(third == 1, terms[1], terms[2]),
         )
-        out_ref[pl.ds(8 * v, 8), :] = out.astype(BF16)
+        at = (2 * v + FIRST_QUERY - FIRST_PARTIAL) % requests // 2
+        out_ref[pl.ds(8 * at, 8), :] = out.astype(BF16)
 
 
 def combine_kernel(got_ref, own_ref, w_ref, out_ref):
@@ -367,7 +369,7 @@
         functools.partial(query_kernel, head_dim), "query", tiles, [VMEM] * 5
     )(rows, held_gain, held_query, cosine, sine)
 
-    queries = exchange(query, "pool", pools, FIRST)
+    queries = exchange(query, "pool", pools, FIRST_QUERY)
 
     table, held_cache, new_kv, own = call(
         functools.partial(window_kernel, slots_here, block_len, head_dim),
@@ -405,7 +407,7 @@
         limit=12 << 20,
     )(table, queries, held_cache)
 
-    got = exchange(partial, "pool", pools, FIRST)
+    got = exchange(partial, "pool", pools, FIRST_PARTIAL)
 
     mixed = call(
         combine_kernel,

time: 61.3 us -> 62.3 us (1.016)
  waiting for transfers between devices: 0.01 us -> 3.94 us
  starting transfers between devices: 14.6 us -> 11.9 us
    all_to_all x1, waiting for transfers between devices: 0.01 us -> 3.94 us  [exchange(): lax.all_to_all(x, axis, split_axis=0, concat_axis=0, tiled=True, axis_ind...]
    all_to_all x1, starting transfers between devices: 14.6 us -> 11.9 us  [exchange(): lax.all_to_all(x, axis, split_axis=0, concat_axis=0, tiled=True, axis_ind...]
  transfers between devices with their start and end apart: 1 -> 1, of which waited for: 0 -> 1; matrix products, arithmetic and copies ran while one was open for 0% -> 0% of each run, Pallas kernels for 4% -> 4%
where the time goes in v14:
time: 62.3 us; the launch traced here: 62 us
  blocking collectives  36.9 us (59%)
  starting transfers between devices  11.9 us (19%)
  Pallas kernels  7.91 us (13%)
  waiting for transfers between devices  3.94 us (6%)
  between operations  0.69 us (1%)
    all_to_all x3, blocking collectives, exchange(): lax.all_to_all(x, axis, split_axis=0, concat_axis=0, tiled=True, axis_ind...  36.9 us
    all_to_all x1, starting transfers between devices, exchange(): lax.all_to_all(x, axis, split_axis=0, concat_axis=0, tiled=True, axis_ind...  11.9 us
    all_to_all x1, waiting for transfers between devices, exchange(): lax.all_to_all(x, axis, split_axis=0, concat_axis=0, tiled=True, axis_ind...  3.94 us
    pallas_call x1, Pallas kernels, per_device(): call(functools.partial(window_kernel, slots_here, block_len, head_dim), '...  2.64 us
    pallas_call x1, Pallas kernels, per_device(): call(attend_kernel, 'attend', tiles, [SMEM, VMEM, VMEM], [per_request, pl...  2.32 us
    pallas_call x1, Pallas kernels, per_device(): call(functools.partial(prepare_kernel, head_dim), 'prepare', (jax.ShapeDt...  1.28 us
  transfers between devices with their start and end apart: 1, of which 1 were waited for; matrix products, arithmetic and copies ran while one was open for 0% of the time, Pallas kernels for 4%

profile of v14, /device:TPU:1, one launch (start us, length us, event | category | flops | bytes accessed | tf_op | source)
XLA Modules:
  0.0 62.0 jit_solution(18044085552873213126)
XLA Ops:
  0.6 1.3 %prepare.1 = (f32[16,128]{1,0:T(8,128)S(1)}, bf16[2048,256]{1,0:T(8,128)(2,1)S(1)}, f32[16,128]{1,0:T(8,128)S(1)}, f32[8,128]{1,0:T(8,128)S(1)}, f32[8,128]{1,0:T(8,128)S(1)}) custom-call(f32[2,128]{1,0:T(2,128)} %bitcast.20, s32[64]{0:T(128)} %rest_0_.3, bf16[2048,256]{1,0:T(8,128)(2,1)} %rest_0_.2, f32[16,128]{1,0:T(8,128)} %bitcast.19), custom_call_target="tpu_custom_call" | custom-call | tf_op jit(solution)/shard_map/prepare/pallas_call | solution.py:347
  1.9 13.1 %all_to_all.20 = f32[8,2,128]{2,1,0:T(2,128)S(1)} all-to-all(f32[8,2,128]{2,1,0:T(2,128)S(1)} %bitcast.17), channel_id=1, replica_groups={{4,5,6,7,0,1,2,3},{12,13,14,15,8,9,10,11},{20,21,22,23,16,17,18,19},{28..., dimensions={0} | all-to-all | bytes 16384 | tf_op jit(solution)/shard_map/all_to_all | solution.py:327
  15.0 1.1 %query.1.rest_2_ = bf16[256,128]{1,0:T(8,128)(2,1)} custom-call(f32[16,128]{1,0:T(8,128)S(1)} %bitcast.14, f32[16,128]{1,0:T(8,128)S(1)} %get-tuple-element.12.gain_ref, bf16[2048,256]{1,0:T(8,128)(2,1)S(1)} %get-tuple-element.15.w_ref, f32[8,128]{1,0:T(8,128)S(1)} %get-tuple-element.13.cos_ref, f32[8,128]{1,0:T(8,128)S(1)} %get-tuple-element.14.sin_ref), custom_call_target="tpu_custom_call" | custom-call | tf_op jit(solution)/shard_map/query/pallas_call | solution.py:368
  16.1 11.9 %all-to-all-start.1 = ((bf16[64,4,128]{2,1,0:T(4,128)(2,1)}), bf16[64,4,128]{2,1,0:T(4,128)(2,1)S(1)}, u32[]{:S(2)}, u32[]{:S(2)}) async-start(bf16[64,4,128]{2,1,0:T(4,128)(2,1)} %bitcast.5), calls=%async_computation.1 | async-start | bytes 131072 | tf_op jit(solution)/shard_map/all_to_all | solution.py:327
  28.0 2.6 %window.1 = (s32[96,128]{1,0:T(8,128)S(1)}, bf16[96,128,128]{2,1,0:T(8,128)(2,1)S(1)}, bf16[1,128]{1,0:T(2,128)(2,1)}, f32[8,128]{1,0:T(8,128)S(1)}) custom-call(f32[16,128]{1,0:T(8,128)S(1)} %bitcast.15, f32[16,128]{1,0:T(8,128)S(1)} %get-tuple-element.12.gain_ref, f32[8,128]{1,0:T(8,128)S(1)} %get-tuple-element.13.cos_ref, ...), custom_call_target="tpu_custom_call" | custom-call | tf_op jit(solution)/shard_map/window/pallas_call | solution.py:374
  30.6 0.0 copy-start.1
  30.7 0.1 slice_reduce_fusion.tab_ref
  30.8 3.9 %all-to-all-done.1 = bf16[64,4,128]{2,1,0:T(4,128)(2,1)S(1)} async-done(((bf16[64,4,128]{2,1,0:T(4,128)(2,1)}), bf16[64,4,128]{2,1,0:T(4,128)(2,1)S(1)}, u32[]{:S(2)}, u32[]{:S(2)}) %all-to-all-start.1) | async-done | bytes 65568 | tf_op jit(solution)/shard_map/all_to_all | solution.py:327
  34.7 0.0 copy-start
  34.7 2.3 %attend.1 = bf16[256,128]{1,0:T(8,128)(2,1)S(1)} custom-call(s32[96]{0:T(128)S(1)} %slice_reduce_fusion.tab_ref, bf16[256,128]{1,0:T(8,128)(2,1)S(1)} %bitcast.11, bf16[96,128,128]{2,1,0:T(8,128)(2,1)S(1)} %get-tuple-element.17.kv_ref), custom_call_target="tpu_custom_call" | custom-call | tf_op jit(solution)/shard_map/attend/pallas_call | solution.py:396
  37.0 14.2 %all_to_all.21 = bf16[64,4,128]{2,1,0:T(4,128)(2,1)S(1)} all-to-all(bf16[64,4,128]{2,1,0:T(4,128)(2,1)S(1)} %bitcast.12), channel_id=1, replica_groups={{288,296,304,312,320,328,336,344,352,360,368,376,384,392,400,408,416,42..., dimensions={0} | all-to-all | bytes 131072 | tf_op jit(solution)/shard_map/all_to_all | solution.py:327
  51.2 0.0 copy-done
  51.2 0.6 combine.1
  51.8 9.7 %all_to_all.22 = f32[8,2,128]{2,1,0:T(2,128)S(1)} all-to-all(f32[8,2,128]{2,1,0:T(2,128)S(1)} %bitcast.16), channel_id=1, replica_groups={{4,5,6,7,0,1,2,3},{12,13,14,15,8,9,10,11},{20,21,22,23,16,17,18,19},{28..., dimensions={0} | all-to-all | bytes 16384 | tf_op jit(solution)/shard_map/all_to_all | solution.py:327
  61.5 0.0 copy-done.1
  61.5 0.6 add.3
  (2 shorter events, 0.0 us)
Async XLA Ops:
  16.1 18.6 %all-to-all-start.1 = ((bf16[64,4,128]{2,1,0:T(4,128)(2,1)}), bf16[64,4,128]{2,1,0:T(4,128)(2,1)S(1)}, u32[]{:S(2)}, u32[]{:S(2)}) async-start(bf16[64,4,128]{2,1,0:T(4,128)(2,1)} %bitcast.5), calls=%async_computation.1 | async-start | bytes 131072 | tf_op jit(solution)/shard_map/all_to_all | solution.py:327
  30.6 30.8 %copy-start.1 = (f32[1,256]{1,0:T(1,128)S(1)}, f32[1,256]{1,0:T(1,128)}, u32[]{:S(2)}) copy-start(f32[1,256]{1,0:T(1,128)} %param.8) | copy-start | bytes 3076
  34.7 16.5 %copy-start = (bf16[256,2048]{1,0:T(8,128)(2,1)S(1)}, bf16[256,2048]{1,0:T(8,128)(2,1)}, u32[]{:S(2)}) copy-start(bf16[256,2048]{1,0:T(8,128)(2,1)} %w_ref.1) | copy-start | bytes 3145732

commit v15 on v13

--- a/solution.py
+++ b/solution.py
@@ -24,7 +24,7 @@
 TERM = 8
 
 FIRST = 36
-FIRST_SHARD = 4
+FIRST_SHARD = 5
 
 
 def far(x):
@@ -309,12 +309,16 @@
     ]
     line = jnp.broadcast_to(jnp.concatenate(chunks, axis=1), (8, GROUP // 2 * wide)).astype(BF16)
     lines = out_ref.shape[0]
+    products = [
+        jnp.dot(line, w_ref[:, pl.ds(v * 8 * wide, 8 * wide)], preferred_element_type=F32)
+        for v in range(lines // 8)
+    ]
     for v in range(lines // 8):
-        at = (8 * v + FIRST_SHARD * GROUP // 2) % lines * wide
-        part = jnp.dot(line, w_ref[:, pl.ds(at, 8 * wide)], preferred_element_type=F32)
         tile = jnp.zeros((8, wide), F32)
         for k in range(8):
-            tile = jnp.where(row == k, part[:, k * wide : (k + 1) * wide], tile)
+            n = (8 * v + k + FIRST_SHARD * GROUP // 2) % lines
+            part = products[n // 8]
+            tile = jnp.where(row == k, part[:, n % 8 * wide : (n % 8 + 1) * wide], tile)
         out_ref[pl.ds(8 * v, 8), :] = tile
 
 

time: 61.3 us -> 60.7 us (level)
  no operation moved by 1% of the time
where the time goes in v15:
time: 60.7 us; the launch traced here: 60.4 us
  blocking collectives  36.5 us (60%)
  starting transfers between devices  14.6 us (24%)
  Pallas kernels  7.89 us (13%)
  between operations  0.7 us (1%)
    all_to_all x3, blocking collectives, exchange(): lax.all_to_all(x, axis, split_axis=0, concat_axis=0, tiled=True, axis_ind...  36.5 us
    all_to_all x1, starting transfers between devices, exchange(): lax.all_to_all(x, axis, split_axis=0, concat_axis=0, tiled=True, axis_ind...  14.6 us
    pallas_call x1, Pallas kernels, per_device(): call(functools.partial(window_kernel, slots_here, block_len, head_dim), '...  2.64 us
    pallas_call x1, Pallas kernels, per_device(): call(attend_kernel, 'attend', tiles, [SMEM, VMEM, VMEM], [per_request, pl...  2.3 us
    pallas_call x1, Pallas kernels, per_device(): call(functools.partial(prepare_kernel, head_dim), 'prepare', (jax.ShapeDt...  1.28 us
  transfers between devices with their start and end apart: 1, of which 0 were waited for; matrix products, arithmetic and copies ran while one was open for 0% of the time, Pallas kernels for 4%

profile of v15, /device:TPU:1, one launch (start us, length us, event | category | flops | bytes accessed | tf_op | source)
XLA Modules:
  0.0 60.4 jit_solution(12503951648267330535)
XLA Ops:
  0.6 1.3 %prepare.1 = (f32[16,128]{1,0:T(8,128)S(1)}, bf16[2048,256]{1,0:T(8,128)(2,1)S(1)}, f32[16,128]{1,0:T(8,128)S(1)}, f32[8,128]{1,0:T(8,128)S(1)}, f32[8,128]{1,0:T(8,128)S(1)}) custom-call(f32[2,128]{1,0:T(2,128)} %bitcast.20, s32[64]{0:T(128)} %rest_0_.3, bf16[2048,256]{1,0:T(8,128)(2,1)} %rest_0_.2, f32[16,128]{1,0:T(8,128)} %bitcast.19), custom_call_target="tpu_custom_call" | custom-call | tf_op jit(solution)/shard_map/prepare/pallas_call | solution.py:349
  1.9 13.0 %all_to_all.20 = f32[8,2,128]{2,1,0:T(2,128)S(1)} all-to-all(f32[8,2,128]{2,1,0:T(2,128)S(1)} %bitcast.17), channel_id=1, replica_groups={{5,6,7,0,1,2,3,4},{13,14,15,8,9,10,11,12},{21,22,23,16,17,18,19,20},{29..., dimensions={0} | all-to-all | bytes 16384 | tf_op jit(solution)/shard_map/all_to_all | solution.py:329
  14.9 1.1 %query.1.rest_2_ = bf16[256,128]{1,0:T(8,128)(2,1)} custom-call(f32[16,128]{1,0:T(8,128)S(1)} %bitcast.14, f32[16,128]{1,0:T(8,128)S(1)} %get-tuple-element.12.gain_ref, bf16[2048,256]{1,0:T(8,128)(2,1)S(1)} %get-tuple-element.15.w_ref, f32[8,128]{1,0:T(8,128)S(1)} %get-tuple-element.13.cos_ref, f32[8,128]{1,0:T(8,128)S(1)} %get-tuple-element.14.sin_ref), custom_call_target="tpu_custom_call" | custom-call | tf_op jit(solution)/shard_map/query/pallas_call | solution.py:370
  16.0 14.6 %all-to-all-start.1 = ((bf16[64,4,128]{2,1,0:T(4,128)(2,1)}), bf16[64,4,128]{2,1,0:T(4,128)(2,1)S(1)}, u32[]{:S(2)}, u32[]{:S(2)}) async-start(bf16[64,4,128]{2,1,0:T(4,128)(2,1)} %bitcast.5), calls=%async_computation.1 | async-start | bytes 131072 | tf_op jit(solution)/shard_map/all_to_all | solution.py:329
  30.6 2.6 %window.1 = (s32[96,128]{1,0:T(8,128)S(1)}, bf16[96,128,128]{2,1,0:T(8,128)(2,1)S(1)}, bf16[1,128]{1,0:T(2,128)(2,1)}, f32[8,128]{1,0:T(8,128)S(1)}) custom-call(f32[16,128]{1,0:T(8,128)S(1)} %bitcast.15, f32[16,128]{1,0:T(8,128)S(1)} %get-tuple-element.12.gain_ref, f32[8,128]{1,0:T(8,128)S(1)} %get-tuple-element.13.cos_ref, ...), custom_call_target="tpu_custom_call" | custom-call | tf_op jit(solution)/shard_map/window/pallas_call | solution.py:376
  33.2 0.0 copy-start.1
  33.2 0.1 slice_reduce_fusion.tab_ref
  33.3 0.0 all-to-all-done.1
  33.3 0.0 copy-start
  33.4 2.3 %attend.1 = bf16[256,128]{1,0:T(8,128)(2,1)S(1)} custom-call(s32[96]{0:T(128)S(1)} %slice_reduce_fusion.tab_ref, bf16[256,128]{1,0:T(8,128)(2,1)S(1)} %bitcast.11, bf16[96,128,128]{2,1,0:T(8,128)(2,1)S(1)} %get-tuple-element.17.kv_ref), custom_call_target="tpu_custom_call" | custom-call | tf_op jit(solution)/shard_map/attend/pallas_call | solution.py:398
  35.7 14.2 %all_to_all.21 = bf16[64,4,128]{2,1,0:T(4,128)(2,1)S(1)} all-to-all(bf16[64,4,128]{2,1,0:T(4,128)(2,1)S(1)} %bitcast.12), channel_id=1, replica_groups={{288,296,304,312,320,328,336,344,352,360,368,376,384,392,400,408,416,42..., dimensions={0} | all-to-all | bytes 131072 | tf_op jit(solution)/shard_map/all_to_all | solution.py:329
  49.8 0.0 copy-done
  49.8 0.6 combine.1
  50.4 9.4 %all_to_all.22 = f32[8,2,128]{2,1,0:T(2,128)S(1)} all-to-all(f32[8,2,128]{2,1,0:T(2,128)S(1)} %bitcast.16), channel_id=1, replica_groups={{5,6,7,0,1,2,3,4},{13,14,15,8,9,10,11,12},{21,22,23,16,17,18,19,20},{29..., dimensions={0} | all-to-all | bytes 16384 | tf_op jit(solution)/shard_map/all_to_all | solution.py:329
  59.8 0.0 copy-done.1
  59.8 0.6 add.3
  (2 shorter events, 0.0 us)
Async XLA Ops:
  16.0 17.3 %all-to-all-start.1 = ((bf16[64,4,128]{2,1,0:T(4,128)(2,1)}), bf16[64,4,128]{2,1,0:T(4,128)(2,1)S(1)}, u32[]{:S(2)}, u32[]{:S(2)}) async-start(bf16[64,4,128]{2,1,0:T(4,128)(2,1)} %bitcast.5), calls=%async_computation.1 | async-start | bytes 131072 | tf_op jit(solution)/shard_map/all_to_all | solution.py:329
  33.2 26.6 %copy-start.1 = (f32[1,256]{1,0:T(1,128)S(1)}, f32[1,256]{1,0:T(1,128)}, u32[]{:S(2)}) copy-start(f32[1,256]{1,0:T(1,128)} %param.8) | copy-start | bytes 3076
  33.3 16.5 %copy-start = (bf16[256,2048]{1,0:T(8,128)(2,1)S(1)}, bf16[256,2048]{1,0:T(8,128)(2,1)}, u32[]{:S(2)}) copy-start(bf16[256,2048]{1,0:T(8,128)(2,1)} %w_ref.1) | copy-start | bytes 3145732

commit v16 on v15

--- a/solution.py
+++ b/solution.py
@@ -24,7 +24,7 @@
 TERM = 8
 
 FIRST = 36
-FIRST_SHARD = 5
+FIRST_SHARD = 3
 
 
 def far(x):

time: 60.7 us -> 62 us (1.021)
  starting transfers between devices: 14.6 us -> 15.5 us
    all_to_all x1, starting transfers between devices: 14.6 us -> 15.5 us  [exchange(): lax.all_to_all(x, axis, split_axis=0, concat_axis=0, tiled=True, axis_ind...]
where the time goes in v16:
time: 62 us; the launch traced here: 61.7 us
  blocking collectives  37 us (60%)
  starting transfers between devices  15.5 us (25%)
  Pallas kernels  7.87 us (13%)
  between operations  0.7 us (1%)
    all_to_all x3, blocking collectives, exchange(): lax.all_to_all(x, axis, split_axis=0, concat_axis=0, tiled=True, axis_ind...  37 us
    all_to_all x1, starting transfers between devices, exchange(): lax.all_to_all(x, axis, split_axis=0, concat_axis=0, tiled=True, axis_ind...  15.5 us
    pallas_call x1, Pallas kernels, per_device(): call(functools.partial(window_kernel, slots_here, block_len, head_dim), '...  2.64 us
    pallas_call x1, Pallas kernels, per_device(): call(attend_kernel, 'attend', tiles, [SMEM, VMEM, VMEM], [per_request, pl...  2.29 us
    pallas_call x1, Pallas kernels, per_device(): call(functools.partial(prepare_kernel, head_dim), 'prepare', (jax.ShapeDt...  1.28 us
  transfers between devices with their start and end apart: 1, of which 0 were waited for; matrix products, arithmetic and copies ran while one was open for 0% of the time, Pallas kernels for 4%

profile of v16, /device:TPU:1, one launch (start us, length us, event | category | flops | bytes accessed | tf_op | source)
XLA Modules:
  0.0 61.7 jit_solution(5034057565146748539)
XLA Ops:
  0.6 1.3 %prepare.1 = (f32[16,128]{1,0:T(8,128)S(1)}, bf16[2048,256]{1,0:T(8,128)(2,1)S(1)}, f32[16,128]{1,0:T(8,128)S(1)}, f32[8,128]{1,0:T(8,128)S(1)}, f32[8,128]{1,0:T(8,128)S(1)}) custom-call(f32[2,128]{1,0:T(2,128)} %bitcast.20, s32[64]{0:T(128)} %rest_0_.3, bf16[2048,256]{1,0:T(8,128)(2,1)} %rest_0_.2, f32[16,128]{1,0:T(8,128)} %bitcast.19), custom_call_target="tpu_custom_call" | custom-call | tf_op jit(solution)/shard_map/prepare/pallas_call | solution.py:349
  1.9 13.4 %all_to_all.20 = f32[8,2,128]{2,1,0:T(2,128)S(1)} all-to-all(f32[8,2,128]{2,1,0:T(2,128)S(1)} %bitcast.17), channel_id=1, replica_groups={{3,4,5,6,7,0,1,2},{11,12,13,14,15,8,9,10},{19,20,21,22,23,16,17,18},{27..., dimensions={0} | all-to-all | bytes 16384 | tf_op jit(solution)/shard_map/all_to_all | solution.py:329
  15.3 1.1 %query.1.rest_2_ = bf16[256,128]{1,0:T(8,128)(2,1)} custom-call(f32[16,128]{1,0:T(8,128)S(1)} %bitcast.14, f32[16,128]{1,0:T(8,128)S(1)} %get-tuple-element.12.gain_ref, bf16[2048,256]{1,0:T(8,128)(2,1)S(1)} %get-tuple-element.15.w_ref, f32[8,128]{1,0:T(8,128)S(1)} %get-tuple-element.13.cos_ref, f32[8,128]{1,0:T(8,128)S(1)} %get-tuple-element.14.sin_ref), custom_call_target="tpu_custom_call" | custom-call | tf_op jit(solution)/shard_map/query/pallas_call | solution.py:370
  16.4 15.5 %all-to-all-start.1 = ((bf16[64,4,128]{2,1,0:T(4,128)(2,1)}), bf16[64,4,128]{2,1,0:T(4,128)(2,1)S(1)}, u32[]{:S(2)}, u32[]{:S(2)}) async-start(bf16[64,4,128]{2,1,0:T(4,128)(2,1)} %bitcast.5), calls=%async_computation.1 | async-start | bytes 131072 | tf_op jit(solution)/shard_map/all_to_all | solution.py:329
  31.9 2.6 %window.1 = (s32[96,128]{1,0:T(8,128)S(1)}, bf16[96,128,128]{2,1,0:T(8,128)(2,1)S(1)}, bf16[1,128]{1,0:T(2,128)(2,1)}, f32[8,128]{1,0:T(8,128)S(1)}) custom-call(f32[16,128]{1,0:T(8,128)S(1)} %bitcast.15, f32[16,128]{1,0:T(8,128)S(1)} %get-tuple-element.12.gain_ref, f32[8,128]{1,0:T(8,128)S(1)} %get-tuple-element.13.cos_ref, ...), custom_call_target="tpu_custom_call" | custom-call | tf_op jit(solution)/shard_map/window/pallas_call | solution.py:376
  34.6 0.0 copy-start.1
  34.6 0.1 slice_reduce_fusion.tab_ref
  34.7 0.0 all-to-all-done.1
  34.7 0.0 copy-start
  34.7 2.3 %attend.1 = bf16[256,128]{1,0:T(8,128)(2,1)S(1)} custom-call(s32[96]{0:T(128)S(1)} %slice_reduce_fusion.tab_ref, bf16[256,128]{1,0:T(8,128)(2,1)S(1)} %bitcast.11, bf16[96,128,128]{2,1,0:T(8,128)(2,1)S(1)} %get-tuple-element.17.kv_ref), custom_call_target="tpu_custom_call" | custom-call | tf_op jit(solution)/shard_map/attend/pallas_call | solution.py:398
  37.0 14.2 %all_to_all.21 = bf16[64,4,128]{2,1,0:T(4,128)(2,1)S(1)} all-to-all(bf16[64,4,128]{2,1,0:T(4,128)(2,1)S(1)} %bitcast.12), channel_id=1, replica_groups={{288,296,304,312,320,328,336,344,352,360,368,376,384,392,400,408,416,42..., dimensions={0} | all-to-all | bytes 131072 | tf_op jit(solution)/shard_map/all_to_all | solution.py:329
  51.1 0.0 copy-done
  51.1 0.6 combine.1
  51.7 9.4 %all_to_all.22 = f32[8,2,128]{2,1,0:T(2,128)S(1)} all-to-all(f32[8,2,128]{2,1,0:T(2,128)S(1)} %bitcast.16), channel_id=1, replica_groups={{3,4,5,6,7,0,1,2},{11,12,13,14,15,8,9,10},{19,20,21,22,23,16,17,18},{27..., dimensions={0} | all-to-all | bytes 16384 | tf_op jit(solution)/shard_map/all_to_all | solution.py:329
  61.1 0.0 copy-done.1
  61.1 0.6 add.3
  (2 shorter events, 0.0 us)
Async XLA Ops:
  16.4 18.2 %all-to-all-start.1 = ((bf16[64,4,128]{2,1,0:T(4,128)(2,1)}), bf16[64,4,128]{2,1,0:T(4,128)(2,1)S(1)}, u32[]{:S(2)}, u32[]{:S(2)}) async-start(bf16[64,4,128]{2,1,0:T(4,128)(2,1)} %bitcast.5), calls=%async_computation.1 | async-start | bytes 131072 | tf_op jit(solution)/shard_map/all_to_all | solution.py:329
  34.6 26.6 %copy-start.1 = (f32[1,256]{1,0:T(1,128)S(1)}, f32[1,256]{1,0:T(1,128)}, u32[]{:S(2)}) copy-start(f32[1,256]{1,0:T(1,128)} %param.8) | copy-start | bytes 3076
  34.7 16.5 %copy-start = (bf16[256,2048]{1,0:T(8,128)(2,1)S(1)}, bf16[256,2048]{1,0:T(8,128)(2,1)}, u32[]{:S(2)}) copy-start(bf16[256,2048]{1,0:T(8,128)(2,1)} %w_ref.1) | copy-start | bytes 3145732
